TPU v7x, 128 devices: a whole 4x4x4 slice. The times are simulated.
128 devices in a mesh: dp: 4 (over x), row: 4 (over z_hi, core), col: 8 (over y, z_lo).
Axes of the slice: x: 4, y: 4, z: 4 (z_hi: 2, z_lo: 2; z = z_hi * 2 + z_lo), core: 2. Of those that a mesh axis runs over, the one named last changes fastest.
Arguments:
- activation: bfloat16 [2048, 16384], P('dp', ('row', 'col')), may hold values from -50 to 50
- weight: bfloat16 [8192, 16384], P(('dp', 'col'), 'row'), may hold values from -6 to 6
- prune_mask: int32 [8192, 128], P(('dp', 'col')), may hold values 0 or 1
- channel_rank: int32 [128], replicated, may hold values from 0 to 127, each once
Outputs:
- pruned_weight: bfloat16 [8192, 16384], P(('dp', 'col'), 'row')
- hessian: float32 [16384, 16384], P(('dp', 'col'), 'row')
All inputs are finite; a program needn't handle non-finite values. No bound on the sum of `prune_mask` on one device may be relied on, other than what follows from the above.
Results may differ from a plain program's by a relative error of at most 0.001.
Values may be sent and summed in bfloat16 or wider, within the bound.
No kernel may reach another device: no remote copies, remote signals or barrier semaphores. Data moves between devices by JAX's collectives and lax.ppermute only.
A program may use at most 192 MiB of HBM per device.

v0:
```python
import jax
import jax.numpy as jnp
from jax import lax
from jax.sharding import PartitionSpec as P

PANEL = 128
KEEP = 8


DAMPING = 0.01


def from_root(block, axis, owner):
    block = jnp.where(lax.axis_index(axis) == owner, block, jnp.zeros_like(block))
    return lax.psum(block, axis)


def panel_factor(block):
    identity = jnp.eye(block.shape[0], dtype=jnp.float32)
    lower_factor = jnp.linalg.cholesky(block)
    lower_inverse = lax.linalg.triangular_solve(lower_factor, identity, left_side=True, lower=True)
    inverse = jnp.dot(lower_inverse.T, lower_inverse, precision=lax.Precision.HIGHEST)
    return jnp.linalg.cholesky(inverse).T


def panel_sweep(start_cols, keep_weight, factor):
    positions = jnp.arange(start_cols.shape[1])

    def sweep_step(j, carry):
        current, errors = carry
        column = lax.dynamic_index_in_dim(current, j, 1, keepdims=False)
        keep_col = lax.dynamic_index_in_dim(keep_weight, j, 1, keepdims=False)
        factor_row = lax.dynamic_index_in_dim(factor, j, 0, keepdims=False)
        pivot = lax.dynamic_index_in_dim(factor_row, j, 0, keepdims=False)
        error_col = (1.0 - keep_col) * column / pivot
        factor_row = jnp.where(positions > j, factor_row, 0.0)
        current = current - error_col[:, None] * factor_row[None, :]
        errors = lax.dynamic_update_index_in_dim(errors, error_col, j, 1)
        return (current, errors)

    current, errors = lax.fori_loop(
        0, start_cols.shape[1], sweep_step, (start_cols, jnp.zeros_like(start_cols))
    )
    return (keep_weight * current, errors)


def body(activation, weight, prune_mask, channel_rank):
    tok_dev = activation.shape[0]
    dp_size = lax.axis_size("dp")
    col_size = lax.axis_size("col")
    tokens = tok_dev * dp_size
    chan_count = weight.shape[1]
    all_channels = chan_count * lax.axis_size("row")
    shard_rows = all_channels // (dp_size * col_size)
    row_pos = lax.axis_index("row")
    shard_index = lax.axis_index("dp") * col_size + lax.axis_index("col")
    contract_tokens = (((0,), (0,)), ((), ()))
    gathered = lax.all_gather(activation, ("row", "col"), axis=1, tiled=True)
    own_cols = lax.dynamic_slice_in_dim(gathered, row_pos * chan_count, chan_count, 1)
    grouped = lax.dynamic_index_in_dim(
        gathered.reshape(tok_dev, dp_size, col_size, shard_rows),
        lax.axis_index("col"),
        2,
        keepdims=False,
    )
    grouped = grouped.reshape(tok_dev, dp_size * shard_rows)
    summed = lax.psum_scatter(
        lax.dot_general(grouped, own_cols, contract_tokens, preferred_element_type=jnp.float32),
        "dp",
        scatter_dimension=0,
        tiled=True,
    )
    global_row = shard_index * shard_rows + jnp.arange(shard_rows)[:, None]
    global_col = row_pos * chan_count + jnp.arange(chan_count)[None, :]
    on_diag = global_row == global_col
    hessian = summed * (2.0 / tokens) + jnp.where(on_diag, DAMPING, 0.0)
    local_diag = jnp.sum(jnp.where(on_diag, hessian, 0.0), axis=0)
    diagonal = lax.psum(local_diag, ("dp", "col"))
    panel_rows = from_root(hessian[:PANEL, :], ("dp", "col"), 0)
    identity = jnp.eye(PANEL, dtype=jnp.float32)
    factor = panel_factor(jnp.where(row_pos == 0, panel_rows[:, :PANEL], identity))
    keep_weight = jnp.where((prune_mask == 1) | (channel_rank < KEEP)[None, :], 1.0, 0.0).astype(
        jnp.float32
    )
    pruned_panel, errors = panel_sweep(weight[:, :PANEL].astype(jnp.float32), keep_weight, factor)
    correction = jnp.dot(errors, factor, precision=lax.Precision.HIGHEST)
    correction = from_root(correction, "row", 0)
    updated = (
        weight.astype(jnp.float32)
        + jnp.dot(correction, panel_rows, precision=lax.Precision.HIGHEST) / diagonal[None, :]
    )
    padded = jnp.pad(pruned_panel, ((0, 0), (0, chan_count - PANEL)))
    is_panel = row_pos * chan_count + jnp.arange(chan_count) < PANEL
    pruned_weight = jnp.where(is_panel[None, :], padded, updated).astype(jnp.bfloat16)
    return (pruned_weight, hessian)


def solution(mesh):
    return jax.shard_map(
        body,
        mesh=mesh,
        in_specs=(P("dp", ("row", "col")), P(("dp", "col"), "row"), P(("dp", "col"), None), P()),
        out_specs=(P(("dp", "col"), "row"), P(("dp", "col"), "row")),
        check_vma=False,
    )
```

profile of v0, /device:TPU:64, one launch (start us, length us, event | category | flops | bytes accessed | tf_op | source)
XLA Modules:
  0.0 1017.4 jit_solution(7274042227965237371)
XLA Ops:
  7.2 2.0 copy.21
  9.3 105.7 %all-gather.2.cloned.1.call-done = bf16[512,16384]{0,1:T(8,128)(2,1)} async-done(((bf16[512,512]{0,1:T(8,128)(2,1)}), bf16[512,16384]{0,1:T(8,128)(2,1)}) %all-gather.2.cloned.1.call-update) | async-done | bytes 16777232 | tf_op jit(solution)/shard_map/all_gather | solution.py:58
  115.0 1.7 constant_dynamic-slice_fusion.1
  116.8 17.5 %fusion.8 = f32[2048,4096]{0,1:T(8,128)} fusion(bf16[512,2048]{0,1:T(8,128)(2,1)S(1)} %bitcast.39, bf16[512,16384]{0,1:T(8,128)(2,1)} %all-gather.2.cloned.1.call-done, s32[]{:T(128)S(6)} %select_n.86), kind=kOutput, calls=%fused_computation.14 | convolution fusion | flops 8589934592 | bytes 39845892 | tf_op jit(solution)/shard_map/dot_general | solution.py:68
  134.3 284.0 %reduce-scatter.2.cloned.1.call-done = f32[512,4096]{0,1:T(8,128)} async-done(((f32[2048,4096]{0,1:T(8,128)}), f32[512,4096]{0,1:T(8,128)}) %reduce-scatter.2.cloned.1.call-update) | async-done | bytes 8388624 | tf_op jit(solution)/shard_map/reduce_scatter | solution.py:67
  418.3 5.4 fusion.4
  423.8 3.2 copy-done
  426.9 1.6 slice_select_fusion
  429.0 8.9 copy.29
  437.9 156.4 %psum.23 = f32[4096]{0:T(1024)S(1)} all-reduce(f32[4096]{0:T(1024)S(1)} %get-tuple-element.221), channel_id=1, replica_groups=mesh['dp'=4,'row'=4,'col'=8] {'dp','col'}, use_global_device_ids=true, to_apply=%region_8.10 | all-reduce | flops 4096 | bytes 32768 | tf_op jit(solution)/shard_map/psum | solution.py:78
  594.3 147.0 %all-reduce.4.cloned.1.call-done = f32[128,4096]{0,1:T(8,128)} async-done(((f32[128,4096]{0,1:T(8,128)}), f32[128,4096]{0,1:T(8,128)}) %all-reduce.4.cloned.1.call-update) | async-done | bytes 2097168 | tf_op jit(solution)/shard_map/psum | solution.py:15
  741.3 0.9 slice_select_fusion.1
  742.3 0.9 fusion.14
  743.1 11.7 %cholesky.44 = f32[128,128]{1,0:T(8,128)S(1)} custom-call(f32[128,128]{1,0:T(8,128)S(1)} %fusion.14), custom_call_target="Cholesky" | custom-call | tf_op jit(solution)/shard_map/jit(cholesky)/cholesky | solution.py:20
  755.5 0.7 fusion.10
  756.2 9.8 custom-call.5
  766.7 11.7 %cholesky.55 = f32[128,128]{1,0:T(8,128)S(1)} custom-call(f32[128,128]{1,0:T(8,128)S(1)} %fusion.11), custom_call_target="Cholesky" | custom-call | tf_op jit(solution)/shard_map/jit(cholesky)/cholesky | solution.py:23
  778.4 0.7 compare_reduce_fusion
  779.1 0.7 fusion.17
  779.9 183.9 %while.19 = (s32[]{:T(128)}, f32[256,128]{0,1:T(8,128)S(1)}, f32[256,128]{0,1:T(8,128)S(1)}, f32[256,128]{0,1:T(8,128)S(1)}, f32[128,128]{1,0:T(8,128)S(1)}, /*index=5*/s32[]{:T(128)}, s32[]{:T(128)}, s32[]{:T(128)}) while((s32[]{:T(128)}, f32[256,128]{0,1:T(8,128)S(1)}, f32[256,128]{0,1:T(8,128)S(1)}, f32[256,128]{0,1:T(8,128)S(1)}, ...), condition=%wide.region_5.7_spmd.clone, body=%wide.region_4.6_spmd.clone.sunk | while | flops 66563 | bytes 270973 | solution.py:41
  780.5 0.7 multiply_divide_fusion.2
  782.0 0.7 multiply_divide_fusion.2
  787.7 0.7 multiply_divide_fusion.2
  789.1 0.7 multiply_divide_fusion.2
  790.6 0.7 multiply_divide_fusion.2
  796.3 0.7 multiply_divide_fusion.2
  797.8 0.7 multiply_divide_fusion.2
  799.2 0.7 multiply_divide_fusion.2
  806.4 0.7 multiply_divide_fusion.2
  807.8 0.7 multiply_divide_fusion.2
  809.2 0.7 multiply_divide_fusion.2
  815.0 0.7 multiply_divide_fusion.2
  816.4 0.7 multiply_divide_fusion.2
  817.8 0.7 multiply_divide_fusion.2
  823.6 0.7 multiply_divide_fusion.2
  825.0 0.7 multiply_divide_fusion.2
  826.5 0.7 multiply_divide_fusion.2
  833.6 0.7 multiply_divide_fusion.2
  835.1 0.7 multiply_divide_fusion.2
  836.5 0.7 multiply_divide_fusion.2
  842.2 0.7 multiply_divide_fusion.2
  843.7 0.7 multiply_divide_fusion.2
  845.1 0.7 multiply_divide_fusion.2
  850.9 0.7 multiply_divide_fusion.2
  852.3 0.7 multiply_divide_fusion.2
  853.7 0.7 multiply_divide_fusion.2
  860.9 0.7 multiply_divide_fusion.2
  862.3 0.7 multiply_divide_fusion.2
  863.8 0.7 multiply_divide_fusion.2
  869.5 0.7 multiply_divide_fusion.2
  871.0 0.7 multiply_divide_fusion.2
  872.4 0.7 multiply_divide_fusion.2
  878.1 0.7 multiply_divide_fusion.2
  879.6 0.7 multiply_divide_fusion.2
  881.0 0.7 multiply_divide_fusion.2
  888.2 0.7 multiply_divide_fusion.2
  889.6 0.7 multiply_divide_fusion.2
  891.0 0.7 multiply_divide_fusion.2
  896.8 0.7 multiply_divide_fusion.2
  898.2 0.7 multiply_divide_fusion.2
  899.7 0.7 multiply_divide_fusion.2
  964.0 1.7 convolution_select_fusion
  965.8 38.1 %all-reduce.6.cloned.1.call-done = f32[256,128]{1,0:T(8,128)} async-done(((f32[256,128]{1,0:T(8,128)}), f32[256,128]{1,0:T(8,128)}) %all-reduce.6.cloned.1.call-update) | async-done | bytes 131088 | tf_op jit(solution)/shard_map/psum | solution.py:15
  1003.9 6.9 fusion.7
  (636 shorter events, 153.3 us)
Async XLA Ops:
  7.2 107.9 %all-gather.2.cloned.1.call-start = ((), (), s32[]{:S(2)}) async-start(), calls=%async_computation.1 | async-start | bytes 17301504 | tf_op jit(solution)/shard_map/all_gather | solution.py:58
  9.3 409.1 %reduce-scatter.2.cloned.1.call-start = ((), (), s32[]{:S(2)}) async-start(), calls=%async_computation.2 | async-start | bytes 41943040 | tf_op jit(solution)/shard_map/reduce_scatter | solution.py:67
  134.3 607.0 %all-reduce.4.cloned.1.call-start = ((), (), s32[]{:S(2)}) async-start(), calls=%async_computation.3 | async-start | bytes 4194304 | tf_op jit(solution)/shard_map/psum | solution.py:15
  423.7 3.2 copy-start
  423.7 4.9 copy-start.3
  423.7 4.9 copy-start.1
  423.8 5.0 slice-start
  428.6 575.3 %all-reduce.6.cloned.1.call-start = ((), (), s32[]{:S(2)}) async-start(), calls=%async_computation.4 | async-start | bytes 262144 | tf_op jit(solution)/shard_map/psum | solution.py:15
  437.9 566.0 %copy-start.2 = (bf16[256,4096]{1,0:T(8,128)(2,1)S(1)}, bf16[256,4096]{1,0:T(8,128)(2,1)}, u32[]{:S(2)}) copy-start(bf16[256,4096]{1,0:T(8,128)(2,1)} %param.8) | copy-start | bytes 6291460
Sparse Core Ops, SparseCore 0:
  10.2 104.7 all-gather.1
  134.4 283.9 reduce-scatter.1
  428.7 312.5 all-reduce.3
  965.8 38.0 all-reduce.5
where the time goes:
time: 1030 us; the launch traced here: 1020 us
  waiting for transfers between devices  575 us (56%)
  blocking collectives  156 us (15%)
  other arithmetic  142 us (14%)
  local copies, waits for them, and re-layouts  97.2 us (9%)
  matrix products  26.7 us (3%)
  between operations  14 us (1%)
    reduce_scatter x1, waiting for transfers between devices, body(): lax.psum_scatter(lax.dot_general(grouped, own_cols, contract_tokens, pref...  284 us
    psum x2, waiting for transfers between devices, from_root(): return lax.psum(block, axis)  185 us
    psum x1, blocking collectives, body(): diagonal = lax.psum(local_diag, ('dp', 'col'))  156 us
    all_gather x1, waiting for transfers between devices, body(): gathered = lax.all_gather(activation, ('row', 'col'), axis=1, tiled=True)  106 us
    div x128, other arithmetic, sweep_step(): error_col = (1.0 - keep_col) * column / pivot  83.9 us
    dynamic_slice x128, local copies, waits for them, and re-layouts, sweep_step(): pivot = lax.dynamic_index_in_dim(factor_row, j, 0, keepdims=False)  75.3 us
  transfers between devices with their start and end apart: 4, of which 4 were waited for; matrix products, arithmetic and copies ran while one was open for 1% of the time, Pallas kernels for 0%

commit v1 on v0

v1 whole, which is shorter than its diff:
```python
import functools

import jax
import jax.numpy as jnp
from jax import lax
from jax.experimental import pallas as pl
from jax.experimental.pallas import tpu as pltpu
from jax.sharding import PartitionSpec as P

PANEL = 128
KEEP = 8
DAMPING = 0.01

NX = 4
NY = 4
NZ = 2
NROW = 4
VMEM_LIMIT = 56 * 1024 * 1024


def x_perm(k):
    return [(i, (i + k) % NX) for i in range(NX)]


def y_perm(k):
    return [(y * NZ + z, ((y + k) % NY) * NZ + z) for y in range(NY) for z in range(NZ)]


Z_PERM = [(y * NZ + z, y * NZ + 1 - z) for y in range(NY) for z in range(NZ)]


def send_x(a, k):
    return lax.ppermute(a, "dp", x_perm(k))


def send_y(a, k):
    return lax.ppermute(a, "col", y_perm(k))


def send_z(a):
    return lax.ppermute(a, "col", Z_PERM)


SHIFTS = (0, -1, 1, 2)


def gather_small(a, send):
    return [a, send(a, 1), send(a, -1), send(a, 2)]


def gather_ring(a, b, send):
    a_left, b_right = send(a, 1), send(b, -1)
    b_left, a_right = send(b, 1), send(a, -1)
    a_far, b_far = send(a_left, 1), send(b_right, -1)
    return [a, a_left, a_right, a_far], [b, b_left, b_right, b_far]


def panel_kernel(ap_ref, wp_ref, mask_ref, rank_ref, corr_ref, panel_ref):
    hess = jnp.zeros((PANEL, PANEL), jnp.float32)
    for k in range(NX):
        blk = ap_ref[k]
        hess += lax.dot_general(blk, blk, (((0,), (0,)), ((), ())), preferred_element_type=jnp.float32)
    tokens = NX * ap_ref.shape[1]
    row = lax.broadcasted_iota(jnp.int32, (PANEL, PANEL), 0)
    col = lax.broadcasted_iota(jnp.int32, (PANEL, PANEL), 1)
    hess = hess * (2.0 / tokens) + jnp.where(row == col, DAMPING, 0.0)
    lane = lax.broadcasted_iota(jnp.int32, (1, PANEL), 1)
    tiles = [hess[8 * t : 8 * t + 8] for t in range(PANEL // 8)]
    ratio = [None] * PANEL
    for j in reversed(range(PANEL)):
        own = tiles[j // 8][j % 8 : j % 8 + 1]
        r = own / own[:, j : j + 1]
        ratio[j] = jnp.where(lane < j, r, 0.0)
        for t in range((j + 7) // 8):
            tiles[t] = tiles[t] - tiles[t][:, j : j + 1] * r
    ratio_tiles = [jnp.concatenate(ratio[8 * t : 8 * t + 8], axis=0) for t in range(PANEL // 8)]

    keep = jnp.where((mask_ref[...] == 1) | (rank_ref[...] < KEEP), 1.0, 0.0)
    keep_t = keep.T
    w_t = wp_ref[...].astype(jnp.float32).T
    rows = w_t.shape[1]
    acc = [jnp.zeros((8, rows), jnp.float32) for _ in range(PANEL // 8)]
    corr = [None] * PANEL
    for j in range(PANEL):
        c = jnp.where(keep_t[j : j + 1] > 0.5, -acc[j // 8][j % 8 : j % 8 + 1], w_t[j : j + 1])
        corr[j] = c
        for t in range((j + 1) // 8, PANEL // 8):
            acc[t] = acc[t] + ratio_tiles[t][:, j : j + 1] * c
    corr_t = jnp.concatenate(corr, axis=0)
    corr_ref[...] = corr_t.T
    panel_ref[...] = jnp.where(keep_t > 0.5, w_t - corr_t, 0.0).T.astype(panel_ref.dtype)


def panel_step(ap, wp, mask, rank):
    rows = wp.shape[0]
    return pl.pallas_call(
        panel_kernel,
        out_shape=(
            jax.ShapeDtypeStruct((rows, PANEL), jnp.float32),
            jax.ShapeDtypeStruct((rows, PANEL), jnp.bfloat16),
        ),
        compiler_params=pltpu.CompilerParams(vmem_limit_bytes=VMEM_LIMIT),
        name="panel_sweep",
    )(ap, wp, mask, rank.reshape(1, PANEL))


def columns_kernel(entry_axis, tok, scale, info, lhs_ref, corr_ref, panel_ref, w_ref, *rest):
    pieces = rest[:NX] if entry_axis else rest[:1]
    out_ref, hess_ref = rest[-2], rest[-1]
    rows = hess_ref.shape[0]
    step = pl.program_id(0)
    acc = None
    diag = None
    for k in range(NX):
        piece = pieces[k][0] if entry_axis else pieces[0][k]
        part = jnp.dot(lhs_ref[:, k * tok : (k + 1) * tok], piece, preferred_element_type=jnp.float32)
        acc = part if acc is None else acc + part
        wide = piece.astype(jnp.float32)
        square = jnp.sum(wide * wide, axis=0, keepdims=True)
        diag = square if diag is None else diag + square
    acc = acc * scale
    diag = diag * scale + DAMPING
    col0 = info[0] + info[2 + step] * hess_ref.shape[1]
    hess = acc[:rows]
    row = lax.broadcasted_iota(jnp.int32, hess.shape, 0)
    col = lax.broadcasted_iota(jnp.int32, hess.shape, 1)
    hess_ref[...] = hess + jnp.where(row - col == col0 - info[1], DAMPING, 0.0)
    change = jnp.dot(
        corr_ref[...], acc[rows:], precision=lax.Precision.HIGHEST, preferred_element_type=jnp.float32
    )
    out_ref[...] = (w_ref[...].astype(jnp.float32) + change / diag).astype(out_ref.dtype)

    @pl.when(col0 == 0)
    def _():
        out_ref[:, :PANEL] = panel_ref[...]


def columns_step(info, lhs, corr, panel, weight, pieces, entry_axis, out, hess):
    entries = pieces[0].shape[0] if entry_axis else 1
    tok, width = pieces[0].shape[1:]
    out_rows, chans = weight.shape
    rows = lhs.shape[0] - PANEL
    fixed = lambda i, info: (0, 0)
    at_block = lambda i, info: (0, info[2 + i])
    in_specs = [
        pl.BlockSpec(lhs.shape, fixed),
        pl.BlockSpec(corr.shape, fixed),
        pl.BlockSpec(panel.shape, fixed),
        pl.BlockSpec((out_rows, width), at_block),
    ]
    if entry_axis:
        in_specs += [pl.BlockSpec((1, tok, width), lambda i, info: (i, 0, 0))] * NX
    else:
        in_specs += [pl.BlockSpec((NX, tok, width), lambda i, info: (0, 0, 0))]
    operands = [lhs, corr, panel, weight, *pieces]
    aliases = {}
    if out is not None:
        in_specs += [pl.BlockSpec(memory_space=pl.ANY)] * 2
        operands += [out, hess]
        aliases = {len(operands) - 1: 0, len(operands): 1}
    body = functools.partial(columns_kernel, entry_axis, tok, 2.0 / (NX * tok))
    return pl.pallas_call(
        body,
        grid_spec=pltpu.PrefetchScalarGridSpec(
            num_scalar_prefetch=1,
            grid=(entries,),
            in_specs=in_specs,
            out_specs=(
                pl.BlockSpec((out_rows, width), at_block),
                pl.BlockSpec((rows, width), at_block),
            ),
        ),
        out_shape=(
            jax.ShapeDtypeStruct((out_rows, chans), weight.dtype),
            jax.ShapeDtypeStruct((rows, chans), jnp.float32),
        ),
        input_output_aliases=aliases,
        compiler_params=pltpu.CompilerParams(vmem_limit_bytes=VMEM_LIMIT),
        name="columns",
    )(info, *operands)


def body(activation, weight, prune_mask, channel_rank):
    tok, block = activation.shape
    chans = weight.shape[1]
    d, r, c = lax.axis_index("dp"), lax.axis_index("row"), lax.axis_index("col")
    y, z = c // NZ, c % NZ
    ncol = NY * NZ

    ap = activation[:, :PANEL]
    ap = jnp.where((r == 0) & (c == 0), ap, jnp.zeros_like(ap))
    got = [lax.ppermute(ap, ("row", "col"), [(0, k)]) for k in range(1, ncol)]
    ap = functools.reduce(jnp.add, got, ap)
    got = [lax.ppermute(ap, ("row", "col"), [(i, k * ncol + i) for i in range(ncol)]) for k in range(1, NROW)]
    ap = functools.reduce(jnp.add, got, ap)
    ap = jnp.stack(gather_small(ap, send_x))
    wp = jnp.where(r == 0, weight[:, :PANEL], jnp.zeros_like(weight[:, :PANEL]))
    wp = functools.reduce(jnp.add, [lax.ppermute(wp, "row", [(0, k)]) for k in range(1, NROW)], wp)
    corr, panel = panel_step(ap, wp, prune_mask, channel_rank)

    swap = [(i * NROW + j, j * NROW + i) for i in range(NX) for j in range(NROW)]
    own = lax.ppermute(activation, ("dp", "row"), swap)
    core = lax.ppermute(own, "row", [(i, i ^ 1) for i in range(NROW)])
    pair = [own, core]
    pair += [lax.ppermute(p, "row", [(i, i ^ 2) for i in range(NROW)]) for p in (own, core)]
    stacked = jnp.stack(pair)
    rows = [lax.dynamic_index_in_dim(stacked, ((d + s) % NX) ^ r, 0, keepdims=False) for s in SHIFTS]
    lhs = jnp.concatenate(
        [jnp.concatenate(rows, axis=0), ap.reshape(NX * tok, PANEL)], axis=1
    ).T

    half = block // 2
    first = activation[:, :half]
    near = jnp.stack(gather_small(first, send_y))
    first_a, first_b = gather_ring(near, send_z(near), send_x)
    second = activation[:, half:]
    second_z = send_z(second)
    second_a, second_b = gather_ring(
        jnp.stack(gather_small(second, send_x)), jnp.stack(gather_small(second_z, send_x)), send_y
    )

    base = jnp.stack([r * chans, (d * ncol + c) * block])

    def info(cols, part):
        return jnp.concatenate([base, jnp.stack([k * 2 + part for k in cols])]).astype(jnp.int32)

    def cblock(dy, dz):
        return ((y + dy) % NY) * NZ + (z + dz) % NZ

    out = hess = None
    for i in range(len(SHIFTS)):
        for dz, arrays in ((0, second_a), (1, second_b)):
            cols = info([cblock(SHIFTS[i], dz)], 1)
            out, hess = columns_step(cols, lhs, corr, panel, weight, [arrays[i]], False, out, hess)
    for dz, arrays in ((0, first_a), (1, first_b)):
        cols = info([cblock(s, dz) for s in SHIFTS], 0)
        out, hess = columns_step(cols, lhs, corr, panel, weight, arrays, True, out, hess)
    return (out, hess)


def solution(mesh):
    return jax.shard_map(
        body,
        mesh=mesh,
        in_specs=(P("dp", ("row", "col")), P(("dp", "col"), "row"), P(("dp", "col"), None), P()),
        out_specs=(P(("dp", "col"), "row"), P(("dp", "col"), "row")),
        check_vma=False,
    )
```

time: 1030 us -> 248 us (0.24)
  the two profiles are of different devices: /device:TPU:64 before, /device:TPU:2 now
where the time goes in v1:
time: 248 us; the launch traced here: 247 us
  Pallas kernels  77 us (31%)
  waiting for transfers between devices  76.5 us (31%)
  starting transfers between devices  70.9 us (29%)
  other arithmetic  12.3 us (5%)
  local copies, waits for them, and re-layouts  9.13 us (4%)
    pallas_call x10, Pallas kernels, columns_step(): pl.pallas_call(body, grid_spec=pltpu.PrefetchScalarGridSpec(num_scalar_pr...  62.9 us
    ppermute x2, waiting for transfers between devices, body(): lax.ppermute(p, 'row', [(i, i ^ 2) for i in range(NROW)])  34.5 us
    ppermute x15, starting transfers between devices, send_x(): return lax.ppermute(a, 'dp', x_perm(k))  31.5 us
    ppermute x9, waiting for transfers between devices, send_y(): return lax.ppermute(a, 'col', y_perm(k))  21.8 us
    ppermute x7, starting transfers between devices, body(): got = [lax.ppermute(ap, ('row', 'col'), [(0, k)]) for k in range(1, ncol)]  14.1 us
    pallas_call x1, Pallas kernels, panel_step(): pl.pallas_call(panel_kernel, out_shape=(jax.ShapeDtypeStruct((rows, PANEL...  14 us
    ppermute x9, starting transfers between devices, send_y(): return lax.ppermute(a, 'col', y_perm(k))  12.5 us
    ppermute x2, waiting for transfers between devices, send_z(): return lax.ppermute(a, 'col', Z_PERM)  9.93 us
  transfers between devices with their start and end apart: 43, of which 9 were waited for; matrix products, arithmetic and copies ran while one was open for 8% of the time, Pallas kernels for 27%

profile of v1, /device:TPU:2, one launch (start us, length us, event | category | flops | bytes accessed | tf_op | source)
XLA Modules:
  0.0 246.9 jit_solution(8104192088353609179)
XLA Ops:
  0.7 1.0 slice_select_fusion
  1.6 6.3 %collective-permute-start.10 = (bf16[512,128]{1,0:T(8,128)(2,1)S(1)}, bf16[512,128]{1,0:T(8,128)(2,1)S(1)}, u32[]{:S(2)}, u32[]{:S(2)}) collective-permute-start(bf16[512,128]{1,0:T(8,128)(2,1)S(1)} %slice_select_fusion), channel_id=1, source_target_pairs={{0,7},{32,39},{64,71},{96,103}} | collective-permute-start | bytes 393224 | tf_op jit(solution)/shard_map/ppermute | solution.py:192
  7.9 1.3 collective-permute-start.4
  9.2 1.3 collective-permute-start.5
  10.5 1.3 collective-permute-start.6
  11.8 1.3 collective-permute-start.7
  13.1 1.3 collective-permute-start.8
  14.5 1.3 collective-permute-start.9
  15.8 0.9 slice_select_fusion.1
  16.6 1.3 collective-permute-start.17
  17.9 1.3 collective-permute-start.18
  19.2 1.3 collective-permute-start.19
  20.6 1.0 add_add_fusion.1
  21.5 1.3 collective-permute-start.11
  22.8 1.1 slice_bitcast_fusion
  24.0 1.6 collective-permute-start.36
  25.5 1.3 collective-permute-start.12
  27.4 2.1 collective-permute-start.38
  29.6 1.3 collective-permute-start.13
  30.9 1.9 collective-permute-start
  33.8 3.5 %collective-permute-start.21 = (bf16[512,256]{1,0:T(8,128)(2,1)S(1)}, bf16[512,256]{1,0:T(8,128)(2,1)S(1)}, u32[]{:S(2)}, u32[]{:S(2)}) collective-permute-start(bf16[512,256]{1,0:T(8,128)(2,1)S(1)} %get-tuple-element.51), channel_id=1, source_target_pairs={{0,6},{1,7},{2,0},{3,1},{4,2},{5,3},{6,4},{7,5},{8,14},{9,15},{10,... | collective-permute-start | bytes 786440 | tf_op jit(solution)/shard_map/ppermute | solution.py:37
  37.3 1.4 collective-permute-done.38
  39.2 9.9 %collective-permute-done.30 = bf16[512,256]{1,0:T(8,128)(2,1)S(1)} collective-permute-done((bf16[512,256]{1,0:T(8,128)(2,1)S(1)}, bf16[512,256]{1,0:T(8,128)(2,1)S(1)}, u32[]{:S(2)}, u32[]{:S(2)}) %collective-permute-start.30) | collective-permute-done | bytes 262176 | tf_op jit(solution)/shard_map/ppermute | solution.py:41
  49.1 3.5 %collective-permute-start.31 = (bf16[512,256]{1,0:T(8,128)(2,1)S(1)}, bf16[512,256]{1,0:T(8,128)(2,1)S(1)}, u32[]{:S(2)}, u32[]{:S(2)}) collective-permute-start(bf16[512,256]{1,0:T(8,128)(2,1)S(1)} %collective-permute-done.30), channel_id=1, source_target_pairs={{0,32},{32,64},{64,96},{96,0},{1,33},{33,65},{65,97},{97,1},{2,34}... | collective-permute-start | bytes 786440 | tf_op jit(solution)/shard_map/ppermute | solution.py:33
  52.9 3.9 %collective-permute-start.16 = (bf16[512,128]{1,0:T(8,128)(2,1)S(1)}, bf16[512,128]{1,0:T(8,128)(2,1)}, u32[]{:S(2)}, u32[]{:S(2)}) collective-permute-start(bf16[512,128]{1,0:T(8,128)(2,1)S(1)} %add_add_fusion), channel_id=1, source_target_pairs={{0,64},{32,96},{64,0},{96,32},{1,65},{33,97},{65,1},{97,33},{2,66}... | collective-permute-start | bytes 393224 | tf_op jit(solution)/shard_map/ppermute | solution.py:33
  56.8 3.2 %collective-permute-start.32 = (bf16[512,256]{1,0:T(8,128)(2,1)S(1)}, bf16[512,256]{1,0:T(8,128)(2,1)S(1)}, u32[]{:S(2)}, u32[]{:S(2)}) collective-permute-start(bf16[512,256]{1,0:T(8,128)(2,1)S(1)} %collective-permute-done.30), channel_id=1, source_target_pairs={{0,96},{32,0},{64,32},{96,64},{1,97},{33,1},{65,33},{97,65},{2,98}... | collective-permute-start | bytes 786440 | tf_op jit(solution)/shard_map/ppermute | solution.py:33
  60.2 1.0 collective-permute-start.39
  61.2 2.9 %collective-permute-done.16 = bf16[512,128]{1,0:T(8,128)(2,1)} collective-permute-done((bf16[512,128]{1,0:T(8,128)(2,1)S(1)}, bf16[512,128]{1,0:T(8,128)(2,1)}, u32[]{:S(2)}, u32[]{:S(2)}) %collective-permute-start.16) | collective-permute-done | bytes 131104 | tf_op jit(solution)/shard_map/ppermute | solution.py:33
  64.1 2.1 collective-permute-start.41
  66.1 1.6 collective-permute-start.23
  67.8 2.6 %collective-permute-start.33 = (bf16[512,256]{1,0:T(8,128)(2,1)S(1)}, bf16[512,256]{1,0:T(8,128)(2,1)S(1)}, u32[]{:S(2)}, u32[]{:S(2)}) collective-permute-start(bf16[512,256]{1,0:T(8,128)(2,1)S(1)} %collective-permute-done.30), channel_id=1, source_target_pairs={{0,64},{32,96},{64,0},{96,32},{1,65},{33,97},{65,1},{97,33},{2,66}... | collective-permute-start | bytes 786440 | tf_op jit(solution)/shard_map/ppermute | solution.py:33
  70.4 5.4 %collective-permute-done.33 = bf16[512,256]{1,0:T(8,128)(2,1)S(1)} collective-permute-done((bf16[512,256]{1,0:T(8,128)(2,1)S(1)}, bf16[512,256]{1,0:T(8,128)(2,1)S(1)}, u32[]{:S(2)}, u32[]{:S(2)}) %collective-permute-start.33) | collective-permute-done | bytes 262176 | tf_op jit(solution)/shard_map/ppermute | solution.py:33
  75.9 2.0 collective-permute-start.27
  77.9 1.1 collective-permute-start.2
  79.1 22.0 %collective-permute-done.2 = bf16[512,512]{1,0:T(8,128)(2,1)S(1)} collective-permute-done((bf16[512,512]{1,0:T(8,128)(2,1)S(1)}, bf16[512,512]{1,0:T(8,128)(2,1)S(1)}, u32[]{:S(2)}, u32[]{:S(2)}) %collective-permute-start.2) | collective-permute-done | bytes 524320 | tf_op jit(solution)/shard_map/ppermute | solution.py:205
  101.1 0.8 collective-permute-start.42
  101.9 2.4 collective-permute-start.34
  104.3 4.9 %collective-permute-start.25 = (bf16[4,512,256]{2,1,0:T(8,128)(2,1)}, bf16[4,512,256]{2,1,0:T(8,128)(2,1)}, u32[]{:S(2)}, u32[]{:S(2)}) collective-permute-start(bf16[4,512,256]{2,1,0:T(8,128)(2,1)} %collective-permute-done.23.rest_0_), channel_id=1, source_target_pairs={{0,96},{32,0},{64,32},{96,64},{1,97},{33,1},{65,33},{97,65},{2,98}... | collective-permute-start | bytes 3145736 | tf_op jit(solution)/shard_map/ppermute | solution.py:33
  110.3 12.5 %collective-permute-done.3 = bf16[512,512]{1,0:T(8,128)(2,1)} collective-permute-done((bf16[512,512]{1,0:T(8,128)(2,1)}, bf16[512,512]{1,0:T(8,128)(2,1)}, u32[]{:S(2)}, u32[]{:S(2)}) %collective-permute-start.3) | collective-permute-done | bytes 524320 | tf_op jit(solution)/shard_map/ppermute | solution.py:205
  123.3 5.2 %collective-permute-done.42.rest_0_ = bf16[4,512,256]{2,1,0:T(8,128)(2,1)} collective-permute-done((bf16[4,512,256]{2,1,0:T(8,128)(2,1)S(1)}, bf16[4,512,256]{2,1,0:T(8,128)(2,1)}, u32[]{:S(2)}, u32[]{:S(2)}) %collective-permute-start.42) | collective-permute-done | bytes 1048608 | tf_op jit(solution)/shard_map/ppermute | solution.py:37
  128.5 2.5 %collective-permute-start.24 = (bf16[4,512,256]{2,1,0:T(8,128)(2,1)}, bf16[4,512,256]{2,1,0:T(8,128)(2,1)}, u32[]{:S(2)}, u32[]{:S(2)}) collective-permute-start(bf16[4,512,256]{2,1,0:T(8,128)(2,1)} %collective-permute-done.23.rest_0_), channel_id=1, source_target_pairs={{0,32},{32,64},{64,96},{96,0},{1,33},{33,65},{65,97},{97,1},{2,34}... | collective-permute-start | bytes 3145736 | tf_op jit(solution)/shard_map/ppermute | solution.py:33
  131.0 16.6 %collective-permute-done.40.rest_0_ = bf16[4,512,256]{2,1,0:T(8,128)(2,1)} collective-permute-done((bf16[4,512,256]{2,1,0:T(8,128)(2,1)S(1)}, bf16[4,512,256]{2,1,0:T(8,128)(2,1)}, u32[]{:S(2)}, u32[]{:S(2)}) %collective-permute-start.40) | collective-permute-done | bytes 1048608 | tf_op jit(solution)/shard_map/ppermute | solution.py:37
  147.5 1.7 collective-permute-start.35
  149.3 4.1 %collective-permute-start.26 = (bf16[4,512,256]{2,1,0:T(8,128)(2,1)}, bf16[4,512,256]{2,1,0:T(8,128)(2,1)}, u32[]{:S(2)}, u32[]{:S(2)}) collective-permute-start(bf16[4,512,256]{2,1,0:T(8,128)(2,1)} %collective-permute-done.25.rest_2_), channel_id=1, source_target_pairs={{0,96},{32,0},{64,32},{96,64},{1,97},{33,1},{65,33},{97,65},{2,98}... | collective-permute-start | bytes 3145736 | tf_op jit(solution)/shard_map/ppermute | solution.py:33
  153.4 0.7 pad_add_fusion.7
  155.3 1.6 add_add_fusion.2.wp_ref
  156.9 1.0 pad_maximum_fusion.4.ap_ref
  158.6 14.0 %panel_sweep.1 = (f32[256,128]{1,0:T(8,128)}, bf16[256,128]{1,0:T(8,128)(2,1)}) custom-call(bf16[4,512,128]{2,1,0:T(8,128)(2,1)} %copy-done, bf16[256,128]{1,0:T(8,128)(2,1)} %add_add_fusion.2.wp_ref, s32[256,128]{1,0:T(8,128)} %mask_ref.1, s32[1,128]{1,0:T(1,128)} %bitcast.68), custom_call_target="tpu_custom_call" | custom-call | tf_op jit(solution)/shard_map/panel_sweep/pallas_call | solution.py:96
  172.7 1.8 pad_maximum_fusion
  174.5 1.2 constant_dynamic-slice_fusion.3
  175.7 1.3 copy.24
  177.2 1.3 copy.26
  178.4 2.0 copy.27
  180.5 3.4 %maximum_bitcast_fusion.lhs_ref = bf16[640,2048]{1,0:T(8,128)(2,1)} fusion(bf16[2048,128]{0,1:T(8,128)(2,1)S(1)} %copy.29, bf16[512,512]{0,1:T(8,128)(2,1)} %bitcast.52, bf16[512,512]{0,1:T(8,128)(2,1)S(1)} %bitcast.51, bf16[512,512]{0,1:T(8,128)(2,1)S(1)} %bitcast.50, bf16[512,512]{0,1:T(8,128)(2,1)S(1)} %bitcast.49), kind=kLoop, calls=%fused_computation | loop fusion | flops 13107200 | bytes 5242880 | tf_op jit(solution)/shard_map/transpose | solution.py:210
  183.9 5.2 %columns.10 = (bf16[256,4096]{1,0:T(8,128)(2,1)}, f32[512,4096]{1,0:T(8,128)}) custom-call(s32[3]{0:T(128)} %get-tuple-element.42.info, bf16[640,2048]{1,0:T(8,128)(2,1)} %maximum_bitcast_fusion.lhs_ref, f32[256,128]{1,0:T(8,128)} %get-tuple-element.22.corr_ref, bf16[256,128]{1,0:T(8,128)(2,1)} %get-tuple-element.23.panel_ref, bf16[256,4096]{1,0:T(8,128)(2,1)} %w_ref.19, ...), custom_call_target="tpu_custom_call" | custom-call | tf_op jit(solution)/shard_map/columns/pallas_call | solution.py:162
  189.2 5.2 %columns.11 = (bf16[256,4096]{1,0:T(8,128)(2,1)}, f32[512,4096]{1,0:T(8,128)}) custom-call(s32[3]{0:T(128)} %get-tuple-element.52.info, bf16[640,2048]{1,0:T(8,128)(2,1)} %maximum_bitcast_fusion.lhs_ref, f32[256,128]{1,0:T(8,128)} %get-tuple-element.22.corr_ref, ...), custom_call_target="tpu_custom_call", output_to_operand_aliasing={{0}: (6, {}), {1}: (7, {})} | custom-call | tf_op jit(solution)/shard_map/columns/pallas_call | solution.py:162
  194.4 5.5 %columns.12 = (bf16[256,4096]{1,0:T(8,128)(2,1)}, f32[512,4096]{1,0:T(8,128)}) custom-call(s32[3]{0:T(128)} %get-tuple-element.53.info, bf16[640,2048]{1,0:T(8,128)(2,1)} %maximum_bitcast_fusion.lhs_ref, f32[256,128]{1,0:T(8,128)} %get-tuple-element.22.corr_ref, ...), custom_call_target="tpu_custom_call", output_to_operand_aliasing={{0}: (6, {}), {1}: (7, {})} | custom-call | tf_op jit(solution)/shard_map/columns/pallas_call | solution.py:162
  199.9 5.2 %columns.13 = (bf16[256,4096]{1,0:T(8,128)(2,1)}, f32[512,4096]{1,0:T(8,128)}) custom-call(s32[3]{0:T(128)} %get-tuple-element.54.info, bf16[640,2048]{1,0:T(8,128)(2,1)} %maximum_bitcast_fusion.lhs_ref, f32[256,128]{1,0:T(8,128)} %get-tuple-element.22.corr_ref, ...), custom_call_target="tpu_custom_call", output_to_operand_aliasing={{0}: (6, {}), {1}: (7, {})} | custom-call | tf_op jit(solution)/shard_map/columns/pallas_call | solution.py:162
  205.1 5.2 %columns.14 = (bf16[256,4096]{1,0:T(8,128)(2,1)}, f32[512,4096]{1,0:T(8,128)}) custom-call(s32[3]{0:T(128)} %get-tuple-element.55.info, bf16[640,2048]{1,0:T(8,128)(2,1)} %maximum_bitcast_fusion.lhs_ref, f32[256,128]{1,0:T(8,128)} %get-tuple-element.22.corr_ref, ...), custom_call_target="tpu_custom_call", output_to_operand_aliasing={{0}: (6, {}), {1}: (7, {})} | custom-call | tf_op jit(solution)/shard_map/columns/pallas_call | solution.py:162
  210.4 5.2 %columns.15 = (bf16[256,4096]{1,0:T(8,128)(2,1)}, f32[512,4096]{1,0:T(8,128)}) custom-call(s32[3]{0:T(128)} %get-tuple-element.56.info, bf16[640,2048]{1,0:T(8,128)(2,1)} %maximum_bitcast_fusion.lhs_ref, f32[256,128]{1,0:T(8,128)} %get-tuple-element.22.corr_ref, ...), custom_call_target="tpu_custom_call", output_to_operand_aliasing={{0}: (6, {}), {1}: (7, {})} | custom-call | tf_op jit(solution)/shard_map/columns/pallas_call | solution.py:162
  215.6 5.2 %columns.16 = (bf16[256,4096]{1,0:T(8,128)(2,1)}, f32[512,4096]{1,0:T(8,128)}) custom-call(s32[3]{0:T(128)} %get-tuple-element.57.info, bf16[640,2048]{1,0:T(8,128)(2,1)} %maximum_bitcast_fusion.lhs_ref, f32[256,128]{1,0:T(8,128)} %get-tuple-element.22.corr_ref, ...), custom_call_target="tpu_custom_call", output_to_operand_aliasing={{0}: (6, {}), {1}: (7, {})} | custom-call | tf_op jit(solution)/shard_map/columns/pallas_call | solution.py:162
  220.8 5.2 %columns.17 = (bf16[256,4096]{1,0:T(8,128)(2,1)}, f32[512,4096]{1,0:T(8,128)}) custom-call(s32[3]{0:T(128)} %get-tuple-element.58.info, bf16[640,2048]{1,0:T(8,128)(2,1)} %maximum_bitcast_fusion.lhs_ref, f32[256,128]{1,0:T(8,128)} %get-tuple-element.22.corr_ref, ...), custom_call_target="tpu_custom_call", output_to_operand_aliasing={{0}: (6, {}), {1}: (7, {})} | custom-call | tf_op jit(solution)/shard_map/columns/pallas_call | solution.py:162
  226.1 10.4 %columns.18 = (bf16[256,4096]{1,0:T(8,128)(2,1)}, f32[512,4096]{1,0:T(8,128)}) custom-call(s32[6]{0:T(128)} %concatenate.49.info, bf16[640,2048]{1,0:T(8,128)(2,1)} %maximum_bitcast_fusion.lhs_ref, f32[256,128]{1,0:T(8,128)} %get-tuple-element.22.corr_ref, ...), custom_call_target="tpu_custom_call", output_to_operand_aliasing={{0}: (9, {}), {1}: (10, {})} | custom-call | tf_op jit(solution)/shard_map/columns/pallas_call | solution.py:162
  236.5 10.4 %columns.19 = (bf16[256,4096]{1,0:T(8,128)(2,1)}, f32[512,4096]{1,0:T(8,128)}) custom-call(s32[6]{0:T(128)} %concatenate.46.info, bf16[640,2048]{1,0:T(8,128)(2,1)} %maximum_bitcast_fusion.lhs_ref, f32[256,128]{1,0:T(8,128)} %get-tuple-element.22.corr_ref, ...), custom_call_target="tpu_custom_call", output_to_operand_aliasing={{0}: (9, {}), {1}: (10, {})} | custom-call | tf_op jit(solution)/shard_map/columns/pallas_call | solution.py:162
  (79 shorter events, 6.5 us)
Async XLA Ops:
  0.6 30.3 %copy-start.4 = (bf16[512,512]{1,0:T(8,128)(2,1)S(1)}, bf16[512,512]{1,0:T(8,128)(2,1)}, u32[]{:S(2)}) copy-start(bf16[512,512]{1,0:T(8,128)(2,1)} %param.4) | copy-start | bytes 1572868
  1.6 11.5 %collective-permute-start.10 = (bf16[512,128]{1,0:T(8,128)(2,1)S(1)}, bf16[512,128]{1,0:T(8,128)(2,1)S(1)}, u32[]{:S(2)}, u32[]{:S(2)}) collective-permute-start(bf16[512,128]{1,0:T(8,128)(2,1)S(1)} %slice_select_fusion), channel_id=1, source_target_pairs={{0,7},{32,39},{64,71},{96,103}} | collective-permute-start | bytes 393224 | tf_op jit(solution)/shard_map/ppermute | solution.py:192
  7.9 6.5 %collective-permute-start.4 = (bf16[512,128]{1,0:T(8,128)(2,1)S(1)}, bf16[512,128]{1,0:T(8,128)(2,1)S(1)}, u32[]{:S(2)}, u32[]{:S(2)}) collective-permute-start(bf16[512,128]{1,0:T(8,128)(2,1)S(1)} %slice_select_fusion), channel_id=1, source_target_pairs={{0,1},{32,33},{64,65},{96,97}} | collective-permute-start | bytes 393224 | tf_op jit(solution)/shard_map/ppermute | solution.py:192
  9.2 7.4 %collective-permute-start.5 = (bf16[512,128]{1,0:T(8,128)(2,1)S(1)}, bf16[512,128]{1,0:T(8,128)(2,1)S(1)}, u32[]{:S(2)}, u32[]{:S(2)}) collective-permute-start(bf16[512,128]{1,0:T(8,128)(2,1)S(1)} %slice_select_fusion), channel_id=1, source_target_pairs={{0,2},{32,34},{64,66},{96,98}} | collective-permute-start | bytes 393224 | tf_op jit(solution)/shard_map/ppermute | solution.py:192
  10.5 7.4 %collective-permute-start.6 = (bf16[512,128]{1,0:T(8,128)(2,1)S(1)}, bf16[512,128]{1,0:T(8,128)(2,1)S(1)}, u32[]{:S(2)}, u32[]{:S(2)}) collective-permute-start(bf16[512,128]{1,0:T(8,128)(2,1)S(1)} %slice_select_fusion), channel_id=1, source_target_pairs={{0,3},{32,35},{64,67},{96,99}} | collective-permute-start | bytes 393224 | tf_op jit(solution)/shard_map/ppermute | solution.py:192
  11.8 7.4 %collective-permute-start.7 = (bf16[512,128]{1,0:T(8,128)(2,1)S(1)}, bf16[512,128]{1,0:T(8,128)(2,1)S(1)}, u32[]{:S(2)}, u32[]{:S(2)}) collective-permute-start(bf16[512,128]{1,0:T(8,128)(2,1)S(1)} %slice_select_fusion), channel_id=1, source_target_pairs={{0,4},{32,36},{64,68},{96,100}} | collective-permute-start | bytes 393224 | tf_op jit(solution)/shard_map/ppermute | solution.py:192
  13.1 7.4 %collective-permute-start.8 = (bf16[512,128]{1,0:T(8,128)(2,1)S(1)}, bf16[512,128]{1,0:T(8,128)(2,1)S(1)}, u32[]{:S(2)}, u32[]{:S(2)}) collective-permute-start(bf16[512,128]{1,0:T(8,128)(2,1)S(1)} %slice_select_fusion), channel_id=1, source_target_pairs={{0,5},{32,37},{64,69},{96,101}} | collective-permute-start | bytes 393224 | tf_op jit(solution)/shard_map/ppermute | solution.py:192
  14.5 6.1 %collective-permute-start.9 = (bf16[512,128]{1,0:T(8,128)(2,1)S(1)}, bf16[512,128]{1,0:T(8,128)(2,1)S(1)}, u32[]{:S(2)}, u32[]{:S(2)}) collective-permute-start(bf16[512,128]{1,0:T(8,128)(2,1)S(1)} %slice_select_fusion), channel_id=1, source_target_pairs={{0,6},{32,38},{64,70},{96,102}} | collective-permute-start | bytes 393224 | tf_op jit(solution)/shard_map/ppermute | solution.py:192
  16.6 8.9 %collective-permute-start.17 = (bf16[256,128]{1,0:T(8,128)(2,1)S(1)}, bf16[256,128]{1,0:T(8,128)(2,1)S(1)}, u32[]{:S(2)}, u32[]{:S(2)}) collective-permute-start(bf16[256,128]{1,0:T(8,128)(2,1)S(1)} %slice_select_fusion.1), channel_id=1, source_target_pairs={{0,8},{1,9},{2,10},{3,11},{4,12},{5,13},{6,14},{7,15},{32,40},{33,... | collective-permute-start | bytes 196616 | tf_op jit(solution)/shard_map/ppermute | solution.py:198
  17.9 8.9 %collective-permute-start.18 = (bf16[256,128]{1,0:T(8,128)(2,1)S(1)}, bf16[256,128]{1,0:T(8,128)(2,1)S(1)}, u32[]{:S(2)}, u32[]{:S(2)}) collective-permute-start(bf16[256,128]{1,0:T(8,128)(2,1)S(1)} %slice_select_fusion.1), channel_id=1, source_target_pairs={{0,16},{1,17},{2,18},{3,19},{4,20},{5,21},{6,22},{7,23},{32,48},{3... | collective-permute-start | bytes 196616 | tf_op jit(solution)/shard_map/ppermute | solution.py:198
  19.2 8.2 %collective-permute-start.19 = (bf16[256,128]{1,0:T(8,128)(2,1)S(1)}, bf16[256,128]{1,0:T(8,128)(2,1)S(1)}, u32[]{:S(2)}, u32[]{:S(2)}) collective-permute-start(bf16[256,128]{1,0:T(8,128)(2,1)S(1)} %slice_select_fusion.1), channel_id=1, source_target_pairs={{0,24},{1,25},{2,26},{3,27},{4,28},{5,29},{6,30},{7,31},{32,56},{3... | collective-permute-start | bytes 196616 | tf_op jit(solution)/shard_map/ppermute | solution.py:198
  21.5 8.0 %collective-permute-start.11 = (bf16[512,128]{1,0:T(8,128)(2,1)S(1)}, bf16[512,128]{1,0:T(8,128)(2,1)S(1)}, u32[]{:S(2)}, u32[]{:S(2)}) collective-permute-start(bf16[512,128]{1,0:T(8,128)(2,1)S(1)} %add_add_fusion.1), channel_id=1, source_target_pairs={{0,8},{1,9},{2,10},{3,11},{4,12},{5,13},{6,14},{7,15},{32,40},{33,... | collective-permute-start | bytes 393224 | tf_op jit(solution)/shard_map/ppermute | solution.py:194
  24.0 9.4 %collective-permute-start.36 = (bf16[512,256]{1,0:T(8,128)(2,1)S(1)}, bf16[512,256]{1,0:T(8,128)(2,1)S(1)}, u32[]{:S(2)}, u32[]{:S(2)}) collective-permute-start(bf16[512,256]{1,0:T(8,128)(2,1)S(1)} %get-tuple-element.50), channel_id=1, source_target_pairs={{0,32},{32,64},{64,96},{96,0},{1,33},{33,65},{65,97},{97,1},{2,34}... | collective-permute-start | bytes 786440 | tf_op jit(solution)/shard_map/ppermute | solution.py:33
  25.5 27.1 %copy-start.9 = (bf16[256,128]{1,0:T(8,128)(2,1)}, bf16[256,128]{1,0:T(8,128)(2,1)S(1)}, u32[]{:S(2)}) copy-start(bf16[256,128]{1,0:T(8,128)(2,1)S(1)} %collective-permute-done.17) | copy-start | bytes 196612
  25.5 5.4 %collective-permute-start.12 = (bf16[512,128]{1,0:T(8,128)(2,1)S(1)}, bf16[512,128]{1,0:T(8,128)(2,1)S(1)}, u32[]{:S(2)}, u32[]{:S(2)}) collective-permute-start(bf16[512,128]{1,0:T(8,128)(2,1)S(1)} %add_add_fusion.1), channel_id=1, source_target_pairs={{0,16},{1,17},{2,18},{3,19},{4,20},{5,21},{6,22},{7,23},{32,48},{3... | collective-permute-start | bytes 393224 | tf_op jit(solution)/shard_map/ppermute | solution.py:194
  26.8 25.8 %copy-start.10 = (bf16[256,128]{1,0:T(8,128)(2,1)}, bf16[256,128]{1,0:T(8,128)(2,1)S(1)}, u32[]{:S(2)}) copy-start(bf16[256,128]{1,0:T(8,128)(2,1)S(1)} %collective-permute-done.18) | copy-start | bytes 196612
  26.8 6.9 %collective-permute-start.37 = (bf16[512,256]{1,0:T(8,128)(2,1)S(1)}, bf16[512,256]{1,0:T(8,128)(2,1)S(1)}, u32[]{:S(2)}, u32[]{:S(2)}) collective-permute-start(bf16[512,256]{1,0:T(8,128)(2,1)S(1)} %get-tuple-element.50), channel_id=1, source_target_pairs={{0,96},{32,0},{64,32},{96,64},{1,97},{33,1},{65,33},{97,65},{2,98}... | collective-permute-start | bytes 786440 | tf_op jit(solution)/shard_map/ppermute | solution.py:33
  27.4 2.1 copy-start.11
  27.4 11.2 %collective-permute-start.38 = (bf16[512,256]{1,0:T(8,128)(2,1)S(1)}, bf16[512,256]{1,0:T(8,128)(2,1)S(1)}, u32[]{:S(2)}, u32[]{:S(2)}) collective-permute-start(bf16[512,256]{1,0:T(8,128)(2,1)S(1)} %get-tuple-element.50), channel_id=1, source_target_pairs={{0,64},{32,96},{64,0},{96,32},{1,65},{33,97},{65,1},{97,33},{2,66}... | collective-permute-start | bytes 786440 | tf_op jit(solution)/shard_map/ppermute | solution.py:33
  29.6 3.8 %collective-permute-start.13 = (bf16[512,128]{1,0:T(8,128)(2,1)S(1)}, bf16[512,128]{1,0:T(8,128)(2,1)S(1)}, u32[]{:S(2)}, u32[]{:S(2)}) collective-permute-start(bf16[512,128]{1,0:T(8,128)(2,1)S(1)} %add_add_fusion.1), channel_id=1, source_target_pairs={{0,24},{1,25},{2,26},{3,27},{4,28},{5,29},{6,30},{7,31},{32,56},{3... | collective-permute-start | bytes 393224 | tf_op jit(solution)/shard_map/ppermute | solution.py:194
  30.9 29.1 %collective-permute-start = (bf16[512,512]{1,0:T(8,128)(2,1)S(1)}, bf16[512,512]{1,0:T(8,128)(2,1)S(1)}, u32[]{:S(2)}, u32[]{:S(2)}) collective-permute-start(bf16[512,512]{1,0:T(8,128)(2,1)S(1)} %copy-done.4), channel_id=1, source_target_pairs={{0,0},{8,32},{16,64},{24,96},{32,8},{40,40},{48,72},{56,104},{64,1... | collective-permute-start | bytes 1572872 | tf_op jit(solution)/shard_map/ppermute | solution.py:202
  33.4 15.8 %collective-permute-start.30 = (bf16[512,256]{1,0:T(8,128)(2,1)S(1)}, bf16[512,256]{1,0:T(8,128)(2,1)S(1)}, u32[]{:S(2)}, u32[]{:S(2)}) collective-permute-start(bf16[512,256]{1,0:T(8,128)(2,1)S(1)} %get-tuple-element.50), channel_id=1, source_target_pairs={{0,1},{1,0},{2,3},{3,2},{4,5},{5,4},{6,7},{7,6},{8,9},{9,8},{10,11... | collective-permute-start | bytes 786440 | tf_op jit(solution)/shard_map/ppermute | solution.py:41
  33.4 15.8 %collective-permute-start.20 = (bf16[512,256]{1,0:T(8,128)(2,1)S(1)}, bf16[512,256]{1,0:T(8,128)(2,1)S(1)}, u32[]{:S(2)}, u32[]{:S(2)}) collective-permute-start(bf16[512,256]{1,0:T(8,128)(2,1)S(1)} %get-tuple-element.51), channel_id=1, source_target_pairs={{0,2},{1,3},{2,4},{3,5},{4,6},{5,7},{6,0},{7,1},{8,10},{9,11},{10,... | collective-permute-start | bytes 786440 | tf_op jit(solution)/shard_map/ppermute | solution.py:37
  33.8 19.0 %collective-permute-start.21 = (bf16[512,256]{1,0:T(8,128)(2,1)S(1)}, bf16[512,256]{1,0:T(8,128)(2,1)S(1)}, u32[]{:S(2)}, u32[]{:S(2)}) collective-permute-start(bf16[512,256]{1,0:T(8,128)(2,1)S(1)} %get-tuple-element.51), channel_id=1, source_target_pairs={{0,6},{1,7},{2,0},{3,1},{4,2},{5,3},{6,4},{7,5},{8,14},{9,15},{10,... | collective-permute-start | bytes 786440 | tf_op jit(solution)/shard_map/ppermute | solution.py:37
  38.7 14.2 %collective-permute-start.22 = (bf16[512,256]{1,0:T(8,128)(2,1)S(1)}, bf16[512,256]{1,0:T(8,128)(2,1)S(1)}, u32[]{:S(2)}, u32[]{:S(2)}) collective-permute-start(bf16[512,256]{1,0:T(8,128)(2,1)S(1)} %get-tuple-element.51), channel_id=1, source_target_pairs={{0,4},{1,5},{2,6},{3,7},{4,0},{5,1},{6,2},{7,3},{8,12},{9,13},{10,... | collective-permute-start | bytes 786440 | tf_op jit(solution)/shard_map/ppermute | solution.py:37
  49.1 7.6 %collective-permute-start.14 = (bf16[512,128]{1,0:T(8,128)(2,1)S(1)}, bf16[512,128]{1,0:T(8,128)(2,1)S(1)}, u32[]{:S(2)}, u32[]{:S(2)}) collective-permute-start(bf16[512,128]{1,0:T(8,128)(2,1)S(1)} %add_add_fusion), channel_id=1, source_target_pairs={{0,32},{32,64},{64,96},{96,0},{1,33},{33,65},{65,97},{97,1},{2,34}... | collective-permute-start | bytes 393224 | tf_op jit(solution)/shard_map/ppermute | solution.py:33
  49.1 17.0 %collective-permute-start.31 = (bf16[512,256]{1,0:T(8,128)(2,1)S(1)}, bf16[512,256]{1,0:T(8,128)(2,1)S(1)}, u32[]{:S(2)}, u32[]{:S(2)}) collective-permute-start(bf16[512,256]{1,0:T(8,128)(2,1)S(1)} %collective-permute-done.30), channel_id=1, source_target_pairs={{0,32},{32,64},{64,96},{96,0},{1,33},{33,65},{65,97},{97,1},{2,34}... | collective-permute-start | bytes 786440 | tf_op jit(solution)/shard_map/ppermute | solution.py:33
  52.8 56.4 %copy-start.3 = (bf16[4,512,256]{2,1,0:T(8,128)(2,1)}, bf16[4,512,256]{2,1,0:T(8,128)(2,1)S(1)}, u32[]{:S(2)}) copy-start(bf16[4,512,256]{2,1,0:T(8,128)(2,1)S(1)} %pad_maximum_fusion.3.rest_0_) | copy-start | bytes 3145732
  52.8 7.4 %collective-permute-start.15 = (bf16[512,128]{1,0:T(8,128)(2,1)S(1)}, bf16[512,128]{1,0:T(8,128)(2,1)S(1)}, u32[]{:S(2)}, u32[]{:S(2)}) collective-permute-start(bf16[512,128]{1,0:T(8,128)(2,1)S(1)} %add_add_fusion), channel_id=1, source_target_pairs={{0,96},{32,0},{64,32},{96,64},{1,97},{33,1},{65,33},{97,65},{2,98}... | collective-permute-start | bytes 393224 | tf_op jit(solution)/shard_map/ppermute | solution.py:33
  52.9 11.2 %collective-permute-start.16 = (bf16[512,128]{1,0:T(8,128)(2,1)S(1)}, bf16[512,128]{1,0:T(8,128)(2,1)}, u32[]{:S(2)}, u32[]{:S(2)}) collective-permute-start(bf16[512,128]{1,0:T(8,128)(2,1)S(1)} %add_add_fusion), channel_id=1, source_target_pairs={{0,64},{32,96},{64,0},{96,32},{1,65},{33,97},{65,1},{97,33},{2,66}... | collective-permute-start | bytes 393224 | tf_op jit(solution)/shard_map/ppermute | solution.py:33
  56.8 11.0 %collective-permute-start.32 = (bf16[512,256]{1,0:T(8,128)(2,1)S(1)}, bf16[512,256]{1,0:T(8,128)(2,1)S(1)}, u32[]{:S(2)}, u32[]{:S(2)}) collective-permute-start(bf16[512,256]{1,0:T(8,128)(2,1)S(1)} %collective-permute-done.30), channel_id=1, source_target_pairs={{0,96},{32,0},{64,32},{96,64},{1,97},{33,1},{65,33},{97,65},{2,98}... | collective-permute-start | bytes 786440 | tf_op jit(solution)/shard_map/ppermute | solution.py:33
  60.0 49.2 %copy-start.7 = (bf16[512,512]{1,0:T(8,128)(2,1)}, bf16[512,512]{1,0:T(8,128)(2,1)S(1)}, u32[]{:S(2)}) copy-start(bf16[512,512]{1,0:T(8,128)(2,1)S(1)} %collective-permute-done) | copy-start | bytes 1572868
  60.0 17.9 %collective-permute-start.1 = (bf16[512,512]{1,0:T(8,128)(2,1)S(1)}, bf16[512,512]{1,0:T(8,128)(2,1)}, u32[]{:S(2)}, u32[]{:S(2)}) collective-permute-start(bf16[512,512]{1,0:T(8,128)(2,1)S(1)} %collective-permute-done), channel_id=1, source_target_pairs={{0,8},{8,0},{16,24},{24,16},{1,9},{9,1},{17,25},{25,17},{2,10},{10... | collective-permute-start | bytes 1572872 | tf_op jit(solution)/shard_map/ppermute | solution.py:203
  60.1 112.6 %copy-start.1 = (bf16[4,512,256]{2,1,0:T(8,128)(2,1)}, bf16[4,512,256]{2,1,0:T(8,128)(2,1)S(1)}, u32[]{:S(2)}) copy-start(bf16[4,512,256]{2,1,0:T(8,128)(2,1)S(1)} %pad_maximum_fusion.1.rest_0_) | copy-start | bytes 3145732
  60.2 41.7 %collective-permute-start.39 = (bf16[4,512,256]{2,1,0:T(8,128)(2,1)S(1)}, bf16[4,512,256]{2,1,0:T(8,128)(2,1)S(1)}, u32[]{:S(2)}, u32[]{:S(2)}) collective-permute-start(bf16[4,512,256]{2,1,0:T(8,128)(2,1)S(1)} %pad_maximum_fusion.3.rest_0_), channel_id=1, source_target_pairs={{0,2},{1,3},{2,4},{3,5},{4,6},{5,7},{6,0},{7,1},{8,10},{9,11},{10,... | collective-permute-start | bytes 3145736 | tf_op jit(solution)/shard_map/ppermute | solution.py:37
  64.1 40.2 %collective-permute-start.41 = (bf16[4,512,256]{2,1,0:T(8,128)(2,1)S(1)}, bf16[4,512,256]{2,1,0:T(8,128)(2,1)S(1)}, u32[]{:S(2)}, u32[]{:S(2)}) collective-permute-start(bf16[4,512,256]{2,1,0:T(8,128)(2,1)S(1)} %pad_maximum_fusion.3.rest_0_), channel_id=1, source_target_pairs={{0,6},{1,7},{2,0},{3,1},{4,2},{5,3},{6,4},{7,5},{8,14},{9,15},{10,... | collective-permute-start | bytes 3145736 | tf_op jit(solution)/shard_map/ppermute | solution.py:37
  66.1 38.2 %collective-permute-start.23 = (bf16[4,512,256]{2,1,0:T(8,128)(2,1)S(1)}, bf16[4,512,256]{2,1,0:T(8,128)(2,1)}, u32[]{:S(2)}, u32[]{:S(2)}) collective-permute-start(bf16[4,512,256]{2,1,0:T(8,128)(2,1)S(1)} %pad_maximum_fusion.1.rest_0_), channel_id=1, source_target_pairs={{0,1},{1,0},{2,3},{3,2},{4,5},{5,4},{6,7},{7,6},{8,9},{9,8},{10,11... | collective-permute-start | bytes 3145736 | tf_op jit(solution)/shard_map/ppermute | solution.py:41
  67.8 8.1 %collective-permute-start.33 = (bf16[512,256]{1,0:T(8,128)(2,1)S(1)}, bf16[512,256]{1,0:T(8,128)(2,1)S(1)}, u32[]{:S(2)}, u32[]{:S(2)}) collective-permute-start(bf16[512,256]{1,0:T(8,128)(2,1)S(1)} %collective-permute-done.30), channel_id=1, source_target_pairs={{0,64},{32,96},{64,0},{96,32},{1,65},{33,97},{65,1},{97,33},{2,66}... | collective-permute-start | bytes 786440 | tf_op jit(solution)/shard_map/ppermute | solution.py:33
  75.9 33.4 %collective-permute-start.27 = (bf16[4,512,256]{2,1,0:T(8,128)(2,1)S(1)}, bf16[4,512,256]{2,1,0:T(8,128)(2,1)}, u32[]{:S(2)}, u32[]{:S(2)}) collective-permute-start(bf16[4,512,256]{2,1,0:T(8,128)(2,1)S(1)} %pad_maximum_fusion.1.rest_0_), channel_id=1, source_target_pairs={{0,32},{32,64},{64,96},{96,0},{1,33},{33,65},{65,97},{97,1},{2,34}... | collective-permute-start | bytes 3145736 | tf_op jit(solution)/shard_map/ppermute | solution.py:33
  77.9 23.2 %collective-permute-start.2 = (bf16[512,512]{1,0:T(8,128)(2,1)S(1)}, bf16[512,512]{1,0:T(8,128)(2,1)S(1)}, u32[]{:S(2)}, u32[]{:S(2)}) collective-permute-start(bf16[512,512]{1,0:T(8,128)(2,1)S(1)} %collective-permute-done), channel_id=1, source_target_pairs={{0,16},{8,24},{16,0},{24,8},{1,17},{9,25},{17,1},{25,9},{2,18},{10... | collective-permute-start | bytes 1572872 | tf_op jit(solution)/shard_map/ppermute | solution.py:205
  79.1 95.4 %copy-start.2 = (bf16[4,512,256]{2,1,0:T(8,128)(2,1)}, bf16[4,512,256]{2,1,0:T(8,128)(2,1)S(1)}, u32[]{:S(2)}) copy-start(bf16[4,512,256]{2,1,0:T(8,128)(2,1)S(1)} %pad_maximum_fusion.2.rest_0_) | copy-start | bytes 3145732
  101.0 8.2 %copy-start.8 = (bf16[512,512]{1,0:T(8,128)(2,1)}, bf16[512,512]{1,0:T(8,128)(2,1)S(1)}, u32[]{:S(2)}) copy-start(bf16[512,512]{1,0:T(8,128)(2,1)S(1)} %collective-permute-done.2) | copy-start | bytes 1572868
  101.1 27.4 %collective-permute-start.42 = (bf16[4,512,256]{2,1,0:T(8,128)(2,1)S(1)}, bf16[4,512,256]{2,1,0:T(8,128)(2,1)}, u32[]{:S(2)}, u32[]{:S(2)}) collective-permute-start(bf16[4,512,256]{2,1,0:T(8,128)(2,1)S(1)} %pad_maximum_fusion.2.rest_0_), channel_id=1, source_target_pairs={{0,2},{1,3},{2,4},{3,5},{4,6},{5,7},{6,0},{7,1},{8,10},{9,11},{10,... | collective-permute-start | bytes 3145736 | tf_op jit(solution)/shard_map/ppermute | solution.py:37
  101.9 55.0 %copy-start.6 = (bf16[4,512,256]{2,1,0:T(8,128)(2,1)}, bf16[4,512,256]{2,1,0:T(8,128)(2,1)S(1)}, u32[]{:S(2)}) copy-start(bf16[4,512,256]{2,1,0:T(8,128)(2,1)S(1)} %collective-permute-done.39.rest_0_) | copy-start | bytes 3145732
  101.9 29.1 %collective-permute-start.34 = (bf16[4,512,256]{2,1,0:T(8,128)(2,1)S(1)}, bf16[4,512,256]{2,1,0:T(8,128)(2,1)}, u32[]{:S(2)}, u32[]{:S(2)}) collective-permute-start(bf16[4,512,256]{2,1,0:T(8,128)(2,1)S(1)} %pad_maximum_fusion.2.rest_0_), channel_id=1, source_target_pairs={{0,6},{1,7},{2,0},{3,1},{4,2},{5,3},{6,4},{7,5},{8,14},{9,15},{10,... | collective-permute-start | bytes 3145736 | tf_op jit(solution)/shard_map/ppermute | solution.py:37
  104.3 4.9 %copy-start.5 = (bf16[4,512,256]{2,1,0:T(8,128)(2,1)}, bf16[4,512,256]{2,1,0:T(8,128)(2,1)S(1)}, u32[]{:S(2)}) copy-start(bf16[4,512,256]{2,1,0:T(8,128)(2,1)S(1)} %collective-permute-done.41.rest_0_) | copy-start | bytes 3145732
  104.3 43.2 %collective-permute-start.40 = (bf16[4,512,256]{2,1,0:T(8,128)(2,1)S(1)}, bf16[4,512,256]{2,1,0:T(8,128)(2,1)}, u32[]{:S(2)}, u32[]{:S(2)}) collective-permute-start(bf16[4,512,256]{2,1,0:T(8,128)(2,1)S(1)} %collective-permute-done.39.rest_0_), channel_id=1, source_target_pairs={{0,2},{1,3},{2,4},{3,5},{4,6},{5,7},{6,0},{7,1},{8,10},{9,11},{10,... | collective-permute-start | bytes 3145736 | tf_op jit(solution)/shard_map/ppermute | solution.py:37
  104.3 45.0 %collective-permute-start.25 = (bf16[4,512,256]{2,1,0:T(8,128)(2,1)}, bf16[4,512,256]{2,1,0:T(8,128)(2,1)}, u32[]{:S(2)}, u32[]{:S(2)}) collective-permute-start(bf16[4,512,256]{2,1,0:T(8,128)(2,1)} %collective-permute-done.23.rest_0_), channel_id=1, source_target_pairs={{0,96},{32,0},{64,32},{96,64},{1,97},{33,1},{65,33},{97,65},{2,98}... | collective-permute-start | bytes 3145736 | tf_op jit(solution)/shard_map/ppermute | solution.py:33
  109.2 13.6 %collective-permute-start.3 = (bf16[512,512]{1,0:T(8,128)(2,1)}, bf16[512,512]{1,0:T(8,128)(2,1)}, u32[]{:S(2)}, u32[]{:S(2)}) collective-permute-start(bf16[512,512]{1,0:T(8,128)(2,1)} %collective-permute-done.1), channel_id=1, source_target_pairs={{0,16},{8,24},{16,0},{24,8},{1,17},{9,25},{17,1},{25,9},{2,18},{10... | collective-permute-start | bytes 1572872 | tf_op jit(solution)/shard_map/ppermute | solution.py:205
  122.8 103.3 %collective-permute-start.28 = (bf16[4,512,256]{2,1,0:T(8,128)(2,1)S(1)}, bf16[4,512,256]{2,1,0:T(8,128)(2,1)}, u32[]{:S(2)}, u32[]{:S(2)}) collective-permute-start(bf16[4,512,256]{2,1,0:T(8,128)(2,1)S(1)} %pad_maximum_fusion.1.rest_0_), channel_id=1, source_target_pairs={{0,96},{32,0},{64,32},{96,64},{1,97},{33,1},{65,33},{97,65},{2,98}... | collective-permute-start | bytes 3145736 | tf_op jit(solution)/shard_map/ppermute | solution.py:33
  128.5 108.0 %collective-permute-start.24 = (bf16[4,512,256]{2,1,0:T(8,128)(2,1)}, bf16[4,512,256]{2,1,0:T(8,128)(2,1)}, u32[]{:S(2)}, u32[]{:S(2)}) collective-permute-start(bf16[4,512,256]{2,1,0:T(8,128)(2,1)} %collective-permute-done.23.rest_0_), channel_id=1, source_target_pairs={{0,32},{32,64},{64,96},{96,0},{1,33},{33,65},{65,97},{97,1},{2,34}... | collective-permute-start | bytes 3145736 | tf_op jit(solution)/shard_map/ppermute | solution.py:33
  130.9 95.1 %collective-permute-start.29 = (bf16[4,512,256]{2,1,0:T(8,128)(2,1)}, bf16[4,512,256]{2,1,0:T(8,128)(2,1)}, u32[]{:S(2)}, u32[]{:S(2)}) collective-permute-start(bf16[4,512,256]{2,1,0:T(8,128)(2,1)} %collective-permute-done.27.rest_1_), channel_id=1, source_target_pairs={{0,32},{32,64},{64,96},{96,0},{1,33},{33,65},{65,97},{97,1},{2,34}... | collective-permute-start | bytes 3145736 | tf_op jit(solution)/shard_map/ppermute | solution.py:33
  147.5 73.3 %collective-permute-start.35 = (bf16[4,512,256]{2,1,0:T(8,128)(2,1)}, bf16[4,512,256]{2,1,0:T(8,128)(2,1)}, u32[]{:S(2)}, u32[]{:S(2)}) collective-permute-start(bf16[4,512,256]{2,1,0:T(8,128)(2,1)} %collective-permute-done.34.rest_0_), channel_id=1, source_target_pairs={{0,6},{1,7},{2,0},{3,1},{4,2},{5,3},{6,4},{7,5},{8,14},{9,15},{10,... | collective-permute-start | bytes 3145736 | tf_op jit(solution)/shard_map/ppermute | solution.py:37
  149.3 87.2 %collective-permute-start.26 = (bf16[4,512,256]{2,1,0:T(8,128)(2,1)}, bf16[4,512,256]{2,1,0:T(8,128)(2,1)}, u32[]{:S(2)}, u32[]{:S(2)}) collective-permute-start(bf16[4,512,256]{2,1,0:T(8,128)(2,1)} %collective-permute-done.25.rest_2_), channel_id=1, source_target_pairs={{0,96},{32,0},{64,32},{96,64},{1,97},{33,1},{65,33},{97,65},{2,98}... | collective-permute-start | bytes 3145736 | tf_op jit(solution)/shard_map/ppermute | solution.py:33
  157.9 0.8 copy-start

commit v2 on v1

v2 whole, which is shorter than its diff:
```python
import functools

import jax
import jax.numpy as jnp
from jax import lax
from jax.experimental import pallas as pl
from jax.experimental.pallas import tpu as pltpu
from jax.sharding import PartitionSpec as P

PANEL = 128
KEEP = 8
DAMPING = 0.01

NX = 4
NY = 4
NZ = 2
NROW = 4
VMEM_LIMIT = 56 * 1024 * 1024


def x_perm(k):
    return [(i, (i + k) % NX) for i in range(NX)]


def y_perm(k):
    return [(y * NZ + z, ((y + k) % NY) * NZ + z) for y in range(NY) for z in range(NZ)]


Z_PERM = [(y * NZ + z, y * NZ + 1 - z) for y in range(NY) for z in range(NZ)]


def send_x(a, k):
    return lax.ppermute(a, "dp", x_perm(k))


def send_y(a, k):
    return lax.ppermute(a, "col", y_perm(k))


def send_z(a):
    return lax.ppermute(a, "col", Z_PERM)


SHIFTS = (0, -1, 1, 2)


def ring_near(a, send):
    return send(a, 1), send(a, -1)


def ring_out(a, b, send):
    return send(a, 1), send(b, -1)


def ring_in(a, b, send):
    return send(b, 1), send(a, -1)


def ring_far(left, right, send):
    mid = left.shape[0] // 2
    return send(left[:mid], 1), send(right[mid:], -1)


def panel_kernel(ap_ref, wp_ref, mask_ref, rank_ref, corr_ref, panel_ref):
    hess = jnp.zeros((PANEL, PANEL), jnp.float32)
    for k in range(NX):
        blk = ap_ref[k]
        hess += lax.dot_general(blk, blk, (((0,), (0,)), ((), ())), preferred_element_type=jnp.float32)
    tokens = NX * ap_ref.shape[1]
    row = lax.broadcasted_iota(jnp.int32, (PANEL, PANEL), 0)
    col = lax.broadcasted_iota(jnp.int32, (PANEL, PANEL), 1)
    hess = hess * (2.0 / tokens) + jnp.where(row == col, DAMPING, 0.0)
    lane = lax.broadcasted_iota(jnp.int32, (1, PANEL), 1)
    tiles = [hess[8 * t : 8 * t + 8] for t in range(PANEL // 8)]
    ratio = [None] * PANEL
    for j in reversed(range(PANEL)):
        own = tiles[j // 8][j % 8 : j % 8 + 1]
        r = own / own[:, j : j + 1]
        ratio[j] = jnp.where(lane < j, r, 0.0)
        for t in range((j + 7) // 8):
            tiles[t] = tiles[t] - tiles[t][:, j : j + 1] * r
    ratio_tiles = [jnp.concatenate(ratio[8 * t : 8 * t + 8], axis=0) for t in range(PANEL // 8)]

    keep = jnp.where((mask_ref[...] == 1) | (rank_ref[...] < KEEP), 1.0, 0.0)
    keep_t = keep.T
    w_t = wp_ref[...].astype(jnp.float32).T
    rows = w_t.shape[1]
    acc = [jnp.zeros((8, rows), jnp.float32) for _ in range(PANEL // 8)]
    corr = [None] * PANEL
    for j in range(PANEL):
        c = jnp.where(keep_t[j : j + 1] > 0.5, -acc[j // 8][j % 8 : j % 8 + 1], w_t[j : j + 1])
        corr[j] = c
        for t in range((j + 1) // 8, PANEL // 8):
            acc[t] = acc[t] + ratio_tiles[t][:, j : j + 1] * c
    corr_t = jnp.concatenate(corr, axis=0)
    corr_ref[...] = corr_t.T
    panel_ref[...] = jnp.where(keep_t > 0.5, w_t - corr_t, 0.0).T.astype(panel_ref.dtype)


def panel_step(ap, wp, mask, rank):
    rows = wp.shape[0]
    return pl.pallas_call(
        panel_kernel,
        out_shape=(
            jax.ShapeDtypeStruct((rows, PANEL), jnp.float32),
            jax.ShapeDtypeStruct((rows, PANEL), jnp.bfloat16),
        ),
        compiler_params=pltpu.CompilerParams(vmem_limit_bytes=VMEM_LIMIT),
        cost_estimate=pl.CostEstimate(flops=1 << 33, transcendentals=0, bytes_accessed=1 << 25),
        name="panel_sweep",
    )(ap, wp, mask, rank.reshape(1, PANEL))


def lhs_kernel(block, info, own_ref, own_z_ref, core_ref, ap_ref, lhs_ref):
    tok = own_ref.shape[0]
    for m, piece in enumerate((own_ref, core_ref.at[0], own_z_ref, core_ref.at[1])):
        lhs_ref[:block, pl.ds(pl.multiple_of(info[m] * tok, tok), tok)] = piece[...].T
    for k in range(NX):
        lhs_ref[block:, k * tok : (k + 1) * tok] = ap_ref[k].T


def lhs_step(slots, own, own_z, core, ap):
    tok, block = own.shape
    shape = (block + PANEL, NX * tok)
    whole = pl.BlockSpec(memory_space=pltpu.VMEM)
    return pl.pallas_call(
        functools.partial(lhs_kernel, block),
        out_shape=jax.ShapeDtypeStruct(shape, own.dtype),
        in_specs=[pl.BlockSpec(memory_space=pltpu.SMEM)] + [whole] * 4,
        out_specs=whole,
        compiler_params=pltpu.CompilerParams(vmem_limit_bytes=VMEM_LIMIT),
        cost_estimate=pl.CostEstimate(flops=1 << 31, transcendentals=0, bytes_accessed=1 << 23),
        name="lhs",
    )(slots, own, own_z, core, ap)


def columns_kernel(pairs, tok, width, n_pieces, has_in, has_out, info, lhs_ref, corr_ref, panel_ref, w_hbm, *rest):
    pieces = rest[:n_pieces]
    part_in = rest[n_pieces] if has_in else None
    x_buf, w_buf, out_buf, hess_buf, part_buf, in_sem, out_sem = rest[-7:]
    outs = rest[-10:-7] if has_out else (*rest[-9:-7], None)
    out_hbm, hess_hbm, part_out = outs
    rows = hess_buf.shape[1]
    all_rows = lhs_ref.shape[0]
    scale = 2.0 / (NX * tok)

    def column(p, h):
        return pl.multiple_of(info[2 + 2 * p + h] * width, width)

    def loads(p):
        slot = p % 2
        low, high, places, begin, leave = pairs[p]
        copies = []
        for h in range(2):
            lanes = pl.ds(h * width, width)
            for k in range(high - low):
                which, lead = places[h][k]
                copies.append((pieces[which].at[lead], x_buf.at[slot, pl.ds(k * tok, tok), lanes]))
            if leave is None:
                copies.append((w_hbm.at[:, pl.ds(column(p, h), width)], w_buf.at[slot, :, lanes]))
        if begin is not None:
            copies.append((part_in.at[begin], part_buf.at[slot]))
        return [pltpu.make_async_copy(a, b, in_sem.at[slot, n]) for n, (a, b) in enumerate(copies)]

    def stores(p):
        slot = p % 2
        leave = pairs[p][4]
        copies = []
        if leave is not None:
            copies.append((part_buf.at[slot], part_out.at[leave]))
        else:
            for h in range(2):
                lanes = pl.ds(h * width, width)
                copies.append((hess_buf.at[slot, :, lanes], hess_hbm.at[:, pl.ds(column(p, h), width)]))
                copies.append((out_buf.at[slot, :, lanes], out_hbm.at[:, pl.ds(column(p, h), width)]))
        return [pltpu.make_async_copy(a, b, out_sem.at[slot, n]) for n, (a, b) in enumerate(copies)]

    for copy in loads(0):
        copy.start()
    for p in range(len(pairs)):
        slot = p % 2
        low, high, _, begin, leave = pairs[p]
        if p + 1 < len(pairs):
            for copy in loads(p + 1):
                copy.start()
        for copy in loads(p):
            copy.wait()
        if p >= 2:
            for copy in stores(p - 2):
                copy.wait()
        x = x_buf[slot, : (high - low) * tok]
        acc = jnp.dot(lhs_ref[:, low * tok : high * tok], x, preferred_element_type=jnp.float32)
        wide = x.astype(jnp.float32)
        diag = jnp.sum(wide * wide, axis=0, keepdims=True)
        if begin is not None:
            acc = acc + part_buf[slot, :all_rows]
            diag = diag + part_buf[slot, all_rows : all_rows + 1]
        if leave is not None:
            part_buf[slot, :all_rows] = acc
            part_buf[slot, all_rows:] = jnp.broadcast_to(diag, (8, 2 * width))
        else:
            acc = acc * scale
            diag = diag * scale + DAMPING
            change = jnp.dot(
                corr_ref[...],
                acc[rows:] / diag,
                precision=lax.Precision.HIGHEST,
                preferred_element_type=jnp.float32,
            )
            out_buf[slot] = (w_buf[slot].astype(jnp.float32) + change).astype(out_buf.dtype)
            row = lax.broadcasted_iota(jnp.int32, (rows, width), 0)
            col = lax.broadcasted_iota(jnp.int32, (rows, width), 1)
            for h in range(2):
                lanes = slice(h * width, (h + 1) * width)
                col0 = info[0] + column(p, h)
                hess_buf[slot, :, lanes] = acc[:rows, lanes] + jnp.where(row - col == col0 - info[1], DAMPING, 0.0)

                @pl.when(col0 == 0)
                def _():
                    out_buf[slot, :, h * width : h * width + PANEL] = panel_ref[...]

        for copy in stores(p):
            copy.start()
    for p in range(max(0, len(pairs) - 2), len(pairs)):
        for copy in stores(p):
            copy.wait()


def columns_step(base, lhs, corr, panel, weight, pieces, entries, low, high, begin, leave, parts, out, hess):
    tok, width = pieces[0].shape[1:]
    out_rows, chans = weight.shape
    rows = lhs.shape[0] - PANEL
    info = jnp.concatenate([base, jnp.stack([place for place, _ in entries])]).astype(jnp.int32)
    pairs = [
        (low[i], high[i], (entries[2 * i][1], entries[2 * i + 1][1]), begin[i], leave[i])
        for i in range(len(entries) // 2)
    ]
    n_out = sum(a is not None for a in leave)
    fixed = lambda i, info: (0, 0)
    anywhere = pl.BlockSpec(memory_space=pltpu.HBM)
    operands = [lhs, corr, panel, weight, *pieces]
    if parts is not None:
        operands.append(parts)
    in_specs = [pl.BlockSpec(a.shape, fixed) for a in (lhs, corr, panel)] + [anywhere] * (len(operands) - 3)
    aliases = {}
    if out is not None:
        in_specs += [anywhere] * 2
        operands += [out, hess]
        aliases = {len(operands) - 1: 0, len(operands): 1}
    part = (lhs.shape[0] + 8, 2 * width)
    out_shape = [
        jax.ShapeDtypeStruct((out_rows, chans), weight.dtype),
        jax.ShapeDtypeStruct((rows, chans), jnp.float32),
    ]
    if n_out:
        out_shape.append(jax.ShapeDtypeStruct((n_out, *part), jnp.float32))
    body = functools.partial(columns_kernel, pairs, tok, width, len(pieces), parts is not None, n_out > 0)
    total = len(entries) * width
    return pl.pallas_call(
        body,
        grid_spec=pltpu.PrefetchScalarGridSpec(
            num_scalar_prefetch=1,
            grid=(1,),
            in_specs=in_specs,
            out_specs=[anywhere] * len(out_shape),
            scratch_shapes=[
                pltpu.VMEM((2, NX * tok, 2 * width), jnp.bfloat16),
                pltpu.VMEM((2, out_rows, 2 * width), weight.dtype),
                pltpu.VMEM((2, out_rows, 2 * width), weight.dtype),
                pltpu.VMEM((2, rows, 2 * width), jnp.float32),
                pltpu.VMEM((2, *part), jnp.float32),
                pltpu.SemaphoreType.DMA((2, 2 * NX + 3)),
                pltpu.SemaphoreType.DMA((2, 4)),
            ],
        ),
        out_shape=out_shape,
        input_output_aliases=aliases,
        compiler_params=pltpu.CompilerParams(vmem_limit_bytes=VMEM_LIMIT),
        cost_estimate=pl.CostEstimate(
            flops=2 * total * NX * tok * lhs.shape[0],
            transcendentals=0,
            bytes_accessed=total * (NX * tok * 2 + rows * 4 + out_rows * 4) + lhs.size * 2,
        ),
        name="columns",
    )(info, *operands)


def body(activation, weight, prune_mask, channel_rank):
    tok, block = activation.shape
    chans = weight.shape[1]
    d, r, c = lax.axis_index("dp"), lax.axis_index("row"), lax.axis_index("col")
    y, z = c // NZ, c % NZ
    ncol = NY * NZ
    half = block // 2

    other = send_z(activation)

    everywhere = ("dp", "row", "col")
    per_x = NROW * ncol
    ap = jnp.where((r == 0) & (c == 0), activation[:, :PANEL], jnp.zeros((tok, PANEL), activation.dtype))
    ap = functools.reduce(
        jnp.add, [lax.ppermute(ap, ("row", "col"), [(0, k * NZ)]) for k in range(1, NY)], ap
    )
    ap, other, activation = lax.optimization_barrier((ap, other, activation))
    swap = [(i * NROW + j, j * NROW + i) for i in range(NX) for j in range(NROW)]
    own = lax.ppermute(activation, ("dp", "row"), swap)
    ap = jnp.concatenate(
        [ap]
        + [
            lax.ppermute(ap, everywhere, [(a * per_x + k * NZ, b * per_x + k * NZ) for a, b in x_perm(s) for k in range(NY)])
            for s in (1, -1, 2)
        ]
    )
    other, ap, activation = lax.optimization_barrier((other, ap, activation))

    first = jnp.stack([activation[:, :half], other[:, :half]])
    second = jnp.stack([activation[:, half:], other[:, half:]])
    first_left, first_right = ring_near(first, send_y)
    second_left, second_right = ring_near(second, send_x)
    ap = ap + lax.ppermute(ap, ("row", "col"), [(i, i + 1) for i in range(0, ncol, NZ)])
    first_left, first_right, second_left, second_right, ap = lax.optimization_barrier(
        (first_left, first_right, second_left, second_right, ap)
    )
    first_far = ring_far(first_left, first_right, send_y)
    second_far = ring_far(second_left, second_right, send_x)
    wp = jnp.where(r == 0, weight[:, :PANEL], jnp.zeros_like(weight[:, :PANEL]))
    both = jnp.concatenate([ap, wp])
    both = both + lax.ppermute(both, "row", [(0, 1)])
    both = both + lax.ppermute(both, "row", [(0, 2), (1, 3)])
    first = (jnp.concatenate([first, first_left]), jnp.concatenate([first_right, *first_far]))
    second = (jnp.concatenate([second, second_left]), jnp.concatenate([second_right, *second_far]))
    first, second, both, own = lax.optimization_barrier((first, second, both, own))

    first_out, second_out = ring_out(*first, send_x), ring_out(*second, send_y)
    ap, wp = both[: NX * tok].reshape(NX, tok, PANEL), both[NX * tok :]
    corr, panel = panel_step(ap, wp, prune_mask, channel_rank)
    own_z = lax.ppermute(own, "row", [(i, i ^ 2) for i in range(NROW)])
    first, second, first_out, second_out, corr, own_z = lax.optimization_barrier(
        (first, second, first_out, second_out, corr, own_z)
    )
    first_in, second_in = ring_in(*first, send_x), ring_in(*second, send_y)
    core = lax.ppermute(jnp.stack([own, own_z]), "row", [(i, i ^ 1) for i in range(NROW)])
    order = jnp.array([0, 2, 3, 1], jnp.int32)
    lhs = lhs_step(order[((r ^ jnp.arange(NROW)) - d) % NX], own, own_z, core, ap)
    first_out, second_out, first_in, second_in, lhs = lax.optimization_barrier(
        (first_out, second_out, first_in, second_in, lhs)
    )
    first_far, second_far = ring_out(*first_out, send_x), ring_out(*second_out, send_y)

    base = jnp.stack([r * chans, (d * ncol + c) * block])
    step = functools.partial(columns_step, base, lhs, corr, panel, weight)

    def place(dy, dz, part):
        return (((y + dy) % NY) * NZ + (z + dz) % NZ) * 2 + part

    def second_entries(shifts):
        return [
            (place(s, dz, 1), [(2 * i + k // 2, (k % 2) * NZ + dz) for k in range(NX)])
            for i, s in enumerate(shifts)
            for dz in range(NZ)
        ]

    def first_entries(skip, ks):
        return [
            (place(s, dz, 0), [(skip + 2 * k + i // 2, (i % 2) * NZ + dz) for k in ks])
            for i, s in enumerate(SHIFTS)
            for dz in range(NZ)
        ]

    far = NX - 1
    pieces = [*second, second_out[0], second_in[0], second_in[1], second_out[1]]
    skip = len(pieces)
    pieces += [*first, first_out[0], first_in[0], first_in[1], first_out[1]]
    entries = second_entries(SHIFTS[:far]) + first_entries(skip, range(far))
    none, slots = [None] * NX, list(range(NX))
    out, hess, parts = step(
        pieces, entries, [0] * 7, [NX] * 3 + [far] * 4, [None] * 7, none[:3] + slots, None, None, None
    )
    entries = second_entries(SHIFTS[far:])
    entries += [(place, [(2 + which, lead)]) for place, ((which, lead),) in first_entries(0, [0])]
    out, hess = step(
        [*second_far, *first_far], entries, [0] + [far] * 4, [NX] * 5, [None] + slots, [None] * 5, parts, out, hess
    )
    return (out, hess)


def solution(mesh):
    return jax.shard_map(
        body,
        mesh=mesh,
        in_specs=(P("dp", ("row", "col")), P(("dp", "col"), "row"), P(("dp", "col"), None), P()),
        out_specs=(P(("dp", "col"), "row"), P(("dp", "col"), "row")),
        check_vma=False,
    )
```

time: 248 us -> 178 us (0.72)
  the two profiles are of different devices: /device:TPU:2 before, /device:TPU:64 now
where the time goes in v2:
time: 178 us; the launch traced here: 177 us
  waiting for transfers between devices  60.9 us (34%)
  starting transfers between devices  53.8 us (30%)
  Pallas kernels  49.7 us (28%)
  other arithmetic  6.91 us (4%)
  local copies, waits for them, and re-layouts  5.03 us (3%)
    ppermute x10, waiting for transfers between devices, send_x(): return lax.ppermute(a, 'dp', x_perm(k))  39.2 us
    pallas_call x2, Pallas kernels, columns_step(): pl.pallas_call(body, grid_spec=pltpu.PrefetchScalarGridSpec(num_scalar_pr...  31.6 us
    ppermute x10, starting transfers between devices, send_y(): return lax.ppermute(a, 'col', y_perm(k))  16.4 us
    ppermute x1, starting transfers between devices, body(): own = lax.ppermute(activation, ('dp', 'row'), swap)  15.8 us
    pallas_call x1, Pallas kernels, panel_step(): pl.pallas_call(panel_kernel, out_shape=(jax.ShapeDtypeStruct((rows, PANEL...  14.1 us
    ppermute x10, starting transfers between devices, send_x(): return lax.ppermute(a, 'dp', x_perm(k))  13.2 us
    ppermute x1, waiting for transfers between devices, send_z(): return lax.ppermute(a, 'col', Z_PERM)  8.28 us
    ppermute x10, waiting for transfers between devices, send_y(): return lax.ppermute(a, 'col', y_perm(k))  6.8 us
  transfers between devices with their start and end apart: 33, of which 13 were waited for; matrix products, arithmetic and copies ran while one was open for 5% of the time, Pallas kernels for 20%

profile of v2, /device:TPU:64, one launch (start us, length us, event | category | flops | bytes accessed | tf_op | source)
XLA Modules:
  0.0 177.5 jit_solution(1694604167625356551)
XLA Ops:
  0.6 1.7 collective-permute-start.3
  2.3 0.9 slice_select_fusion
  3.3 0.7 collective-permute-start
  4.0 0.7 collective-permute-start.1
  4.7 0.7 collective-permute-start.2
  5.4 1.0 add_add_fusion
  6.3 8.3 %collective-permute-done.3 = bf16[512,512]{1,0:T(8,128)(2,1)S(1)} collective-permute-done((bf16[512,512]{1,0:T(8,128)(2,1)}, bf16[512,512]{1,0:T(8,128)(2,1)S(1)}, u32[]{:S(2)}, u32[]{:S(2)}) %collective-permute-start.3) | collective-permute-done | bytes 524320 | tf_op jit(solution)/shard_map/ppermute | solution.py:41
  14.6 0.7 collective-permute-start.4
  15.3 0.7 collective-permute-start.5
  15.9 0.7 collective-permute-start.6
  16.7 0.1 slice_bitcast_fusion
  16.8 2.8 %collective-permute-start.10 = (bf16[2,512,256]{2,1,0:T(8,128)(2,1)S(1)}, bf16[2,512,256]{2,1,0:T(8,128)(2,1)S(1)}, u32[]{:S(2)}, u32[]{:S(2)}) collective-permute-start(bf16[2,512,256]{2,1,0:T(8,128)(2,1)S(1)} %pad_maximum_fusion.8), channel_id=1, source_target_pairs={{0,96},{32,0},{64,32},{96,64},{1,97},{33,1},{65,33},{97,65},{2,98}... | collective-permute-start | bytes 1572872 | tf_op jit(solution)/shard_map/ppermute | solution.py:33
  19.7 0.7 collective-permute-start.11
  20.4 0.1 pad_maximum_fusion.7
  20.4 1.6 collective-permute-start.7
  22.1 1.7 collective-permute-start.8
  23.7 0.8 slice_select_fusion.1
  24.6 0.1 add.236
  24.7 5.2 %collective-permute-done.10 = bf16[2,512,256]{2,1,0:T(8,128)(2,1)S(1)} collective-permute-done((bf16[2,512,256]{2,1,0:T(8,128)(2,1)S(1)}, bf16[2,512,256]{2,1,0:T(8,128)(2,1)S(1)}, u32[]{:S(2)}, u32[]{:S(2)}) %collective-permute-start.10) | collective-permute-done | bytes 524320 | tf_op jit(solution)/shard_map/ppermute | solution.py:33
  30.0 3.4 %collective-permute-done.9 = bf16[2,512,256]{2,1,0:T(8,128)(2,1)S(1)} collective-permute-done((bf16[2,512,256]{2,1,0:T(8,128)(2,1)S(1)}, bf16[2,512,256]{2,1,0:T(8,128)(2,1)S(1)}, u32[]{:S(2)}, u32[]{:S(2)}) %collective-permute-start.9) | collective-permute-done | bytes 524320 | tf_op jit(solution)/shard_map/ppermute | solution.py:33
  33.4 0.9 collective-permute-done.7
  34.3 0.7 collective-permute-start.16
  35.1 0.5 collective-permute-start.14
  35.6 0.2 fusion.2
  35.8 1.3 collective-permute-start.17
  37.1 15.8 %collective-permute-start.18 = (bf16[512,512]{1,0:T(8,128)(2,1)S(1)}, bf16[512,512]{1,0:T(8,128)(2,1)S(1)}, u32[]{:S(2)}, u32[]{:S(2)}) collective-permute-start(bf16[512,512]{1,0:T(8,128)(2,1)S(1)} %copy-done.1), channel_id=1, source_target_pairs={{0,0},{8,32},{16,64},{24,96},{32,8},{40,40},{48,72},{56,104},{64,1... | collective-permute-start | bytes 1572872 | tf_op jit(solution)/shard_map/ppermute | solution.py:306
  52.9 0.1 collective-permute-start.15
  53.0 1.6 collective-permute-start.12
  54.7 0.1 pad_maximum_fusion.2.rest_0_
  54.8 1.7 collective-permute-start.13
  56.5 0.1 pad_maximum_fusion.rest_6_
  56.7 8.3 %collective-permute-done.15 = bf16[1,512,256]{2,1,0:T(8,128)(2,1)S(1)} collective-permute-done((bf16[1,512,256]{2,1,0:T(8,128)(2,1)S(1)}, bf16[1,512,256]{2,1,0:T(8,128)(2,1)S(1)}, u32[]{:S(2)}, u32[]{:S(2)}) %collective-permute-start.15) | collective-permute-done | bytes 262176 | tf_op jit(solution)/shard_map/ppermute | solution.py:33
  64.9 1.2 pad_maximum_fusion.3.rest_1_
  66.1 1.1 pad_maximum_fusion.1.rest_7_
  67.2 6.6 %collective-permute-done.17 = bf16[2304,128]{1,0:T(8,128)(2,1)S(1)} collective-permute-done((bf16[2304,128]{1,0:T(8,128)(2,1)S(1)}, bf16[2304,128]{1,0:T(8,128)(2,1)S(1)}, u32[]{:S(2)}, u32[]{:S(2)}) %collective-permute-start.17) | collective-permute-done | bytes 589856 | tf_op jit(solution)/shard_map/ppermute | solution.py:329
  73.8 0.2 add.238
  74.0 0.3 collective-permute-start.19
  74.4 3.0 %collective-permute-start.20 = (bf16[4,512,256]{2,1,0:T(8,128)(2,1)}, bf16[4,512,256]{2,1,0:T(8,128)(2,1)}, u32[]{:S(2)}, u32[]{:S(2)}) collective-permute-start(bf16[4,512,256]{2,1,0:T(8,128)(2,1)} %pad_maximum_fusion.1.rest_7_), channel_id=1, source_target_pairs={{0,96},{32,0},{64,32},{96,64},{1,97},{33,1},{65,33},{97,65},{2,98}... | collective-permute-start | bytes 3145736 | tf_op jit(solution)/shard_map/ppermute | solution.py:33
  77.3 1.6 collective-permute-start.21
  78.9 1.7 collective-permute-start.22
  80.6 0.8 slice.46
  81.4 0.6 slice.47.wp_ref
  82.0 14.1 %panel_sweep.1 = (f32[256,128]{1,0:T(8,128)}, bf16[256,128]{1,0:T(8,128)(2,1)}) custom-call(bf16[4,512,128]{2,1,0:T(8,128)(2,1)} %bitcast.32, bf16[256,128]{1,0:T(8,128)(2,1)} %slice.47.wp_ref, s32[256,128]{1,0:T(8,128)} %mask_ref.1, s32[1,128]{1,0:T(1,128)} %bitcast.36), custom_call_target="tpu_custom_call" | custom-call | flops 8589934592 | bytes 33554432 | tf_op jit(solution)/shard_map/panel_sweep/pallas_call | solution.py:102
  96.1 4.2 %collective-permute-done.19.rest_8_ = bf16[4,512,256]{2,1,0:T(8,128)(2,1)} collective-permute-done((bf16[4,512,256]{2,1,0:T(8,128)(2,1)S(1)}, bf16[4,512,256]{2,1,0:T(8,128)(2,1)}, u32[]{:S(2)}, u32[]{:S(2)}) %collective-permute-start.19) | collective-permute-done | bytes 1048608 | tf_op jit(solution)/shard_map/ppermute | solution.py:33
  100.3 2.7 %collective-permute-done.21.rest_2_ = bf16[4,512,256]{2,1,0:T(8,128)(2,1)} collective-permute-done((bf16[4,512,256]{2,1,0:T(8,128)(2,1)S(1)}, bf16[4,512,256]{2,1,0:T(8,128)(2,1)}, u32[]{:S(2)}, u32[]{:S(2)}) %collective-permute-start.21) | collective-permute-done | bytes 1048608 | tf_op jit(solution)/shard_map/ppermute | solution.py:37
  102.9 0.3 collective-permute-done.22.rest_5_
  103.2 1.1 pad_maximum_fusion.4
  104.3 3.2 %collective-permute-start.25 = (bf16[4,512,256]{2,1,0:T(8,128)(2,1)S(1)}, bf16[4,512,256]{2,1,0:T(8,128)(2,1)}, u32[]{:S(2)}, u32[]{:S(2)}) collective-permute-start(bf16[4,512,256]{2,1,0:T(8,128)(2,1)S(1)} %pad_maximum_fusion.rest_6_), channel_id=1, source_target_pairs={{0,96},{32,0},{64,32},{96,64},{1,97},{33,1},{65,33},{97,65},{2,98}... | collective-permute-start | bytes 3145736 | tf_op jit(solution)/shard_map/ppermute | solution.py:33
  107.5 1.3 collective-permute-start.26
  108.8 1.9 %collective-permute-start.27 = (bf16[4,512,256]{2,1,0:T(8,128)(2,1)S(1)}, bf16[4,512,256]{2,1,0:T(8,128)(2,1)}, u32[]{:S(2)}, u32[]{:S(2)}) collective-permute-start(bf16[4,512,256]{2,1,0:T(8,128)(2,1)S(1)} %pad_maximum_fusion.2.rest_0_), channel_id=1, source_target_pairs={{0,6},{1,7},{2,0},{3,1},{4,2},{5,3},{6,4},{7,5},{8,14},{9,15},{10,... | collective-permute-start | bytes 3145736 | tf_op jit(solution)/shard_map/ppermute | solution.py:37
  110.8 1.2 gather_fusion
  112.0 4.0 %lhs.1.lhs_ref = bf16[640,2048]{1,0:T(8,128)(2,1)} custom-call(s32[4]{0:T(128)} %gather_fusion, bf16[512,512]{1,0:T(8,128)(2,1)} %copy-done.7, bf16[512,512]{1,0:T(8,128)(2,1)} %copy-done.8, bf16[2,512,512]{2,1,0:T(8,128)(2,1)} %collective-permute-done.28.core_ref, bf16[4,512,128]{2,1,0:T(8,128)(2,1)} %bitcast.33), custom_call_target="tpu_custom_call" | custom-call | flops 2147483648 | bytes 8388608 | tf_op jit(solution)/shard_map/lhs/pallas_call | solution.py:126
  116.0 15.4 %collective-permute-done.24.rest_9_ = bf16[4,512,256]{2,1,0:T(8,128)(2,1)} collective-permute-done((bf16[4,512,256]{2,1,0:T(8,128)(2,1)}, bf16[4,512,256]{2,1,0:T(8,128)(2,1)}, u32[]{:S(2)}, u32[]{:S(2)}) %collective-permute-start.24) | collective-permute-done | bytes 1048608 | tf_op jit(solution)/shard_map/ppermute | solution.py:33
  131.4 2.7 %collective-permute-done.26.rest_3_ = bf16[4,512,256]{2,1,0:T(8,128)(2,1)} collective-permute-done((bf16[4,512,256]{2,1,0:T(8,128)(2,1)}, bf16[4,512,256]{2,1,0:T(8,128)(2,1)}, u32[]{:S(2)}, u32[]{:S(2)}) %collective-permute-start.26) | collective-permute-done | bytes 1048608 | tf_op jit(solution)/shard_map/ppermute | solution.py:37
  134.1 1.0 collective-permute-start.29
  135.1 2.2 %collective-permute-start.30 = (bf16[4,512,256]{2,1,0:T(8,128)(2,1)}, bf16[4,512,256]{2,1,0:T(8,128)(2,1)S(1)}, u32[]{:S(2)}, u32[]{:S(2)}) collective-permute-start(bf16[4,512,256]{2,1,0:T(8,128)(2,1)} %collective-permute-done.22.rest_5_), channel_id=1, source_target_pairs={{0,6},{1,7},{2,0},{3,1},{4,2},{5,3},{6,4},{7,5},{8,14},{9,15},{10,... | collective-permute-start | bytes 3145736 | tf_op jit(solution)/shard_map/ppermute | solution.py:37
  137.3 3.2 %collective-permute-start.32 = (bf16[4,512,256]{2,1,0:T(8,128)(2,1)}, bf16[4,512,256]{2,1,0:T(8,128)(2,1)}, u32[]{:S(2)}, u32[]{:S(2)}) collective-permute-start(bf16[4,512,256]{2,1,0:T(8,128)(2,1)} %collective-permute-done.20.rest_11_), channel_id=1, source_target_pairs={{0,96},{32,0},{64,32},{96,64},{1,97},{33,1},{65,33},{97,65},{2,98}... | collective-permute-start | bytes 3145736 | tf_op jit(solution)/shard_map/ppermute | solution.py:33
  140.6 0.6 concatenate.28.info
  141.2 0.6 concatenate.35.info
  141.8 17.6 %columns.2 = (bf16[256,4096]{1,0:T(8,128)(2,1)}, f32[512,4096]{1,0:T(8,128)}, f32[4,648,512]{2,1,0:T(8,128)}) custom-call(s32[16]{0:T(128)} %concatenate.35.info, bf16[640,2048]{1,0:T(8,128)(2,1)} %lhs.1.lhs_ref, f32[256,128]{1,0:T(8,128)} %get-tuple-element.71.corr_ref, bf16[256,128]{1,0:T(8,128)(2,1)} %get-tuple-element.72.panel_ref, ...), custom_call_target="tpu_custom_call" | custom-call | flops 9395240960 | bytes 28311552 | tf_op jit(solution)/shard_map/columns/pallas_call | solution.py:259
  159.4 0.2 collective-permute-done.29.rest_0_
  159.7 2.7 %collective-permute-done.31.rest_2_ = bf16[4,512,256]{2,1,0:T(8,128)(2,1)S(1)} collective-permute-done((bf16[4,512,256]{2,1,0:T(8,128)(2,1)}, bf16[4,512,256]{2,1,0:T(8,128)(2,1)S(1)}, u32[]{:S(2)}, u32[]{:S(2)}) %collective-permute-start.31) | collective-permute-done | bytes 1048608 | tf_op jit(solution)/shard_map/ppermute | solution.py:33
  162.4 1.0 copy-done.6
  163.3 14.0 %columns.3 = (bf16[256,4096]{1,0:T(8,128)(2,1)}, f32[512,4096]{1,0:T(8,128)}) custom-call(s32[12]{0:T(128)} %concatenate.28.info, bf16[640,2048]{1,0:T(8,128)(2,1)} %lhs.1.lhs_ref, f32[256,128]{1,0:T(8,128)} %get-tuple-element.71.corr_ref, bf16[256,128]{1,0:T(8,128)(2,1)} %get-tuple-element.72.panel_ref, ...), custom_call_target="tpu_custom_call", output_to_operand_aliasing={{0}: (10, {}), {1}: (11, {})} | custom-call | flops 6710886400 | bytes 20971520 | tf_op jit(solution)/shard_map/columns/pallas_call | solution.py:259
  (51 shorter events, 0.3 us)
Async XLA Ops:
  0.6 16.1 %copy-start.1 = (bf16[512,512]{1,0:T(8,128)(2,1)S(1)}, bf16[512,512]{1,0:T(8,128)(2,1)}, u32[]{:S(2)}) copy-start(bf16[512,512]{1,0:T(8,128)(2,1)} %param.5) | copy-start | bytes 1572868
  0.6 14.0 %collective-permute-start.3 = (bf16[512,512]{1,0:T(8,128)(2,1)}, bf16[512,512]{1,0:T(8,128)(2,1)S(1)}, u32[]{:S(2)}, u32[]{:S(2)}) collective-permute-start(bf16[512,512]{1,0:T(8,128)(2,1)} %param.5), channel_id=1, source_target_pairs={{0,1},{1,0},{2,3},{3,2},{4,5},{5,4},{6,7},{7,6},{8,9},{9,8},{10,11... | collective-permute-start | bytes 1572872 | tf_op jit(solution)/shard_map/ppermute | solution.py:41
  3.3 2.0 %collective-permute-start = (bf16[512,128]{1,0:T(8,128)(2,1)S(1)}, bf16[512,128]{1,0:T(8,128)(2,1)S(1)}, u32[]{:S(2)}, u32[]{:S(2)}) collective-permute-start(bf16[512,128]{1,0:T(8,128)(2,1)S(1)} %slice_select_fusion), channel_id=1, source_target_pairs={{0,2},{32,34},{64,66},{96,98}} | collective-permute-start | bytes 393224 | tf_op jit(solution)/shard_map/ppermute | solution.py:302
  4.0 1.4 collective-permute-start.1
  4.7 0.7 collective-permute-start.2
  14.6 2.0 %collective-permute-start.4 = (bf16[512,128]{1,0:T(8,128)(2,1)S(1)}, bf16[512,128]{1,0:T(8,128)(2,1)S(1)}, u32[]{:S(2)}, u32[]{:S(2)}) collective-permute-start(bf16[512,128]{1,0:T(8,128)(2,1)S(1)} %add_add_fusion), channel_id=1, source_target_pairs={{0,32},{2,34},{4,36},{6,38},{32,64},{34,66},{36,68},{38,70},{64,96... | collective-permute-start | bytes 393224 | tf_op jit(solution)/shard_map/ppermute | solution.py:310
  15.3 1.4 collective-permute-start.5
  15.9 0.7 collective-permute-start.6
  16.8 13.1 %collective-permute-start.10 = (bf16[2,512,256]{2,1,0:T(8,128)(2,1)S(1)}, bf16[2,512,256]{2,1,0:T(8,128)(2,1)S(1)}, u32[]{:S(2)}, u32[]{:S(2)}) collective-permute-start(bf16[2,512,256]{2,1,0:T(8,128)(2,1)S(1)} %pad_maximum_fusion.8), channel_id=1, source_target_pairs={{0,96},{32,0},{64,32},{96,64},{1,97},{33,1},{65,33},{97,65},{2,98}... | collective-permute-start | bytes 1572872 | tf_op jit(solution)/shard_map/ppermute | solution.py:33
  19.7 13.7 %collective-permute-start.9 = (bf16[2,512,256]{2,1,0:T(8,128)(2,1)S(1)}, bf16[2,512,256]{2,1,0:T(8,128)(2,1)S(1)}, u32[]{:S(2)}, u32[]{:S(2)}) collective-permute-start(bf16[2,512,256]{2,1,0:T(8,128)(2,1)S(1)} %pad_maximum_fusion.8), channel_id=1, source_target_pairs={{0,32},{32,64},{64,96},{96,0},{1,33},{33,65},{65,97},{97,1},{2,34}... | collective-permute-start | bytes 1572872 | tf_op jit(solution)/shard_map/ppermute | solution.py:33
  19.7 4.9 %collective-permute-start.11 = (bf16[2048,128]{1,0:T(8,128)(2,1)S(1)}, bf16[2048,128]{1,0:T(8,128)(2,1)S(1)}, u32[]{:S(2)}, u32[]{:S(2)}) collective-permute-start(bf16[2048,128]{1,0:T(8,128)(2,1)S(1)} %pad_maximum_fusion.6), channel_id=1, source_target_pairs={{0,1},{2,3},{4,5},{6,7},{32,33},{34,35},{36,37},{38,39},{64,65},{6... | collective-permute-start | bytes 1572872 | tf_op jit(solution)/shard_map/ppermute | solution.py:320
  20.4 13.9 %collective-permute-start.7 = (bf16[2,512,256]{2,1,0:T(8,128)(2,1)S(1)}, bf16[2,512,256]{2,1,0:T(8,128)(2,1)S(1)}, u32[]{:S(2)}, u32[]{:S(2)}) collective-permute-start(bf16[2,512,256]{2,1,0:T(8,128)(2,1)S(1)} %pad_maximum_fusion.7), channel_id=1, source_target_pairs={{0,2},{1,3},{2,4},{3,5},{4,6},{5,7},{6,0},{7,1},{8,10},{9,11},{10,... | collective-permute-start | bytes 1572872 | tf_op jit(solution)/shard_map/ppermute | solution.py:37
  22.1 12.2 %collective-permute-start.8 = (bf16[2,512,256]{2,1,0:T(8,128)(2,1)S(1)}, bf16[2,512,256]{2,1,0:T(8,128)(2,1)S(1)}, u32[]{:S(2)}, u32[]{:S(2)}) collective-permute-start(bf16[2,512,256]{2,1,0:T(8,128)(2,1)S(1)} %pad_maximum_fusion.7), channel_id=1, source_target_pairs={{0,6},{1,7},{2,0},{3,1},{4,2},{5,3},{6,4},{7,5},{8,14},{9,15},{10,... | collective-permute-start | bytes 1572872 | tf_op jit(solution)/shard_map/ppermute | solution.py:37
  34.3 1.3 collective-permute-start.16
  35.1 19.7 %collective-permute-start.14 = (bf16[1,512,256]{2,1,0:T(8,128)(2,1)S(1)}, bf16[1,512,256]{2,1,0:T(8,128)(2,1)S(1)}, u32[]{:S(2)}, u32[]{:S(2)}) collective-permute-start(bf16[1,512,256]{2,1,0:T(8,128)(2,1)S(1)} %slice.43), channel_id=1, source_target_pairs={{0,32},{32,64},{64,96},{96,0},{1,33},{33,65},{65,97},{97,1},{2,34}... | collective-permute-start | bytes 786440 | tf_op jit(solution)/shard_map/ppermute | solution.py:33
  35.8 38.0 %collective-permute-start.17 = (bf16[2304,128]{1,0:T(8,128)(2,1)S(1)}, bf16[2304,128]{1,0:T(8,128)(2,1)S(1)}, u32[]{:S(2)}, u32[]{:S(2)}) collective-permute-start(bf16[2304,128]{1,0:T(8,128)(2,1)S(1)} %fusion.2), channel_id=1, source_target_pairs={{0,16},{8,24},{1,17},{9,25},{2,18},{10,26},{3,19},{11,27},{4,20},{... | collective-permute-start | bytes 1769480 | tf_op jit(solution)/shard_map/ppermute | solution.py:329
  37.1 36.9 %collective-permute-start.18 = (bf16[512,512]{1,0:T(8,128)(2,1)S(1)}, bf16[512,512]{1,0:T(8,128)(2,1)S(1)}, u32[]{:S(2)}, u32[]{:S(2)}) collective-permute-start(bf16[512,512]{1,0:T(8,128)(2,1)S(1)} %copy-done.1), channel_id=1, source_target_pairs={{0,0},{8,32},{16,64},{24,96},{32,8},{40,40},{48,72},{56,104},{64,1... | collective-permute-start | bytes 1572872 | tf_op jit(solution)/shard_map/ppermute | solution.py:306
  52.9 12.0 %collective-permute-start.15 = (bf16[1,512,256]{2,1,0:T(8,128)(2,1)S(1)}, bf16[1,512,256]{2,1,0:T(8,128)(2,1)S(1)}, u32[]{:S(2)}, u32[]{:S(2)}) collective-permute-start(bf16[1,512,256]{2,1,0:T(8,128)(2,1)S(1)} %slice.44), channel_id=1, source_target_pairs={{0,96},{32,0},{64,32},{96,64},{1,97},{33,1},{65,33},{97,65},{2,98}... | collective-permute-start | bytes 786440 | tf_op jit(solution)/shard_map/ppermute | solution.py:33
  53.0 13.1 %collective-permute-start.12 = (bf16[1,512,256]{2,1,0:T(8,128)(2,1)S(1)}, bf16[1,512,256]{2,1,0:T(8,128)(2,1)S(1)}, u32[]{:S(2)}, u32[]{:S(2)}) collective-permute-start(bf16[1,512,256]{2,1,0:T(8,128)(2,1)S(1)} %slice.41), channel_id=1, source_target_pairs={{0,2},{1,3},{2,4},{3,5},{4,6},{5,7},{6,0},{7,1},{8,10},{9,11},{10,... | collective-permute-start | bytes 786440 | tf_op jit(solution)/shard_map/ppermute | solution.py:37
  54.8 54.0 %copy-start.2 = (bf16[4,512,256]{2,1,0:T(8,128)(2,1)}, bf16[4,512,256]{2,1,0:T(8,128)(2,1)S(1)}, u32[]{:S(2)}) copy-start(bf16[4,512,256]{2,1,0:T(8,128)(2,1)S(1)} %pad_maximum_fusion.2.rest_0_) | copy-start | bytes 3145732
  54.8 11.3 %collective-permute-start.13 = (bf16[1,512,256]{2,1,0:T(8,128)(2,1)S(1)}, bf16[1,512,256]{2,1,0:T(8,128)(2,1)S(1)}, u32[]{:S(2)}, u32[]{:S(2)}) collective-permute-start(bf16[1,512,256]{2,1,0:T(8,128)(2,1)S(1)} %slice.42), channel_id=1, source_target_pairs={{0,6},{1,7},{2,0},{3,1},{4,2},{5,3},{6,4},{7,5},{8,14},{9,15},{10,... | collective-permute-start | bytes 786440 | tf_op jit(solution)/shard_map/ppermute | solution.py:37
  56.7 47.6 %copy-start.3 = (bf16[4,512,256]{2,1,0:T(8,128)(2,1)}, bf16[4,512,256]{2,1,0:T(8,128)(2,1)S(1)}, u32[]{:S(2)}) copy-start(bf16[4,512,256]{2,1,0:T(8,128)(2,1)S(1)} %pad_maximum_fusion.rest_6_) | copy-start | bytes 3145732
  74.0 29.2 %copy-start.7 = (bf16[512,512]{1,0:T(8,128)(2,1)}, bf16[512,512]{1,0:T(8,128)(2,1)S(1)}, u32[]{:S(2)}) copy-start(bf16[512,512]{1,0:T(8,128)(2,1)S(1)} %collective-permute-done.18.own_ref) | copy-start | bytes 1572868
  74.0 26.2 %collective-permute-start.19 = (bf16[4,512,256]{2,1,0:T(8,128)(2,1)S(1)}, bf16[4,512,256]{2,1,0:T(8,128)(2,1)}, u32[]{:S(2)}, u32[]{:S(2)}) collective-permute-start(bf16[4,512,256]{2,1,0:T(8,128)(2,1)S(1)} %pad_maximum_fusion.rest_6_), channel_id=1, source_target_pairs={{0,32},{32,64},{64,96},{96,0},{1,33},{33,65},{65,97},{97,1},{2,34}... | collective-permute-start | bytes 3145736 | tf_op jit(solution)/shard_map/ppermute | solution.py:33
  74.4 25.9 %collective-permute-start.20 = (bf16[4,512,256]{2,1,0:T(8,128)(2,1)}, bf16[4,512,256]{2,1,0:T(8,128)(2,1)}, u32[]{:S(2)}, u32[]{:S(2)}) collective-permute-start(bf16[4,512,256]{2,1,0:T(8,128)(2,1)} %pad_maximum_fusion.1.rest_7_), channel_id=1, source_target_pairs={{0,96},{32,0},{64,32},{96,64},{1,97},{33,1},{65,33},{97,65},{2,98}... | collective-permute-start | bytes 3145736 | tf_op jit(solution)/shard_map/ppermute | solution.py:33
  77.3 25.6 %collective-permute-start.21 = (bf16[4,512,256]{2,1,0:T(8,128)(2,1)S(1)}, bf16[4,512,256]{2,1,0:T(8,128)(2,1)}, u32[]{:S(2)}, u32[]{:S(2)}) collective-permute-start(bf16[4,512,256]{2,1,0:T(8,128)(2,1)S(1)} %pad_maximum_fusion.2.rest_0_), channel_id=1, source_target_pairs={{0,2},{1,3},{2,4},{3,5},{4,6},{5,7},{6,0},{7,1},{8,10},{9,11},{10,... | collective-permute-start | bytes 3145736 | tf_op jit(solution)/shard_map/ppermute | solution.py:37
  78.9 24.3 %collective-permute-start.22 = (bf16[4,512,256]{2,1,0:T(8,128)(2,1)}, bf16[4,512,256]{2,1,0:T(8,128)(2,1)}, u32[]{:S(2)}, u32[]{:S(2)}) collective-permute-start(bf16[4,512,256]{2,1,0:T(8,128)(2,1)} %pad_maximum_fusion.3.rest_1_), channel_id=1, source_target_pairs={{0,6},{1,7},{2,0},{3,1},{4,2},{5,3},{6,4},{7,5},{8,14},{9,15},{10,... | collective-permute-start | bytes 3145736 | tf_op jit(solution)/shard_map/ppermute | solution.py:37
  82.0 14.1 %collective-permute-start.23 = (bf16[512,512]{1,0:T(8,128)(2,1)S(1)}, bf16[512,512]{1,0:T(8,128)(2,1)S(1)}, u32[]{:S(2)}, u32[]{:S(2)}) collective-permute-start(bf16[512,512]{1,0:T(8,128)(2,1)S(1)} %collective-permute-done.18.own_ref), channel_id=1, source_target_pairs={{0,16},{8,24},{16,0},{24,8},{1,17},{9,25},{17,1},{25,9},{2,18},{10... | collective-permute-start | bytes 1572872 | tf_op jit(solution)/shard_map/ppermute | solution.py:337
  96.1 14.7 %copy-start = (s32[4]{0:T(128)S(1)}, s32[4]{0:T(128)}, u32[]{:S(2)}) copy-start(s32[4]{0:T(128)} %constant.174.clone) | copy-start | bytes 52
  96.1 11.4 %copy-start.8 = (bf16[512,512]{1,0:T(8,128)(2,1)}, bf16[512,512]{1,0:T(8,128)(2,1)S(1)}, u32[]{:S(2)}) copy-start(bf16[512,512]{1,0:T(8,128)(2,1)S(1)} %collective-permute-done.23.own_z_ref) | copy-start | bytes 1572868
  104.3 7.7 %collective-permute-start.28 = (bf16[2,512,512]{2,1,0:T(8,128)(2,1)}, bf16[2,512,512]{2,1,0:T(8,128)(2,1)}, u32[]{:S(2)}, u32[]{:S(2)}) collective-permute-start(bf16[2,512,512]{2,1,0:T(8,128)(2,1)} %pad_maximum_fusion.4), channel_id=1, source_target_pairs={{0,8},{8,0},{16,24},{24,16},{1,9},{9,1},{17,25},{25,17},{2,10},{10... | collective-permute-start | bytes 3145736 | tf_op jit(solution)/shard_map/ppermute | solution.py:342
  104.3 27.1 %collective-permute-start.24 = (bf16[4,512,256]{2,1,0:T(8,128)(2,1)}, bf16[4,512,256]{2,1,0:T(8,128)(2,1)}, u32[]{:S(2)}, u32[]{:S(2)}) collective-permute-start(bf16[4,512,256]{2,1,0:T(8,128)(2,1)} %pad_maximum_fusion.1.rest_7_), channel_id=1, source_target_pairs={{0,32},{32,64},{64,96},{96,0},{1,33},{33,65},{65,97},{97,1},{2,34}... | collective-permute-start | bytes 3145736 | tf_op jit(solution)/shard_map/ppermute | solution.py:33
  104.3 27.1 %collective-permute-start.25 = (bf16[4,512,256]{2,1,0:T(8,128)(2,1)S(1)}, bf16[4,512,256]{2,1,0:T(8,128)(2,1)}, u32[]{:S(2)}, u32[]{:S(2)}) collective-permute-start(bf16[4,512,256]{2,1,0:T(8,128)(2,1)S(1)} %pad_maximum_fusion.rest_6_), channel_id=1, source_target_pairs={{0,96},{32,0},{64,32},{96,64},{1,97},{33,1},{65,33},{97,65},{2,98}... | collective-permute-start | bytes 3145736 | tf_op jit(solution)/shard_map/ppermute | solution.py:33
  107.5 26.5 %collective-permute-start.26 = (bf16[4,512,256]{2,1,0:T(8,128)(2,1)}, bf16[4,512,256]{2,1,0:T(8,128)(2,1)}, u32[]{:S(2)}, u32[]{:S(2)}) collective-permute-start(bf16[4,512,256]{2,1,0:T(8,128)(2,1)} %pad_maximum_fusion.3.rest_1_), channel_id=1, source_target_pairs={{0,2},{1,3},{2,4},{3,5},{4,6},{5,7},{6,0},{7,1},{8,10},{9,11},{10,... | collective-permute-start | bytes 3145736 | tf_op jit(solution)/shard_map/ppermute | solution.py:37
  108.8 25.2 %collective-permute-start.27 = (bf16[4,512,256]{2,1,0:T(8,128)(2,1)S(1)}, bf16[4,512,256]{2,1,0:T(8,128)(2,1)}, u32[]{:S(2)}, u32[]{:S(2)}) collective-permute-start(bf16[4,512,256]{2,1,0:T(8,128)(2,1)S(1)} %pad_maximum_fusion.2.rest_0_), channel_id=1, source_target_pairs={{0,6},{1,7},{2,0},{3,1},{4,2},{5,3},{6,4},{7,5},{8,14},{9,15},{10,... | collective-permute-start | bytes 3145736 | tf_op jit(solution)/shard_map/ppermute | solution.py:37
  134.1 25.6 %collective-permute-start.29 = (bf16[4,512,256]{2,1,0:T(8,128)(2,1)}, bf16[4,512,256]{2,1,0:T(8,128)(2,1)S(1)}, u32[]{:S(2)}, u32[]{:S(2)}) collective-permute-start(bf16[4,512,256]{2,1,0:T(8,128)(2,1)} %collective-permute-done.21.rest_2_), channel_id=1, source_target_pairs={{0,2},{1,3},{2,4},{3,5},{4,6},{5,7},{6,0},{7,1},{8,10},{9,11},{10,... | collective-permute-start | bytes 3145736 | tf_op jit(solution)/shard_map/ppermute | solution.py:37
  135.1 24.6 %collective-permute-start.30 = (bf16[4,512,256]{2,1,0:T(8,128)(2,1)}, bf16[4,512,256]{2,1,0:T(8,128)(2,1)S(1)}, u32[]{:S(2)}, u32[]{:S(2)}) collective-permute-start(bf16[4,512,256]{2,1,0:T(8,128)(2,1)} %collective-permute-done.22.rest_5_), channel_id=1, source_target_pairs={{0,6},{1,7},{2,0},{3,1},{4,2},{5,3},{6,4},{7,5},{8,14},{9,15},{10,... | collective-permute-start | bytes 3145736 | tf_op jit(solution)/shard_map/ppermute | solution.py:37
  137.3 25.0 %collective-permute-start.31 = (bf16[4,512,256]{2,1,0:T(8,128)(2,1)}, bf16[4,512,256]{2,1,0:T(8,128)(2,1)S(1)}, u32[]{:S(2)}, u32[]{:S(2)}) collective-permute-start(bf16[4,512,256]{2,1,0:T(8,128)(2,1)} %collective-permute-done.19.rest_8_), channel_id=1, source_target_pairs={{0,32},{32,64},{64,96},{96,0},{1,33},{33,65},{65,97},{97,1},{2,34}... | collective-permute-start | bytes 3145736 | tf_op jit(solution)/shard_map/ppermute | solution.py:33
  137.3 25.0 %collective-permute-start.32 = (bf16[4,512,256]{2,1,0:T(8,128)(2,1)}, bf16[4,512,256]{2,1,0:T(8,128)(2,1)}, u32[]{:S(2)}, u32[]{:S(2)}) collective-permute-start(bf16[4,512,256]{2,1,0:T(8,128)(2,1)} %collective-permute-done.20.rest_11_), channel_id=1, source_target_pairs={{0,96},{32,0},{64,32},{96,64},{1,97},{33,1},{65,33},{97,65},{2,98}... | collective-permute-start | bytes 3145736 | tf_op jit(solution)/shard_map/ppermute | solution.py:33
  159.7 2.7 %copy-start.4 = (bf16[4,512,256]{2,1,0:T(8,128)(2,1)}, bf16[4,512,256]{2,1,0:T(8,128)(2,1)S(1)}, u32[]{:S(2)}) copy-start(bf16[4,512,256]{2,1,0:T(8,128)(2,1)S(1)} %collective-permute-done.29.rest_0_) | copy-start | bytes 3145732
  159.7 2.7 %copy-start.5 = (bf16[4,512,256]{2,1,0:T(8,128)(2,1)}, bf16[4,512,256]{2,1,0:T(8,128)(2,1)S(1)}, u32[]{:S(2)}) copy-start(bf16[4,512,256]{2,1,0:T(8,128)(2,1)S(1)} %collective-permute-done.30.rest_1_) | copy-start | bytes 3145732
  162.3 1.0 copy-start.6

commit v3 on v2

--- a/solution.py
+++ b/solution.py
@@ -208,12 +208,17 @@
                 preferred_element_type=jnp.float32,
             )
             out_buf[slot] = (w_buf[slot].astype(jnp.float32) + change).astype(out_buf.dtype)
-            row = lax.broadcasted_iota(jnp.int32, (rows, width), 0)
-            col = lax.broadcasted_iota(jnp.int32, (rows, width), 1)
+            hess_buf[slot] = acc[:rows]
             for h in range(2):
                 lanes = slice(h * width, (h + 1) * width)
                 col0 = info[0] + column(p, h)
-                hess_buf[slot, :, lanes] = acc[:rows, lanes] + jnp.where(row - col == col0 - info[1], DAMPING, 0.0)
+                ahead = col0 - info[1]
+
+                @pl.when((ahead > -width) & (ahead < rows))
+                def _():
+                    row = lax.broadcasted_iota(jnp.int32, (rows, width), 0)
+                    col = lax.broadcasted_iota(jnp.int32, (rows, width), 1)
+                    hess_buf[slot, :, lanes] = hess_buf[slot, :, lanes] + jnp.where(row - col == ahead, DAMPING, 0.0)
 
                 @pl.when(col0 == 0)
                 def _():
@@ -302,8 +307,6 @@
         jnp.add, [lax.ppermute(ap, ("row", "col"), [(0, k * NZ)]) for k in range(1, NY)], ap
     )
     ap, other, activation = lax.optimization_barrier((ap, other, activation))
-    swap = [(i * NROW + j, j * NROW + i) for i in range(NX) for j in range(NROW)]
-    own = lax.ppermute(activation, ("dp", "row"), swap)
     ap = jnp.concatenate(
         [ap]
         + [
@@ -329,23 +332,25 @@
     both = both + lax.ppermute(both, "row", [(0, 2), (1, 3)])
     first = (jnp.concatenate([first, first_left]), jnp.concatenate([first_right, *first_far]))
     second = (jnp.concatenate([second, second_left]), jnp.concatenate([second_right, *second_far]))
-    first, second, both, own = lax.optimization_barrier((first, second, both, own))
+    first, second, activation = lax.optimization_barrier((first, second, activation))
 
     first_out, second_out = ring_out(*first, send_x), ring_out(*second, send_y)
     ap, wp = both[: NX * tok].reshape(NX, tok, PANEL), both[NX * tok :]
     corr, panel = panel_step(ap, wp, prune_mask, channel_rank)
+    swap = [(i * NROW + j, j * NROW + i) for i in range(NX) for j in range(NROW)]
+    own = lax.ppermute(activation, ("dp", "row"), swap)
+    first, second, first_out, second_out, corr, own = lax.optimization_barrier(
+        (first, second, first_out, second_out, corr, own)
+    )
+    first_in, second_in = ring_in(*first, send_x), ring_in(*second, send_y)
     own_z = lax.ppermute(own, "row", [(i, i ^ 2) for i in range(NROW)])
-    first, second, first_out, second_out, corr, own_z = lax.optimization_barrier(
-        (first, second, first_out, second_out, corr, own_z)
-    )
-    first_in, second_in = ring_in(*first, send_x), ring_in(*second, send_y)
+    first_out, second_out, first_in, second_in, own, own_z = lax.optimization_barrier(
+        (first_out, second_out, first_in, second_in, own, own_z)
+    )
+    first_far, second_far = ring_out(*first_out, send_x), ring_out(*second_out, send_y)
     core = lax.ppermute(jnp.stack([own, own_z]), "row", [(i, i ^ 1) for i in range(NROW)])
     order = jnp.array([0, 2, 3, 1], jnp.int32)
     lhs = lhs_step(order[((r ^ jnp.arange(NROW)) - d) % NX], own, own_z, core, ap)
-    first_out, second_out, first_in, second_in, lhs = lax.optimization_barrier(
-        (first_out, second_out, first_in, second_in, lhs)
-    )
-    first_far, second_far = ring_out(*first_out, send_x), ring_out(*second_out, send_y)
 
     base = jnp.stack([r * chans, (d * ncol + c) * block])
     step = functools.partial(columns_step, base, lhs, corr, panel, weight)

time: 178 us -> 163 us (0.916)
  waiting for transfers between devices: 60.9 us -> 49.7 us
  other arithmetic: 6.91 us -> 3.94 us
  starting transfers between devices: 53.8 us -> 51.4 us
  local copies, waits for them, and re-layouts: 5.03 us -> 6.83 us
    ppermute x10, waiting for transfers between devices: 39.2 us -> 16.1 us  [send_x(): return lax.ppermute(a, 'dp', x_perm(k))]
    ppermute x1, starting transfers between devices: 15.8 us -> 2.5 us  [body(): own = lax.ppermute(activation, ('dp', 'row'), swap)]
    ppermute x1, waiting for transfers between devices: 0.01 us -> 10.9 us  [body(): own_z = lax.ppermute(own, 'row', [(i, i ^ 2) for i in range(NROW)])]
    ppermute x1, starting transfers between devices: 0.01 us -> 3.96 us  [body(): own_z = lax.ppermute(own, 'row', [(i, i ^ 2) for i in range(NROW)])]
    ppermute x10, starting transfers between devices: 13.2 us -> 17.1 us  [send_x(): return lax.ppermute(a, 'dp', x_perm(k))]
    ppermute x1, waiting for transfers between devices: 6.63 us -> 10.5 us  [body(): both = both + lax.ppermute(both, 'row', [(0, 2), (1, 3)])]
    ppermute x10, waiting for transfers between devices: 6.8 us -> 3.76 us  [send_y(): return lax.ppermute(a, 'col', y_perm(k))]
    ppermute x1, starting transfers between devices: 0.01 us -> 3.01 us  [body(): lax.ppermute(jnp.stack([own, own_z]), 'row', [(i, i ^ 1) for i in range(N...]
  transfers between devices with their start and end apart: 33 -> 33, of which waited for: 13 -> 13; matrix products, arithmetic and copies ran while one was open for 5% -> 5% of each run, Pallas kernels for 20% -> 22%
where the time goes in v3:
time: 163 us; the launch traced here: 162 us
  starting transfers between devices  51.4 us (32%)
  waiting for transfers between devices  49.7 us (30%)
  Pallas kernels  49.3 us (30%)
  local copies, waits for them, and re-layouts  6.83 us (4%)
  other arithmetic  3.94 us (2%)
    pallas_call x2, Pallas kernels, columns_step(): pl.pallas_call(body, grid_spec=pltpu.PrefetchScalarGridSpec(num_scalar_pr...  31.3 us
    ppermute x10, starting transfers between devices, send_x(): return lax.ppermute(a, 'dp', x_perm(k))  17.1 us
    ppermute x10, starting transfers between devices, send_y(): return lax.ppermute(a, 'col', y_perm(k))  16.5 us
    ppermute x10, waiting for transfers between devices, send_x(): return lax.ppermute(a, 'dp', x_perm(k))  16.1 us
    pallas_call x1, Pallas kernels, panel_step(): pl.pallas_call(panel_kernel, out_shape=(jax.ShapeDtypeStruct((rows, PANEL...  14.1 us
    ppermute x1, waiting for transfers between devices, body(): own_z = lax.ppermute(own, 'row', [(i, i ^ 2) for i in range(NROW)])  10.9 us
    ppermute x1, waiting for transfers between devices, body(): both = both + lax.ppermute(both, 'row', [(0, 2), (1, 3)])  10.5 us
    ppermute x1, waiting for transfers between devices, send_z(): return lax.ppermute(a, 'col', Z_PERM)  8.29 us
  transfers between devices with their start and end apart: 33, of which 13 were waited for; matrix products, arithmetic and copies ran while one was open for 5% of the time, Pallas kernels for 22%

profile of v3, /device:TPU:64, one launch (start us, length us, event | category | flops | bytes accessed | tf_op | source)
XLA Modules:
  0.0 162.5 jit_solution(10876068243563321925)
XLA Ops:
  0.6 1.7 %collective-permute-start.3 = (bf16[512,512]{1,0:T(8,128)(2,1)}, bf16[512,512]{1,0:T(8,128)(2,1)S(1)}, u32[]{:S(2)}, u32[]{:S(2)}) collective-permute-start(bf16[512,512]{1,0:T(8,128)(2,1)} %param.5), channel_id=1, source_target_pairs={{0,1},{1,0},{2,3},{3,2},{4,5},{5,4},{6,7},{7,6},{8,9},{9,8},{10,11... | collective-permute-start | bytes 1572872 | tf_op jit(solution)/shard_map/ppermute | solution.py:41
  2.3 0.9 slice_select_fusion
  3.3 0.7 collective-permute-start
  4.0 0.7 collective-permute-start.1
  4.7 0.7 collective-permute-start.2
  5.4 0.9 add_add_fusion
  6.3 8.3 %collective-permute-done.3 = bf16[512,512]{1,0:T(8,128)(2,1)S(1)} collective-permute-done((bf16[512,512]{1,0:T(8,128)(2,1)}, bf16[512,512]{1,0:T(8,128)(2,1)S(1)}, u32[]{:S(2)}, u32[]{:S(2)}) %collective-permute-start.3) | collective-permute-done | bytes 524320 | tf_op jit(solution)/shard_map/ppermute | solution.py:41
  14.6 0.7 collective-permute-start.4
  15.3 0.7 collective-permute-start.5
  15.9 0.7 collective-permute-start.6
  16.8 2.8 %collective-permute-start.10 = (bf16[2,512,256]{2,1,0:T(8,128)(2,1)S(1)}, bf16[2,512,256]{2,1,0:T(8,128)(2,1)S(1)}, u32[]{:S(2)}, u32[]{:S(2)}) collective-permute-start(bf16[2,512,256]{2,1,0:T(8,128)(2,1)S(1)} %pad_maximum_fusion.8), channel_id=1, source_target_pairs={{0,96},{32,0},{64,32},{96,64},{1,97},{33,1},{65,33},{97,65},{2,98}... | collective-permute-start | bytes 1572872 | tf_op jit(solution)/shard_map/ppermute | solution.py:33
  19.7 0.7 collective-permute-start.11
  20.4 1.6 %collective-permute-start.7 = (bf16[2,512,256]{2,1,0:T(8,128)(2,1)S(1)}, bf16[2,512,256]{2,1,0:T(8,128)(2,1)S(1)}, u32[]{:S(2)}, u32[]{:S(2)}) collective-permute-start(bf16[2,512,256]{2,1,0:T(8,128)(2,1)S(1)} %pad_maximum_fusion.7), channel_id=1, source_target_pairs={{0,2},{1,3},{2,4},{3,5},{4,6},{5,7},{6,0},{7,1},{8,10},{9,11},{10,... | collective-permute-start | bytes 1572872 | tf_op jit(solution)/shard_map/ppermute | solution.py:37
  22.1 1.7 %collective-permute-start.8 = (bf16[2,512,256]{2,1,0:T(8,128)(2,1)S(1)}, bf16[2,512,256]{2,1,0:T(8,128)(2,1)S(1)}, u32[]{:S(2)}, u32[]{:S(2)}) collective-permute-start(bf16[2,512,256]{2,1,0:T(8,128)(2,1)S(1)} %pad_maximum_fusion.7), channel_id=1, source_target_pairs={{0,6},{1,7},{2,0},{3,1},{4,2},{5,3},{6,4},{7,5},{8,14},{9,15},{10,... | collective-permute-start | bytes 1572872 | tf_op jit(solution)/shard_map/ppermute | solution.py:37
  23.7 0.8 slice_select_fusion.1
  24.6 0.1 add.238
  24.7 5.2 %collective-permute-done.10 = bf16[2,512,256]{2,1,0:T(8,128)(2,1)S(1)} collective-permute-done((bf16[2,512,256]{2,1,0:T(8,128)(2,1)S(1)}, bf16[2,512,256]{2,1,0:T(8,128)(2,1)S(1)}, u32[]{:S(2)}, u32[]{:S(2)}) %collective-permute-start.10) | collective-permute-done | bytes 524320 | tf_op jit(solution)/shard_map/ppermute | solution.py:33
  30.0 3.4 %collective-permute-done.9 = bf16[2,512,256]{2,1,0:T(8,128)(2,1)S(1)} collective-permute-done((bf16[2,512,256]{2,1,0:T(8,128)(2,1)S(1)}, bf16[2,512,256]{2,1,0:T(8,128)(2,1)S(1)}, u32[]{:S(2)}, u32[]{:S(2)}) %collective-permute-start.9) | collective-permute-done | bytes 524320 | tf_op jit(solution)/shard_map/ppermute | solution.py:33
  33.4 0.9 collective-permute-done.7
  34.3 0.7 collective-permute-start.20
  35.1 0.5 collective-permute-start.14
  35.6 2.8 %collective-permute-start.15 = (bf16[1,512,256]{2,1,0:T(8,128)(2,1)S(1)}, bf16[1,512,256]{2,1,0:T(8,128)(2,1)S(1)}, u32[]{:S(2)}, u32[]{:S(2)}) collective-permute-start(bf16[1,512,256]{2,1,0:T(8,128)(2,1)S(1)} %slice.44), channel_id=1, source_target_pairs={{0,96},{32,0},{64,32},{96,64},{1,97},{33,1},{65,33},{97,65},{2,98}... | collective-permute-start | bytes 786440 | tf_op jit(solution)/shard_map/ppermute | solution.py:33
  38.5 1.6 %collective-permute-start.12 = (bf16[1,512,256]{2,1,0:T(8,128)(2,1)S(1)}, bf16[1,512,256]{2,1,0:T(8,128)(2,1)S(1)}, u32[]{:S(2)}, u32[]{:S(2)}) collective-permute-start(bf16[1,512,256]{2,1,0:T(8,128)(2,1)S(1)} %slice.41), channel_id=1, source_target_pairs={{0,2},{1,3},{2,4},{3,5},{4,6},{5,7},{6,0},{7,1},{8,10},{9,11},{10,... | collective-permute-start | bytes 786440 | tf_op jit(solution)/shard_map/ppermute | solution.py:37
  40.2 1.7 %collective-permute-start.13 = (bf16[1,512,256]{2,1,0:T(8,128)(2,1)S(1)}, bf16[1,512,256]{2,1,0:T(8,128)(2,1)S(1)}, u32[]{:S(2)}, u32[]{:S(2)}) collective-permute-start(bf16[1,512,256]{2,1,0:T(8,128)(2,1)S(1)} %slice.42), channel_id=1, source_target_pairs={{0,6},{1,7},{2,0},{3,1},{4,2},{5,3},{6,4},{7,5},{8,14},{9,15},{10,... | collective-permute-start | bytes 786440 | tf_op jit(solution)/shard_map/ppermute | solution.py:37
  42.0 0.2 fusion.2
  42.2 1.3 collective-permute-start.21
  43.6 0.1 pad_maximum_fusion.3.rest_1_
  43.8 2.4 %collective-permute-done.12 = bf16[1,512,256]{2,1,0:T(8,128)(2,1)S(1)} collective-permute-done((bf16[1,512,256]{2,1,0:T(8,128)(2,1)S(1)}, bf16[1,512,256]{2,1,0:T(8,128)(2,1)S(1)}, u32[]{:S(2)}, u32[]{:S(2)}) %collective-permute-start.12) | collective-permute-done | bytes 262176 | tf_op jit(solution)/shard_map/ppermute | solution.py:37
  46.1 0.5 collective-permute-done.13
  46.6 0.1 pad_maximum_fusion.1.rest_7_
  46.8 3.2 %collective-permute-start.17 = (bf16[4,512,256]{2,1,0:T(8,128)(2,1)S(1)}, bf16[4,512,256]{2,1,0:T(8,128)(2,1)}, u32[]{:S(2)}, u32[]{:S(2)}) collective-permute-start(bf16[4,512,256]{2,1,0:T(8,128)(2,1)S(1)} %pad_maximum_fusion.1.rest_7_), channel_id=1, source_target_pairs={{0,96},{32,0},{64,32},{96,64},{1,97},{33,1},{65,33},{97,65},{2,98}... | collective-permute-start | bytes 3145736 | tf_op jit(solution)/shard_map/ppermute | solution.py:33
  50.0 1.3 collective-permute-start.18
  51.3 2.0 %collective-permute-start.19 = (bf16[4,512,256]{2,1,0:T(8,128)(2,1)S(1)}, bf16[4,512,256]{2,1,0:T(8,128)(2,1)}, u32[]{:S(2)}, u32[]{:S(2)}) collective-permute-start(bf16[4,512,256]{2,1,0:T(8,128)(2,1)S(1)} %pad_maximum_fusion.3.rest_1_), channel_id=1, source_target_pairs={{0,6},{1,7},{2,0},{3,1},{4,2},{5,3},{6,4},{7,5},{8,14},{9,15},{10,... | collective-permute-start | bytes 3145736 | tf_op jit(solution)/shard_map/ppermute | solution.py:37
  53.3 10.5 %collective-permute-done.21 = bf16[2304,128]{1,0:T(8,128)(2,1)S(1)} collective-permute-done((bf16[2304,128]{1,0:T(8,128)(2,1)S(1)}, bf16[2304,128]{1,0:T(8,128)(2,1)S(1)}, u32[]{:S(2)}, u32[]{:S(2)}) %collective-permute-start.21) | collective-permute-done | bytes 589856 | tf_op jit(solution)/shard_map/ppermute | solution.py:332
  63.8 2.5 %collective-permute-start.22 = (bf16[512,512]{1,0:T(8,128)(2,1)S(1)}, bf16[512,512]{1,0:T(8,128)(2,1)S(1)}, u32[]{:S(2)}, u32[]{:S(2)}) collective-permute-start(bf16[512,512]{1,0:T(8,128)(2,1)S(1)} %copy-done.1), channel_id=1, source_target_pairs={{0,0},{8,32},{16,64},{24,96},{32,8},{40,40},{48,72},{56,104},{64,1... | collective-permute-start | bytes 1572872 | tf_op jit(solution)/shard_map/ppermute | solution.py:341
  66.3 0.2 add.240
  66.5 0.9 slice.50
  67.3 0.6 slice.51.wp_ref
  67.9 14.1 %panel_sweep.1 = (f32[256,128]{1,0:T(8,128)}, bf16[256,128]{1,0:T(8,128)(2,1)}) custom-call(bf16[4,512,128]{2,1,0:T(8,128)(2,1)} %bitcast.32, bf16[256,128]{1,0:T(8,128)(2,1)} %slice.51.wp_ref, s32[256,128]{1,0:T(8,128)} %mask_ref.1, s32[1,128]{1,0:T(1,128)} %bitcast.36), custom_call_target="tpu_custom_call" | custom-call | flops 8589934592 | bytes 33554432 | tf_op jit(solution)/shard_map/panel_sweep/pallas_call | solution.py:102
  82.1 4.4 %collective-permute-start.23 = (bf16[4,512,256]{2,1,0:T(8,128)(2,1)S(1)}, bf16[4,512,256]{2,1,0:T(8,128)(2,1)S(1)}, u32[]{:S(2)}, u32[]{:S(2)}) collective-permute-start(bf16[4,512,256]{2,1,0:T(8,128)(2,1)S(1)} %pad_maximum_fusion.1.rest_7_), channel_id=1, source_target_pairs={{0,32},{32,64},{64,96},{96,0},{1,33},{33,65},{65,97},{97,1},{2,34}... | collective-permute-start | bytes 3145736 | tf_op jit(solution)/shard_map/ppermute | solution.py:33
  86.5 1.6 collective-permute-start.25
  88.1 1.7 %collective-permute-start.26 = (bf16[4,512,256]{2,1,0:T(8,128)(2,1)S(1)}, bf16[4,512,256]{2,1,0:T(8,128)(2,1)S(1)}, u32[]{:S(2)}, u32[]{:S(2)}) collective-permute-start(bf16[4,512,256]{2,1,0:T(8,128)(2,1)S(1)} %pad_maximum_fusion.2.rest_0_), channel_id=1, source_target_pairs={{0,6},{1,7},{2,0},{3,1},{4,2},{5,3},{6,4},{7,5},{8,14},{9,15},{10,... | collective-permute-start | bytes 3145736 | tf_op jit(solution)/shard_map/ppermute | solution.py:37
  89.8 4.0 %collective-permute-start.27 = (bf16[512,512]{1,0:T(8,128)(2,1)S(1)}, bf16[512,512]{1,0:T(8,128)(2,1)S(1)}, u32[]{:S(2)}, u32[]{:S(2)}) collective-permute-start(bf16[512,512]{1,0:T(8,128)(2,1)S(1)} %collective-permute-done.22.own_ref), channel_id=1, source_target_pairs={{0,16},{8,24},{16,0},{24,8},{1,17},{9,25},{17,1},{25,9},{2,18},{10... | collective-permute-start | bytes 1572872 | tf_op jit(solution)/shard_map/ppermute | solution.py:346
  93.8 10.9 %collective-permute-done.27.own_z_ref = bf16[512,512]{1,0:T(8,128)(2,1)S(1)} collective-permute-done((bf16[512,512]{1,0:T(8,128)(2,1)S(1)}, bf16[512,512]{1,0:T(8,128)(2,1)S(1)}, u32[]{:S(2)}, u32[]{:S(2)}) %collective-permute-start.27) | collective-permute-done | bytes 524320 | tf_op jit(solution)/shard_map/ppermute | solution.py:346
  104.7 3.0 %collective-permute-done.23.rest_9_ = bf16[4,512,256]{2,1,0:T(8,128)(2,1)S(1)} collective-permute-done((bf16[4,512,256]{2,1,0:T(8,128)(2,1)S(1)}, bf16[4,512,256]{2,1,0:T(8,128)(2,1)S(1)}, u32[]{:S(2)}, u32[]{:S(2)}) %collective-permute-start.23) | collective-permute-done | bytes 1048608 | tf_op jit(solution)/shard_map/ppermute | solution.py:33
  107.7 2.7 %collective-permute-done.24.rest_10_ = bf16[4,512,256]{2,1,0:T(8,128)(2,1)S(1)} collective-permute-done((bf16[4,512,256]{2,1,0:T(8,128)(2,1)S(1)}, bf16[4,512,256]{2,1,0:T(8,128)(2,1)S(1)}, u32[]{:S(2)}, u32[]{:S(2)}) %collective-permute-start.24) | collective-permute-done | bytes 1048608 | tf_op jit(solution)/shard_map/ppermute | solution.py:33
  110.4 0.9 copy-done.14
  111.4 0.4 copy-done.15
  111.7 0.3 copy-done.16
  112.2 3.0 %collective-permute-start.28 = (bf16[2,512,512]{2,1,0:T(8,128)(2,1)S(1)}, bf16[2,512,512]{2,1,0:T(8,128)(2,1)}, u32[]{:S(2)}, u32[]{:S(2)}) collective-permute-start(bf16[2,512,512]{2,1,0:T(8,128)(2,1)S(1)} %pad_maximum_fusion.4), channel_id=1, source_target_pairs={{0,8},{8,0},{16,24},{24,16},{1,9},{9,1},{17,25},{25,17},{2,10},{10... | collective-permute-start | bytes 3145736 | tf_op jit(solution)/shard_map/ppermute | solution.py:351
  115.2 1.1 gather_fusion
  116.3 0.7 concatenate.28.info
  117.0 0.7 concatenate.35.info
  117.7 1.2 collective-permute-start.29
  118.8 2.1 %collective-permute-start.30 = (bf16[4,512,256]{2,1,0:T(8,128)(2,1)}, bf16[4,512,256]{2,1,0:T(8,128)(2,1)S(1)}, u32[]{:S(2)}, u32[]{:S(2)}) collective-permute-start(bf16[4,512,256]{2,1,0:T(8,128)(2,1)} %collective-permute-done.19.rest_5_), channel_id=1, source_target_pairs={{0,6},{1,7},{2,0},{3,1},{4,2},{5,3},{6,4},{7,5},{8,14},{9,15},{10,... | collective-permute-start | bytes 3145736 | tf_op jit(solution)/shard_map/ppermute | solution.py:37
  120.9 2.0 %collective-permute-start.31 = (bf16[4,512,256]{2,1,0:T(8,128)(2,1)S(1)}, bf16[4,512,256]{2,1,0:T(8,128)(2,1)S(1)}, u32[]{:S(2)}, u32[]{:S(2)}) collective-permute-start(bf16[4,512,256]{2,1,0:T(8,128)(2,1)S(1)} %collective-permute-done.16.rest_8_), channel_id=1, source_target_pairs={{0,32},{32,64},{64,96},{96,0},{1,33},{33,65},{65,97},{97,1},{2,34}... | collective-permute-start | bytes 3145736 | tf_op jit(solution)/shard_map/ppermute | solution.py:33
  122.9 1.3 collective-permute-start.32
  124.2 4.0 %lhs.1.lhs_ref = bf16[640,2048]{1,0:T(8,128)(2,1)} custom-call(s32[4]{0:T(128)} %gather_fusion, bf16[512,512]{1,0:T(8,128)(2,1)} %copy-done.10, bf16[512,512]{1,0:T(8,128)(2,1)} %copy-done.11, bf16[2,512,512]{2,1,0:T(8,128)(2,1)} %collective-permute-done.28.core_ref, bf16[4,512,128]{2,1,0:T(8,128)(2,1)} %bitcast.33), custom_call_target="tpu_custom_call" | custom-call | flops 2147483648 | bytes 8388608 | tf_op jit(solution)/shard_map/lhs/pallas_call | solution.py:126
  128.1 17.5 %columns.2 = (bf16[256,4096]{1,0:T(8,128)(2,1)}, f32[512,4096]{1,0:T(8,128)}, f32[4,648,512]{2,1,0:T(8,128)}) custom-call(s32[16]{0:T(128)} %concatenate.35.info, bf16[640,2048]{1,0:T(8,128)(2,1)} %lhs.1.lhs_ref, f32[256,128]{1,0:T(8,128)} %get-tuple-element.71.corr_ref, bf16[256,128]{1,0:T(8,128)(2,1)} %get-tuple-element.72.panel_ref, ...), custom_call_target="tpu_custom_call" | custom-call | flops 9395240960 | bytes 28311552 | tf_op jit(solution)/shard_map/columns/pallas_call | solution.py:264
  145.7 1.1 collective-permute-done.31.rest_2_
  146.8 0.7 collective-permute-done.32.rest_3_
  147.4 0.3 copy-done.8
  147.8 0.7 copy-done.9
  148.5 13.8 %columns.3 = (bf16[256,4096]{1,0:T(8,128)(2,1)}, f32[512,4096]{1,0:T(8,128)}) custom-call(s32[12]{0:T(128)} %concatenate.28.info, bf16[640,2048]{1,0:T(8,128)(2,1)} %lhs.1.lhs_ref, f32[256,128]{1,0:T(8,128)} %get-tuple-element.71.corr_ref, bf16[256,128]{1,0:T(8,128)(2,1)} %get-tuple-element.72.panel_ref, ...), custom_call_target="tpu_custom_call", output_to_operand_aliasing={{0}: (10, {}), {1}: (11, {})} | custom-call | flops 6710886400 | bytes 20971520 | tf_op jit(solution)/shard_map/columns/pallas_call | solution.py:264
  (67 shorter events, 0.9 us)
Async XLA Ops:
  0.6 16.1 %copy-start.1 = (bf16[512,512]{1,0:T(8,128)(2,1)S(1)}, bf16[512,512]{1,0:T(8,128)(2,1)}, u32[]{:S(2)}) copy-start(bf16[512,512]{1,0:T(8,128)(2,1)} %param.5) | copy-start | bytes 1572868
  0.6 14.0 %collective-permute-start.3 = (bf16[512,512]{1,0:T(8,128)(2,1)}, bf16[512,512]{1,0:T(8,128)(2,1)S(1)}, u32[]{:S(2)}, u32[]{:S(2)}) collective-permute-start(bf16[512,512]{1,0:T(8,128)(2,1)} %param.5), channel_id=1, source_target_pairs={{0,1},{1,0},{2,3},{3,2},{4,5},{5,4},{6,7},{7,6},{8,9},{9,8},{10,11... | collective-permute-start | bytes 1572872 | tf_op jit(solution)/shard_map/ppermute | solution.py:41
  3.3 2.0 %collective-permute-start = (bf16[512,128]{1,0:T(8,128)(2,1)S(1)}, bf16[512,128]{1,0:T(8,128)(2,1)S(1)}, u32[]{:S(2)}, u32[]{:S(2)}) collective-permute-start(bf16[512,128]{1,0:T(8,128)(2,1)S(1)} %slice_select_fusion), channel_id=1, source_target_pairs={{0,2},{32,34},{64,66},{96,98}} | collective-permute-start | bytes 393224 | tf_op jit(solution)/shard_map/ppermute | solution.py:307
  4.0 1.4 collective-permute-start.1
  4.7 0.7 collective-permute-start.2
  14.6 2.0 %collective-permute-start.4 = (bf16[512,128]{1,0:T(8,128)(2,1)S(1)}, bf16[512,128]{1,0:T(8,128)(2,1)S(1)}, u32[]{:S(2)}, u32[]{:S(2)}) collective-permute-start(bf16[512,128]{1,0:T(8,128)(2,1)S(1)} %add_add_fusion), channel_id=1, source_target_pairs={{0,32},{2,34},{4,36},{6,38},{32,64},{34,66},{36,68},{38,70},{64,96... | collective-permute-start | bytes 393224 | tf_op jit(solution)/shard_map/ppermute | solution.py:313
  15.3 1.4 collective-permute-start.5
  15.9 0.7 collective-permute-start.6
  16.8 13.1 %collective-permute-start.10 = (bf16[2,512,256]{2,1,0:T(8,128)(2,1)S(1)}, bf16[2,512,256]{2,1,0:T(8,128)(2,1)S(1)}, u32[]{:S(2)}, u32[]{:S(2)}) collective-permute-start(bf16[2,512,256]{2,1,0:T(8,128)(2,1)S(1)} %pad_maximum_fusion.8), channel_id=1, source_target_pairs={{0,96},{32,0},{64,32},{96,64},{1,97},{33,1},{65,33},{97,65},{2,98}... | collective-permute-start | bytes 1572872 | tf_op jit(solution)/shard_map/ppermute | solution.py:33
  19.7 13.7 %collective-permute-start.9 = (bf16[2,512,256]{2,1,0:T(8,128)(2,1)S(1)}, bf16[2,512,256]{2,1,0:T(8,128)(2,1)S(1)}, u32[]{:S(2)}, u32[]{:S(2)}) collective-permute-start(bf16[2,512,256]{2,1,0:T(8,128)(2,1)S(1)} %pad_maximum_fusion.8), channel_id=1, source_target_pairs={{0,32},{32,64},{64,96},{96,0},{1,33},{33,65},{65,97},{97,1},{2,34}... | collective-permute-start | bytes 1572872 | tf_op jit(solution)/shard_map/ppermute | solution.py:33
  19.7 4.9 %collective-permute-start.11 = (bf16[2048,128]{1,0:T(8,128)(2,1)S(1)}, bf16[2048,128]{1,0:T(8,128)(2,1)S(1)}, u32[]{:S(2)}, u32[]{:S(2)}) collective-permute-start(bf16[2048,128]{1,0:T(8,128)(2,1)S(1)} %pad_maximum_fusion.6), channel_id=1, source_target_pairs={{0,1},{2,3},{4,5},{6,7},{32,33},{34,35},{36,37},{38,39},{64,65},{6... | collective-permute-start | bytes 1572872 | tf_op jit(solution)/shard_map/ppermute | solution.py:323
  20.4 13.9 %collective-permute-start.7 = (bf16[2,512,256]{2,1,0:T(8,128)(2,1)S(1)}, bf16[2,512,256]{2,1,0:T(8,128)(2,1)S(1)}, u32[]{:S(2)}, u32[]{:S(2)}) collective-permute-start(bf16[2,512,256]{2,1,0:T(8,128)(2,1)S(1)} %pad_maximum_fusion.7), channel_id=1, source_target_pairs={{0,2},{1,3},{2,4},{3,5},{4,6},{5,7},{6,0},{7,1},{8,10},{9,11},{10,... | collective-permute-start | bytes 1572872 | tf_op jit(solution)/shard_map/ppermute | solution.py:37
  22.1 12.2 %collective-permute-start.8 = (bf16[2,512,256]{2,1,0:T(8,128)(2,1)S(1)}, bf16[2,512,256]{2,1,0:T(8,128)(2,1)S(1)}, u32[]{:S(2)}, u32[]{:S(2)}) collective-permute-start(bf16[2,512,256]{2,1,0:T(8,128)(2,1)S(1)} %pad_maximum_fusion.7), channel_id=1, source_target_pairs={{0,6},{1,7},{2,0},{3,1},{4,2},{5,3},{6,4},{7,5},{8,14},{9,15},{10,... | collective-permute-start | bytes 1572872 | tf_op jit(solution)/shard_map/ppermute | solution.py:37
  34.3 7.7 %collective-permute-start.20 = (bf16[2304,128]{1,0:T(8,128)(2,1)S(1)}, bf16[2304,128]{1,0:T(8,128)(2,1)S(1)}, u32[]{:S(2)}, u32[]{:S(2)}) collective-permute-start(bf16[2304,128]{1,0:T(8,128)(2,1)S(1)} %pad_maximum_fusion.5), channel_id=1, source_target_pairs={{0,8},{1,9},{2,10},{3,11},{4,12},{5,13},{6,14},{7,15},{32,40},{33,... | collective-permute-start | bytes 1769480 | tf_op jit(solution)/shard_map/ppermute | solution.py:331
  35.1 8.5 %collective-permute-start.14 = (bf16[1,512,256]{2,1,0:T(8,128)(2,1)S(1)}, bf16[1,512,256]{2,1,0:T(8,128)(2,1)S(1)}, u32[]{:S(2)}, u32[]{:S(2)}) collective-permute-start(bf16[1,512,256]{2,1,0:T(8,128)(2,1)S(1)} %slice.43), channel_id=1, source_target_pairs={{0,32},{32,64},{64,96},{96,0},{1,33},{33,65},{65,97},{97,1},{2,34}... | collective-permute-start | bytes 786440 | tf_op jit(solution)/shard_map/ppermute | solution.py:33
  35.6 8.0 %collective-permute-start.15 = (bf16[1,512,256]{2,1,0:T(8,128)(2,1)S(1)}, bf16[1,512,256]{2,1,0:T(8,128)(2,1)S(1)}, u32[]{:S(2)}, u32[]{:S(2)}) collective-permute-start(bf16[1,512,256]{2,1,0:T(8,128)(2,1)S(1)} %slice.44), channel_id=1, source_target_pairs={{0,96},{32,0},{64,32},{96,64},{1,97},{33,1},{65,33},{97,65},{2,98}... | collective-permute-start | bytes 786440 | tf_op jit(solution)/shard_map/ppermute | solution.py:33
  38.5 7.7 %collective-permute-start.12 = (bf16[1,512,256]{2,1,0:T(8,128)(2,1)S(1)}, bf16[1,512,256]{2,1,0:T(8,128)(2,1)S(1)}, u32[]{:S(2)}, u32[]{:S(2)}) collective-permute-start(bf16[1,512,256]{2,1,0:T(8,128)(2,1)S(1)} %slice.41), channel_id=1, source_target_pairs={{0,2},{1,3},{2,4},{3,5},{4,6},{5,7},{6,0},{7,1},{8,10},{9,11},{10,... | collective-permute-start | bytes 786440 | tf_op jit(solution)/shard_map/ppermute | solution.py:37
  40.2 6.4 %collective-permute-start.13 = (bf16[1,512,256]{2,1,0:T(8,128)(2,1)S(1)}, bf16[1,512,256]{2,1,0:T(8,128)(2,1)S(1)}, u32[]{:S(2)}, u32[]{:S(2)}) collective-permute-start(bf16[1,512,256]{2,1,0:T(8,128)(2,1)S(1)} %slice.42), channel_id=1, source_target_pairs={{0,6},{1,7},{2,0},{3,1},{4,2},{5,3},{6,4},{7,5},{8,14},{9,15},{10,... | collective-permute-start | bytes 786440 | tf_op jit(solution)/shard_map/ppermute | solution.py:37
  42.0 46.1 %copy-start.2 = (bf16[4,512,256]{2,1,0:T(8,128)(2,1)}, bf16[4,512,256]{2,1,0:T(8,128)(2,1)S(1)}, u32[]{:S(2)}) copy-start(bf16[4,512,256]{2,1,0:T(8,128)(2,1)S(1)} %pad_maximum_fusion.2.rest_0_) | copy-start | bytes 3145732
  42.2 21.6 %collective-permute-start.21 = (bf16[2304,128]{1,0:T(8,128)(2,1)S(1)}, bf16[2304,128]{1,0:T(8,128)(2,1)S(1)}, u32[]{:S(2)}, u32[]{:S(2)}) collective-permute-start(bf16[2304,128]{1,0:T(8,128)(2,1)S(1)} %fusion.2), channel_id=1, source_target_pairs={{0,16},{8,24},{1,17},{9,25},{2,18},{10,26},{3,19},{11,27},{4,20},{... | collective-permute-start | bytes 1769480 | tf_op jit(solution)/shard_map/ppermute | solution.py:332
  43.6 42.9 %copy-start.3 = (bf16[4,512,256]{2,1,0:T(8,128)(2,1)}, bf16[4,512,256]{2,1,0:T(8,128)(2,1)S(1)}, u32[]{:S(2)}) copy-start(bf16[4,512,256]{2,1,0:T(8,128)(2,1)S(1)} %pad_maximum_fusion.rest_6_) | copy-start | bytes 3145732
  43.8 42.8 %copy-start.4 = (bf16[4,512,256]{2,1,0:T(8,128)(2,1)}, bf16[4,512,256]{2,1,0:T(8,128)(2,1)S(1)}, u32[]{:S(2)}) copy-start(bf16[4,512,256]{2,1,0:T(8,128)(2,1)S(1)} %pad_maximum_fusion.3.rest_1_) | copy-start | bytes 3145732
  46.7 35.4 %copy-start.5 = (bf16[4,512,256]{2,1,0:T(8,128)(2,1)}, bf16[4,512,256]{2,1,0:T(8,128)(2,1)S(1)}, u32[]{:S(2)}) copy-start(bf16[4,512,256]{2,1,0:T(8,128)(2,1)S(1)} %pad_maximum_fusion.1.rest_7_) | copy-start | bytes 3145732
  46.7 35.4 %collective-permute-start.16 = (bf16[4,512,256]{2,1,0:T(8,128)(2,1)S(1)}, bf16[4,512,256]{2,1,0:T(8,128)(2,1)S(1)}, u32[]{:S(2)}, u32[]{:S(2)}) collective-permute-start(bf16[4,512,256]{2,1,0:T(8,128)(2,1)S(1)} %pad_maximum_fusion.rest_6_), channel_id=1, source_target_pairs={{0,32},{32,64},{64,96},{96,0},{1,33},{33,65},{65,97},{97,1},{2,34}... | collective-permute-start | bytes 3145736 | tf_op jit(solution)/shard_map/ppermute | solution.py:33
  46.8 35.3 %collective-permute-start.17 = (bf16[4,512,256]{2,1,0:T(8,128)(2,1)S(1)}, bf16[4,512,256]{2,1,0:T(8,128)(2,1)}, u32[]{:S(2)}, u32[]{:S(2)}) collective-permute-start(bf16[4,512,256]{2,1,0:T(8,128)(2,1)S(1)} %pad_maximum_fusion.1.rest_7_), channel_id=1, source_target_pairs={{0,96},{32,0},{64,32},{96,64},{1,97},{33,1},{65,33},{97,65},{2,98}... | collective-permute-start | bytes 3145736 | tf_op jit(solution)/shard_map/ppermute | solution.py:33
  50.0 32.1 %collective-permute-start.18 = (bf16[4,512,256]{2,1,0:T(8,128)(2,1)S(1)}, bf16[4,512,256]{2,1,0:T(8,128)(2,1)}, u32[]{:S(2)}, u32[]{:S(2)}) collective-permute-start(bf16[4,512,256]{2,1,0:T(8,128)(2,1)S(1)} %pad_maximum_fusion.2.rest_0_), channel_id=1, source_target_pairs={{0,2},{1,3},{2,4},{3,5},{4,6},{5,7},{6,0},{7,1},{8,10},{9,11},{10,... | collective-permute-start | bytes 3145736 | tf_op jit(solution)/shard_map/ppermute | solution.py:37
  51.3 30.8 %collective-permute-start.19 = (bf16[4,512,256]{2,1,0:T(8,128)(2,1)S(1)}, bf16[4,512,256]{2,1,0:T(8,128)(2,1)}, u32[]{:S(2)}, u32[]{:S(2)}) collective-permute-start(bf16[4,512,256]{2,1,0:T(8,128)(2,1)S(1)} %pad_maximum_fusion.3.rest_1_), channel_id=1, source_target_pairs={{0,6},{1,7},{2,0},{3,1},{4,2},{5,3},{6,4},{7,5},{8,14},{9,15},{10,... | collective-permute-start | bytes 3145736 | tf_op jit(solution)/shard_map/ppermute | solution.py:37
  63.8 18.3 %collective-permute-start.22 = (bf16[512,512]{1,0:T(8,128)(2,1)S(1)}, bf16[512,512]{1,0:T(8,128)(2,1)S(1)}, u32[]{:S(2)}, u32[]{:S(2)}) collective-permute-start(bf16[512,512]{1,0:T(8,128)(2,1)S(1)} %copy-done.1), channel_id=1, source_target_pairs={{0,0},{8,32},{16,64},{24,96},{32,8},{40,40},{48,72},{56,104},{64,1... | collective-permute-start | bytes 1572872 | tf_op jit(solution)/shard_map/ppermute | solution.py:341
  82.0 33.2 %copy-start = (s32[4]{0:T(128)S(1)}, s32[4]{0:T(128)}, u32[]{:S(2)}) copy-start(s32[4]{0:T(128)} %constant.174.clone) | copy-start | bytes 52
  82.1 42.1 %copy-start.10 = (bf16[512,512]{1,0:T(8,128)(2,1)}, bf16[512,512]{1,0:T(8,128)(2,1)S(1)}, u32[]{:S(2)}) copy-start(bf16[512,512]{1,0:T(8,128)(2,1)S(1)} %collective-permute-done.22.own_ref) | copy-start | bytes 1572868
  82.1 46.0 %copy-start.12 = (bf16[4,512,256]{2,1,0:T(8,128)(2,1)}, bf16[4,512,256]{2,1,0:T(8,128)(2,1)S(1)}, u32[]{:S(2)}) copy-start(bf16[4,512,256]{2,1,0:T(8,128)(2,1)S(1)} %collective-permute-done.16.rest_8_) | copy-start | bytes 3145732
  82.1 25.6 %collective-permute-start.23 = (bf16[4,512,256]{2,1,0:T(8,128)(2,1)S(1)}, bf16[4,512,256]{2,1,0:T(8,128)(2,1)S(1)}, u32[]{:S(2)}, u32[]{:S(2)}) collective-permute-start(bf16[4,512,256]{2,1,0:T(8,128)(2,1)S(1)} %pad_maximum_fusion.1.rest_7_), channel_id=1, source_target_pairs={{0,32},{32,64},{64,96},{96,0},{1,33},{33,65},{65,97},{97,1},{2,34}... | collective-permute-start | bytes 3145736 | tf_op jit(solution)/shard_map/ppermute | solution.py:33
  86.5 23.9 %collective-permute-start.24 = (bf16[4,512,256]{2,1,0:T(8,128)(2,1)S(1)}, bf16[4,512,256]{2,1,0:T(8,128)(2,1)S(1)}, u32[]{:S(2)}, u32[]{:S(2)}) collective-permute-start(bf16[4,512,256]{2,1,0:T(8,128)(2,1)S(1)} %pad_maximum_fusion.rest_6_), channel_id=1, source_target_pairs={{0,96},{32,0},{64,32},{96,64},{1,97},{33,1},{65,33},{97,65},{2,98}... | collective-permute-start | bytes 3145736 | tf_op jit(solution)/shard_map/ppermute | solution.py:33
  86.5 23.9 %collective-permute-start.25 = (bf16[4,512,256]{2,1,0:T(8,128)(2,1)S(1)}, bf16[4,512,256]{2,1,0:T(8,128)(2,1)S(1)}, u32[]{:S(2)}, u32[]{:S(2)}) collective-permute-start(bf16[4,512,256]{2,1,0:T(8,128)(2,1)S(1)} %pad_maximum_fusion.3.rest_1_), channel_id=1, source_target_pairs={{0,2},{1,3},{2,4},{3,5},{4,6},{5,7},{6,0},{7,1},{8,10},{9,11},{10,... | collective-permute-start | bytes 3145736 | tf_op jit(solution)/shard_map/ppermute | solution.py:37
  88.1 22.3 %collective-permute-start.26 = (bf16[4,512,256]{2,1,0:T(8,128)(2,1)S(1)}, bf16[4,512,256]{2,1,0:T(8,128)(2,1)S(1)}, u32[]{:S(2)}, u32[]{:S(2)}) collective-permute-start(bf16[4,512,256]{2,1,0:T(8,128)(2,1)S(1)} %pad_maximum_fusion.2.rest_0_), channel_id=1, source_target_pairs={{0,6},{1,7},{2,0},{3,1},{4,2},{5,3},{6,4},{7,5},{8,14},{9,15},{10,... | collective-permute-start | bytes 3145736 | tf_op jit(solution)/shard_map/ppermute | solution.py:37
  89.8 14.9 %collective-permute-start.27 = (bf16[512,512]{1,0:T(8,128)(2,1)S(1)}, bf16[512,512]{1,0:T(8,128)(2,1)S(1)}, u32[]{:S(2)}, u32[]{:S(2)}) collective-permute-start(bf16[512,512]{1,0:T(8,128)(2,1)S(1)} %collective-permute-done.22.own_ref), channel_id=1, source_target_pairs={{0,16},{8,24},{16,0},{24,8},{1,17},{9,25},{17,1},{25,9},{2,18},{10... | collective-permute-start | bytes 1572872 | tf_op jit(solution)/shard_map/ppermute | solution.py:346
  104.7 7.3 %copy-start.11 = (bf16[512,512]{1,0:T(8,128)(2,1)}, bf16[512,512]{1,0:T(8,128)(2,1)S(1)}, u32[]{:S(2)}) copy-start(bf16[512,512]{1,0:T(8,128)(2,1)S(1)} %collective-permute-done.27.own_z_ref) | copy-start | bytes 1572868
  107.7 2.7 %copy-start.13 = (bf16[4,512,256]{2,1,0:T(8,128)(2,1)}, bf16[4,512,256]{2,1,0:T(8,128)(2,1)S(1)}, u32[]{:S(2)}) copy-start(bf16[4,512,256]{2,1,0:T(8,128)(2,1)S(1)} %collective-permute-done.23.rest_9_) | copy-start | bytes 3145732
  110.4 1.0 copy-start.14
  110.4 1.3 copy-start.15
  110.4 1.6 %copy-start.16 = (bf16[4,512,256]{2,1,0:T(8,128)(2,1)}, bf16[4,512,256]{2,1,0:T(8,128)(2,1)S(1)}, u32[]{:S(2)}) copy-start(bf16[4,512,256]{2,1,0:T(8,128)(2,1)S(1)} %collective-permute-done.26.rest_4_) | copy-start | bytes 3145732
  112.2 12.0 %collective-permute-start.28 = (bf16[2,512,512]{2,1,0:T(8,128)(2,1)S(1)}, bf16[2,512,512]{2,1,0:T(8,128)(2,1)}, u32[]{:S(2)}, u32[]{:S(2)}) collective-permute-start(bf16[2,512,512]{2,1,0:T(8,128)(2,1)S(1)} %pad_maximum_fusion.4), channel_id=1, source_target_pairs={{0,8},{8,0},{16,24},{24,16},{1,9},{9,1},{17,25},{25,17},{2,10},{10... | collective-permute-start | bytes 3145736 | tf_op jit(solution)/shard_map/ppermute | solution.py:351
  117.7 28.0 %collective-permute-start.29 = (bf16[4,512,256]{2,1,0:T(8,128)(2,1)}, bf16[4,512,256]{2,1,0:T(8,128)(2,1)S(1)}, u32[]{:S(2)}, u32[]{:S(2)}) collective-permute-start(bf16[4,512,256]{2,1,0:T(8,128)(2,1)} %collective-permute-done.18.rest_2_), channel_id=1, source_target_pairs={{0,2},{1,3},{2,4},{3,5},{4,6},{5,7},{6,0},{7,1},{8,10},{9,11},{10,... | collective-permute-start | bytes 3145736 | tf_op jit(solution)/shard_map/ppermute | solution.py:37
  118.8 26.8 %collective-permute-start.30 = (bf16[4,512,256]{2,1,0:T(8,128)(2,1)}, bf16[4,512,256]{2,1,0:T(8,128)(2,1)S(1)}, u32[]{:S(2)}, u32[]{:S(2)}) collective-permute-start(bf16[4,512,256]{2,1,0:T(8,128)(2,1)} %collective-permute-done.19.rest_5_), channel_id=1, source_target_pairs={{0,6},{1,7},{2,0},{3,1},{4,2},{5,3},{6,4},{7,5},{8,14},{9,15},{10,... | collective-permute-start | bytes 3145736 | tf_op jit(solution)/shard_map/ppermute | solution.py:37
  120.9 25.9 %collective-permute-start.31 = (bf16[4,512,256]{2,1,0:T(8,128)(2,1)S(1)}, bf16[4,512,256]{2,1,0:T(8,128)(2,1)S(1)}, u32[]{:S(2)}, u32[]{:S(2)}) collective-permute-start(bf16[4,512,256]{2,1,0:T(8,128)(2,1)S(1)} %collective-permute-done.16.rest_8_), channel_id=1, source_target_pairs={{0,32},{32,64},{64,96},{96,0},{1,33},{33,65},{65,97},{97,1},{2,34}... | collective-permute-start | bytes 3145736 | tf_op jit(solution)/shard_map/ppermute | solution.py:33
  122.9 24.6 %collective-permute-start.32 = (bf16[4,512,256]{2,1,0:T(8,128)(2,1)}, bf16[4,512,256]{2,1,0:T(8,128)(2,1)S(1)}, u32[]{:S(2)}, u32[]{:S(2)}) collective-permute-start(bf16[4,512,256]{2,1,0:T(8,128)(2,1)} %collective-permute-done.17.rest_11_), channel_id=1, source_target_pairs={{0,96},{32,0},{64,32},{96,64},{1,97},{33,1},{65,33},{97,65},{2,98}... | collective-permute-start | bytes 3145736 | tf_op jit(solution)/shard_map/ppermute | solution.py:33
  145.6 1.8 %copy-start.6 = (bf16[4,512,256]{2,1,0:T(8,128)(2,1)}, bf16[4,512,256]{2,1,0:T(8,128)(2,1)S(1)}, u32[]{:S(2)}) copy-start(bf16[4,512,256]{2,1,0:T(8,128)(2,1)S(1)} %collective-permute-done.29.rest_0_) | copy-start | bytes 3145732
  145.7 1.8 %copy-start.7 = (bf16[4,512,256]{2,1,0:T(8,128)(2,1)}, bf16[4,512,256]{2,1,0:T(8,128)(2,1)S(1)}, u32[]{:S(2)}) copy-start(bf16[4,512,256]{2,1,0:T(8,128)(2,1)S(1)} %collective-permute-done.30.rest_1_) | copy-start | bytes 3145732
  146.8 1.0 copy-start.8
  147.4 1.0 copy-start.9

commit v4 on v3

--- a/solution.py
+++ b/solution.py
@@ -15,7 +15,7 @@
 NY = 4
 NZ = 2
 NROW = 4
-VMEM_LIMIT = 56 * 1024 * 1024
+VMEM_LIMIT = 28 * 1024 * 1024
 
 
 def x_perm(k):
@@ -134,11 +134,11 @@
     )(slots, own, own_z, core, ap)
 
 
-def columns_kernel(pairs, tok, width, n_pieces, has_in, has_out, info, lhs_ref, corr_ref, panel_ref, w_hbm, *rest):
+def columns_kernel(pairs, tok, width, n_pieces, has_in, has_out, info, lhs_hbm, corr_ref, panel_ref, w_hbm, *rest):
     pieces = rest[:n_pieces]
     part_in = rest[n_pieces] if has_in else None
-    x_buf, w_buf, out_buf, hess_buf, part_buf, in_sem, out_sem = rest[-7:]
-    outs = rest[-10:-7] if has_out else (*rest[-9:-7], None)
+    lhs_ref, x_buf, w_buf, out_buf, hess_buf, part_buf, lhs_sem, in_sem, out_sem = rest[-9:]
+    outs = rest[-12:-9] if has_out else (*rest[-11:-9], None)
     out_hbm, hess_hbm, part_out = outs
     rows = hess_buf.shape[1]
     all_rows = lhs_ref.shape[0]
@@ -175,11 +175,23 @@
                 copies.append((out_buf.at[slot, :, lanes], out_hbm.at[:, pl.ds(column(p, h), width)]))
         return [pltpu.make_async_copy(a, b, out_sem.at[slot, n]) for n, (a, b) in enumerate(copies)]
 
+    cut = (NX - 1) * tok
+    sides = [
+        pltpu.make_async_copy(lhs_hbm.at[:, pl.ds(a, n)], lhs_ref.at[:, pl.ds(a, n)], lhs_sem.at[i])
+        for i, (a, n) in enumerate(((0, cut), (cut, tok)))
+    ]
+    sides[1].start()
     for copy in loads(0):
         copy.start()
+    sides[0].start()
+    sides[1].wait()
+    there = False
     for p in range(len(pairs)):
         slot = p % 2
         low, high, _, begin, leave = pairs[p]
+        if low == 0 and not there:
+            sides[0].wait()
+            there = True
         if p + 1 < len(pairs):
             for copy in loads(p + 1):
                 copy.start()
@@ -231,22 +243,21 @@
             copy.wait()
 
 
-def columns_step(base, lhs, corr, panel, weight, pieces, entries, low, high, begin, leave, parts, out, hess):
+def columns_step(lhs, corr, panel, weight, info, pieces, entries, low, high, begin, leave, parts, out, hess):
     tok, width = pieces[0].shape[1:]
     out_rows, chans = weight.shape
     rows = lhs.shape[0] - PANEL
-    info = jnp.concatenate([base, jnp.stack([place for place, _ in entries])]).astype(jnp.int32)
     pairs = [
         (low[i], high[i], (entries[2 * i][1], entries[2 * i + 1][1]), begin[i], leave[i])
         for i in range(len(entries) // 2)
     ]
     n_out = sum(a is not None for a in leave)
     fixed = lambda i, info: (0, 0)
-    anywhere = pl.BlockSpec(memory_space=pltpu.HBM)
+    anywhere = pl.BlockSpec(memory_space=pl.ANY)
     operands = [lhs, corr, panel, weight, *pieces]
     if parts is not None:
         operands.append(parts)
-    in_specs = [pl.BlockSpec(a.shape, fixed) for a in (lhs, corr, panel)] + [anywhere] * (len(operands) - 3)
+    in_specs = [anywhere] + [pl.BlockSpec(a.shape, fixed) for a in (corr, panel)] + [anywhere] * (len(operands) - 3)
     aliases = {}
     if out is not None:
         in_specs += [anywhere] * 2
@@ -269,11 +280,13 @@
             in_specs=in_specs,
             out_specs=[anywhere] * len(out_shape),
             scratch_shapes=[
+                pltpu.VMEM(lhs.shape, lhs.dtype),
                 pltpu.VMEM((2, NX * tok, 2 * width), jnp.bfloat16),
                 pltpu.VMEM((2, out_rows, 2 * width), weight.dtype),
                 pltpu.VMEM((2, out_rows, 2 * width), weight.dtype),
                 pltpu.VMEM((2, rows, 2 * width), jnp.float32),
                 pltpu.VMEM((2, *part), jnp.float32),
+                pltpu.SemaphoreType.DMA((2,)),
                 pltpu.SemaphoreType.DMA((2, 2 * NX + 3)),
                 pltpu.SemaphoreType.DMA((2, 4)),
             ],
@@ -298,23 +311,45 @@
     ncol = NY * NZ
     half = block // 2
 
+    base = jnp.stack([r * chans, (d * ncol + c) * block])
+    def place(dy, dz, part):
+        return (((y + dy) % NY) * NZ + (z + dz) % NZ) * 2 + part
+
+    def second_entries(shifts):
+        return [
+            (place(s, dz, 1), [(2 * i + k // 2, (k % 2) * NZ + dz) for k in range(NX)])
+            for i, s in enumerate(shifts)
+            for dz in range(NZ)
+        ]
+
+    def first_entries(skip, ks):
+        return [
+            (place(s, dz, 0), [(skip + 2 * k + i // 2, (i % 2) * NZ + dz) for k in ks])
+            for i, s in enumerate(SHIFTS)
+            for dz in range(NZ)
+        ]
+
+    far = NX - 1
+    near_entries = second_entries(SHIFTS[:far]) + first_entries(NX * 2 - 2, range(far))
+    far_entries = [
+        (place, [(2 + which, lead)]) for place, ((which, lead),) in first_entries(0, [0])
+    ] + second_entries(SHIFTS[far:])
+    near_info, far_info = (
+        jnp.concatenate([base, jnp.stack([place for place, _ in entries])]).astype(jnp.int32)
+        for entries in (near_entries, far_entries)
+    )
+    turn = ((r ^ jnp.arange(NROW)) - d) % NX
+    slots = jnp.where(turn == 0, 0, jnp.where(turn == far, 1, turn + 1)).astype(jnp.int32)
+
     other = send_z(activation)
 
-    everywhere = ("dp", "row", "col")
-    per_x = NROW * ncol
     ap = jnp.where((r == 0) & (c == 0), activation[:, :PANEL], jnp.zeros((tok, PANEL), activation.dtype))
-    ap = functools.reduce(
-        jnp.add, [lax.ppermute(ap, ("row", "col"), [(0, k * NZ)]) for k in range(1, NY)], ap
-    )
+    ap = functools.reduce(jnp.add, [send_y(ap, k) for k in (1, -1, 2)], ap)
     ap, other, activation = lax.optimization_barrier((ap, other, activation))
-    ap = jnp.concatenate(
-        [ap]
-        + [
-            lax.ppermute(ap, everywhere, [(a * per_x + k * NZ, b * per_x + k * NZ) for a, b in x_perm(s) for k in range(NY)])
-            for s in (1, -1, 2)
-        ]
-    )
-    other, ap, activation = lax.optimization_barrier((other, ap, activation))
+    ap = jnp.concatenate([ap] + [send_x(ap, k) for k in (1, -1, 2)])
+    other, ap, activation, near_info, far_info, slots = lax.optimization_barrier(
+        (other, ap, activation, near_info, far_info, slots)
+    )
 
     first = jnp.stack([activation[:, :half], other[:, :half]])
     second = jnp.stack([activation[:, half:], other[:, half:]])
@@ -349,42 +384,26 @@
     )
     first_far, second_far = ring_out(*first_out, send_x), ring_out(*second_out, send_y)
     core = lax.ppermute(jnp.stack([own, own_z]), "row", [(i, i ^ 1) for i in range(NROW)])
-    order = jnp.array([0, 2, 3, 1], jnp.int32)
-    lhs = lhs_step(order[((r ^ jnp.arange(NROW)) - d) % NX], own, own_z, core, ap)
-
-    base = jnp.stack([r * chans, (d * ncol + c) * block])
-    step = functools.partial(columns_step, base, lhs, corr, panel, weight)
-
-    def place(dy, dz, part):
-        return (((y + dy) % NY) * NZ + (z + dz) % NZ) * 2 + part
-
-    def second_entries(shifts):
-        return [
-            (place(s, dz, 1), [(2 * i + k // 2, (k % 2) * NZ + dz) for k in range(NX)])
-            for i, s in enumerate(shifts)
-            for dz in range(NZ)
-        ]
-
-    def first_entries(skip, ks):
-        return [
-            (place(s, dz, 0), [(skip + 2 * k + i // 2, (i % 2) * NZ + dz) for k in ks])
-            for i, s in enumerate(SHIFTS)
-            for dz in range(NZ)
-        ]
-
-    far = NX - 1
+    lhs = lhs_step(slots, own, own_z, core, ap)
+
+    step = functools.partial(columns_step, lhs, corr, panel, weight)
     pieces = [*second, second_out[0], second_in[0], second_in[1], second_out[1]]
-    skip = len(pieces)
     pieces += [*first, first_out[0], first_in[0], first_in[1], first_out[1]]
-    entries = second_entries(SHIFTS[:far]) + first_entries(skip, range(far))
-    none, slots = [None] * NX, list(range(NX))
-    out, hess, parts = step(
-        pieces, entries, [0] * 7, [NX] * 3 + [far] * 4, [None] * 7, none[:3] + slots, None, None, None
-    )
-    entries = second_entries(SHIFTS[far:])
-    entries += [(place, [(2 + which, lead)]) for place, ((which, lead),) in first_entries(0, [0])]
+    none, parts = [None] * NX, list(range(NX))
+    out, hess, sums = step(
+        near_info, pieces, near_entries, [0] * 7, [NX] * 3 + [far] * 4, [None] * 7, none[:3] + parts, None, None, None
+    )
     out, hess = step(
-        [*second_far, *first_far], entries, [0] + [far] * 4, [NX] * 5, [None] + slots, [None] * 5, parts, out, hess
+        far_info,
+        [*second_far, *first_far],
+        far_entries,
+        [far] * 4 + [0],
+        [NX] * 5,
+        parts + [None],
+        [None] * 5,
+        sums,
+        out,
+        hess,
     )
     return (out, hess)
 

time: 163 us -> 156 us (0.957)
  Pallas kernels: 49.3 us -> 37.7 us
  waiting for transfers between devices: 49.7 us -> 60.6 us
  local copies, waits for them, and re-layouts: 6.83 us -> 0.39 us
  starting transfers between devices: 51.4 us -> 53.1 us
    ppermute x10 -> x13, waiting for transfers between devices: 3.76 us -> 19.2 us  [send_y(): return lax.ppermute(a, 'col', y_perm(k))]
    ppermute x1, waiting for transfers between devices: 8.29 us -> 0.05 us  [send_z(): return lax.ppermute(a, 'col', Z_PERM)]
    pallas_call x2, Pallas kernels: 31.3 us -> 24 us  [columns_step(): pl.pallas_call(body, grid_spec=pltpu.PrefetchScalarGridSpec(num_scalar_pr...]
    ppermute x10 -> x13, waiting for transfers between devices: 16.1 us -> 23.3 us  [send_x(): return lax.ppermute(a, 'dp', x_perm(k))]
    ppermute x1, waiting for transfers between devices: 10.5 us -> 4.1 us  [body(): both = both + lax.ppermute(both, 'row', [(0, 2), (1, 3)])]
    ppermute x10 -> x13, starting transfers between devices: 16.5 us -> 21.7 us  [send_y(): return lax.ppermute(a, 'col', y_perm(k))]
    ppermute x6 -> x0, starting transfers between devices: 4 us -> none  [the longest x3 2.01 us: body(): lax.ppermute(ap, ('row', 'col'), [(0, k * NZ)])]
    ppermute x10 -> x13, starting transfers between devices: 17.1 us -> 20.8 us  [send_x(): return lax.ppermute(a, 'dp', x_perm(k))]
  transfers between devices with their start and end apart: 33 -> 33, of which waited for: 13 -> 22; matrix products, arithmetic and copies ran while one was open for 5% -> 2% of each run, Pallas kernels for 22% -> 18%
where the time goes in v4:
time: 156 us
  waiting for transfers between devices  60.6 us (39%)
  starting transfers between devices  53.1 us (34%)
  Pallas kernels  37.7 us (24%)
  other arithmetic  3.11 us (2%)
    pallas_call x2, Pallas kernels, columns_step(): pl.pallas_call(body, grid_spec=pltpu.PrefetchScalarGridSpec(num_scalar_pr...  24 us
    ppermute x13, waiting for transfers between devices, send_x(): return lax.ppermute(a, 'dp', x_perm(k))  23.3 us
    ppermute x13, starting transfers between devices, send_y(): return lax.ppermute(a, 'col', y_perm(k))  21.7 us
    ppermute x13, starting transfers between devices, send_x(): return lax.ppermute(a, 'dp', x_perm(k))  20.8 us
    ppermute x13, waiting for transfers between devices, send_y(): return lax.ppermute(a, 'col', y_perm(k))  19.2 us
    pallas_call x1, Pallas kernels, panel_step(): pl.pallas_call(panel_kernel, out_shape=(jax.ShapeDtypeStruct((rows, PANEL...  12.4 us
    ppermute x1, waiting for transfers between devices, body(): own_z = lax.ppermute(own, 'row', [(i, i ^ 2) for i in range(NROW)])  11.6 us
    ppermute x1, waiting for transfers between devices, body(): both = both + lax.ppermute(both, 'row', [(0, 2), (1, 3)])  4.1 us
  transfers between devices with their start and end apart: 33, of which 22 were waited for; matrix products, arithmetic and copies ran while one was open for 2% of the time, Pallas kernels for 18%

profile of v4, /device:TPU:64, one launch (start us, length us, event | category | flops | bytes accessed | tf_op | source)
XLA Modules:
  0.0 156.0 jit_solution(9779920688093967343)
XLA Ops:
  0.6 1.7 %collective-permute-start.3 = (bf16[512,512]{1,0:T(8,128)(2,1)}, bf16[512,512]{1,0:T(8,128)(2,1)S(1)}, u32[]{:S(2)}, u32[]{:S(2)}) collective-permute-start(bf16[512,512]{1,0:T(8,128)(2,1)} %param.4), channel_id=1, source_target_pairs={{0,1},{1,0},{2,3},{3,2},{4,5},{5,4},{6,7},{7,6},{8,9},{9,8},{10,11... | collective-permute-start | bytes 1572872 | tf_op jit(solution)/shard_map/ppermute | solution.py:41
  2.3 0.9 slice_select_fusion
  3.3 1.6 %collective-permute-start = (bf16[512,128]{1,0:T(8,128)(2,1)S(1)}, bf16[512,128]{1,0:T(8,128)(2,1)S(1)}, u32[]{:S(2)}, u32[]{:S(2)}) collective-permute-start(bf16[512,128]{1,0:T(8,128)(2,1)S(1)} %slice_select_fusion), channel_id=1, source_target_pairs={{0,2},{1,3},{2,4},{3,5},{4,6},{5,7},{6,0},{7,1},{8,10},{9,11},{10,... | collective-permute-start | bytes 393224 | tf_op jit(solution)/shard_map/ppermute | solution.py:37
  4.9 1.7 %collective-permute-start.1 = (bf16[512,128]{1,0:T(8,128)(2,1)S(1)}, bf16[512,128]{1,0:T(8,128)(2,1)S(1)}, u32[]{:S(2)}, u32[]{:S(2)}) collective-permute-start(bf16[512,128]{1,0:T(8,128)(2,1)S(1)} %slice_select_fusion), channel_id=1, source_target_pairs={{0,6},{1,7},{2,0},{3,1},{4,2},{5,3},{6,4},{7,5},{8,14},{9,15},{10,... | collective-permute-start | bytes 393224 | tf_op jit(solution)/shard_map/ppermute | solution.py:37
  6.6 2.0 %collective-permute-start.2 = (bf16[512,128]{1,0:T(8,128)(2,1)S(1)}, bf16[512,128]{1,0:T(8,128)(2,1)S(1)}, u32[]{:S(2)}, u32[]{:S(2)}) collective-permute-start(bf16[512,128]{1,0:T(8,128)(2,1)S(1)} %slice_select_fusion), channel_id=1, source_target_pairs={{0,4},{1,5},{2,6},{3,7},{4,0},{5,1},{6,2},{7,3},{8,12},{9,13},{10,... | collective-permute-start | bytes 393224 | tf_op jit(solution)/shard_map/ppermute | solution.py:37
  8.6 1.0 collective-permute-done
  9.6 1.4 collective-permute-done.1
  11.0 2.6 %collective-permute-done.2 = bf16[512,128]{1,0:T(8,128)(2,1)S(1)} collective-permute-done((bf16[512,128]{1,0:T(8,128)(2,1)S(1)}, bf16[512,128]{1,0:T(8,128)(2,1)S(1)}, u32[]{:S(2)}, u32[]{:S(2)}) %collective-permute-start.2) | collective-permute-done | bytes 131104 | tf_op jit(solution)/shard_map/ppermute | solution.py:37
  13.6 0.9 add_add_fusion
  14.6 1.5 collective-permute-start.4
  16.1 1.7 %collective-permute-start.5 = (bf16[512,128]{1,0:T(8,128)(2,1)S(1)}, bf16[512,128]{1,0:T(8,128)(2,1)S(1)}, u32[]{:S(2)}, u32[]{:S(2)}) collective-permute-start(bf16[512,128]{1,0:T(8,128)(2,1)S(1)} %add_add_fusion), channel_id=1, source_target_pairs={{0,96},{32,0},{64,32},{96,64},{1,97},{33,1},{65,33},{97,65},{2,98}... | collective-permute-start | bytes 393224 | tf_op jit(solution)/shard_map/ppermute | solution.py:33
  17.9 1.8 %collective-permute-start.6 = (bf16[512,128]{1,0:T(8,128)(2,1)S(1)}, bf16[512,128]{1,0:T(8,128)(2,1)S(1)}, u32[]{:S(2)}, u32[]{:S(2)}) collective-permute-start(bf16[512,128]{1,0:T(8,128)(2,1)S(1)} %add_add_fusion), channel_id=1, source_target_pairs={{0,64},{32,96},{64,0},{96,32},{1,65},{33,97},{65,1},{97,33},{2,66}... | collective-permute-start | bytes 393224 | tf_op jit(solution)/shard_map/ppermute | solution.py:33
  19.9 1.2 collective-permute-done.4
  21.1 1.1 collective-permute-done.5
  22.2 2.4 %collective-permute-done.6 = bf16[512,128]{1,0:T(8,128)(2,1)S(1)} collective-permute-done((bf16[512,128]{1,0:T(8,128)(2,1)S(1)}, bf16[512,128]{1,0:T(8,128)(2,1)S(1)}, u32[]{:S(2)}, u32[]{:S(2)}) %collective-permute-start.6) | collective-permute-done | bytes 131104 | tf_op jit(solution)/shard_map/ppermute | solution.py:33
  24.8 1.9 %collective-permute-start.10 = (bf16[2,512,256]{2,1,0:T(8,128)(2,1)S(1)}, bf16[2,512,256]{2,1,0:T(8,128)(2,1)S(1)}, u32[]{:S(2)}, u32[]{:S(2)}) collective-permute-start(bf16[2,512,256]{2,1,0:T(8,128)(2,1)S(1)} %pad_maximum_fusion.8), channel_id=1, source_target_pairs={{0,96},{32,0},{64,32},{96,64},{1,97},{33,1},{65,33},{97,65},{2,98}... | collective-permute-start | bytes 1572872 | tf_op jit(solution)/shard_map/ppermute | solution.py:33
  26.7 0.2 collective-permute-start.9
  26.9 0.7 collective-permute-start.11
  27.6 1.6 %collective-permute-start.7 = (bf16[2,512,256]{2,1,0:T(8,128)(2,1)S(1)}, bf16[2,512,256]{2,1,0:T(8,128)(2,1)S(1)}, u32[]{:S(2)}, u32[]{:S(2)}) collective-permute-start(bf16[2,512,256]{2,1,0:T(8,128)(2,1)S(1)} %pad_maximum_fusion.7), channel_id=1, source_target_pairs={{0,2},{1,3},{2,4},{3,5},{4,6},{5,7},{6,0},{7,1},{8,10},{9,11},{10,... | collective-permute-start | bytes 1572872 | tf_op jit(solution)/shard_map/ppermute | solution.py:37
  29.2 1.7 %collective-permute-start.8 = (bf16[2,512,256]{2,1,0:T(8,128)(2,1)S(1)}, bf16[2,512,256]{2,1,0:T(8,128)(2,1)S(1)}, u32[]{:S(2)}, u32[]{:S(2)}) collective-permute-start(bf16[2,512,256]{2,1,0:T(8,128)(2,1)S(1)} %pad_maximum_fusion.7), channel_id=1, source_target_pairs={{0,6},{1,7},{2,0},{3,1},{4,2},{5,3},{6,4},{7,5},{8,14},{9,15},{10,... | collective-permute-start | bytes 1572872 | tf_op jit(solution)/shard_map/ppermute | solution.py:37
  31.0 0.1 add.230
  31.1 6.4 %collective-permute-done.10 = bf16[2,512,256]{2,1,0:T(8,128)(2,1)S(1)} collective-permute-done((bf16[2,512,256]{2,1,0:T(8,128)(2,1)S(1)}, bf16[2,512,256]{2,1,0:T(8,128)(2,1)S(1)}, u32[]{:S(2)}, u32[]{:S(2)}) %collective-permute-start.10) | collective-permute-done | bytes 524320 | tf_op jit(solution)/shard_map/ppermute | solution.py:33
  37.5 1.9 %collective-permute-done.9 = bf16[2,512,256]{2,1,0:T(8,128)(2,1)S(1)} collective-permute-done((bf16[2,512,256]{2,1,0:T(8,128)(2,1)S(1)}, bf16[2,512,256]{2,1,0:T(8,128)(2,1)S(1)}, u32[]{:S(2)}, u32[]{:S(2)}) %collective-permute-start.9) | collective-permute-done | bytes 524320 | tf_op jit(solution)/shard_map/ppermute | solution.py:33
  39.4 1.6 %collective-permute-done.7 = bf16[2,512,256]{2,1,0:T(8,128)(2,1)S(1)} collective-permute-done((bf16[2,512,256]{2,1,0:T(8,128)(2,1)S(1)}, bf16[2,512,256]{2,1,0:T(8,128)(2,1)S(1)}, u32[]{:S(2)}, u32[]{:S(2)}) %collective-permute-start.7) | collective-permute-done | bytes 524320 | tf_op jit(solution)/shard_map/ppermute | solution.py:37
  41.0 0.7 collective-permute-start.20
  41.8 0.4 collective-permute-start.14
  42.1 3.0 %collective-permute-start.15 = (bf16[1,512,256]{2,1,0:T(8,128)(2,1)S(1)}, bf16[1,512,256]{2,1,0:T(8,128)(2,1)S(1)}, u32[]{:S(2)}, u32[]{:S(2)}) collective-permute-start(bf16[1,512,256]{2,1,0:T(8,128)(2,1)S(1)} %slice.44), channel_id=1, source_target_pairs={{0,96},{32,0},{64,32},{96,64},{1,97},{33,1},{65,33},{97,65},{2,98}... | collective-permute-start | bytes 786440 | tf_op jit(solution)/shard_map/ppermute | solution.py:33
  45.2 1.3 collective-permute-start.12
  46.5 2.1 %collective-permute-start.13 = (bf16[1,512,256]{2,1,0:T(8,128)(2,1)S(1)}, bf16[1,512,256]{2,1,0:T(8,128)(2,1)S(1)}, u32[]{:S(2)}, u32[]{:S(2)}) collective-permute-start(bf16[1,512,256]{2,1,0:T(8,128)(2,1)S(1)} %slice.42), channel_id=1, source_target_pairs={{0,6},{1,7},{2,0},{3,1},{4,2},{5,3},{6,4},{7,5},{8,14},{9,15},{10,... | collective-permute-start | bytes 786440 | tf_op jit(solution)/shard_map/ppermute | solution.py:37
  48.6 0.1 pad_maximum_fusion.2.rest_0_
  48.7 0.2 fusion.1
  48.9 1.3 collective-permute-start.21
  50.2 0.1 pad_maximum_fusion.rest_6_
  50.3 0.1 pad_maximum_fusion.3.rest_1_
  50.5 2.4 %collective-permute-done.12 = bf16[1,512,256]{2,1,0:T(8,128)(2,1)S(1)} collective-permute-done((bf16[1,512,256]{2,1,0:T(8,128)(2,1)S(1)}, bf16[1,512,256]{2,1,0:T(8,128)(2,1)S(1)}, u32[]{:S(2)}, u32[]{:S(2)}) %collective-permute-start.12) | collective-permute-done | bytes 262176 | tf_op jit(solution)/shard_map/ppermute | solution.py:37
  52.9 0.1 pad_maximum_fusion.1.rest_7_
  53.1 3.2 %collective-permute-start.17 = (bf16[4,512,256]{2,1,0:T(8,128)(2,1)S(1)}, bf16[4,512,256]{2,1,0:T(8,128)(2,1)S(1)}, u32[]{:S(2)}, u32[]{:S(2)}) collective-permute-start(bf16[4,512,256]{2,1,0:T(8,128)(2,1)S(1)} %pad_maximum_fusion.1.rest_7_), channel_id=1, source_target_pairs={{0,96},{32,0},{64,32},{96,64},{1,97},{33,1},{65,33},{97,65},{2,98}... | collective-permute-start | bytes 3145736 | tf_op jit(solution)/shard_map/ppermute | solution.py:33
  56.4 1.3 collective-permute-start.18
  57.6 2.0 %collective-permute-start.19 = (bf16[4,512,256]{2,1,0:T(8,128)(2,1)S(1)}, bf16[4,512,256]{2,1,0:T(8,128)(2,1)S(1)}, u32[]{:S(2)}, u32[]{:S(2)}) collective-permute-start(bf16[4,512,256]{2,1,0:T(8,128)(2,1)S(1)} %pad_maximum_fusion.3.rest_1_), channel_id=1, source_target_pairs={{0,6},{1,7},{2,0},{3,1},{4,2},{5,3},{6,4},{7,5},{8,14},{9,15},{10,... | collective-permute-start | bytes 3145736 | tf_op jit(solution)/shard_map/ppermute | solution.py:37
  59.6 4.1 %collective-permute-done.21 = bf16[2304,128]{1,0:T(8,128)(2,1)S(1)} collective-permute-done((bf16[2304,128]{1,0:T(8,128)(2,1)S(1)}, bf16[2304,128]{1,0:T(8,128)(2,1)S(1)}, u32[]{:S(2)}, u32[]{:S(2)}) %collective-permute-start.21) | collective-permute-done | bytes 589856 | tf_op jit(solution)/shard_map/ppermute | solution.py:367
  63.7 2.1 %collective-permute-start.22 = (bf16[512,512]{1,0:T(8,128)(2,1)S(1)}, bf16[512,512]{1,0:T(8,128)(2,1)S(1)}, u32[]{:S(2)}, u32[]{:S(2)}) collective-permute-start(bf16[512,512]{1,0:T(8,128)(2,1)S(1)} %copy-done.3), channel_id=1, source_target_pairs={{0,0},{8,32},{16,64},{24,96},{32,8},{40,40},{48,72},{56,104},{64,1... | collective-permute-start | bytes 1572872 | tf_op jit(solution)/shard_map/ppermute | solution.py:376
  65.8 0.2 add.232
  66.1 12.4 %panel_sweep.1 = (f32[256,128]{1,0:T(8,128)S(1)}, bf16[256,128]{1,0:T(8,128)(2,1)S(1)}) custom-call(bf16[4,512,128]{2,1,0:T(8,128)(2,1)S(1)} %bitcast.30, bf16[256,128]{1,0:T(8,128)(2,1)S(1)} %slice.49.wp_ref, s32[256,128]{1,0:T(8,128)S(1)} %copy-done.1, s32[1,128]{1,0:T(1,128)S(1)} %bitcast.34), custom_call_target="tpu_custom_call" | custom-call | flops 8589934592 | bytes 33554432 | tf_op jit(solution)/shard_map/panel_sweep/pallas_call | solution.py:102
  78.4 2.3 %collective-permute-done.22.own_ref = bf16[512,512]{1,0:T(8,128)(2,1)S(1)} collective-permute-done((bf16[512,512]{1,0:T(8,128)(2,1)S(1)}, bf16[512,512]{1,0:T(8,128)(2,1)S(1)}, u32[]{:S(2)}, u32[]{:S(2)}) %collective-permute-start.22) | collective-permute-done | bytes 524320 | tf_op jit(solution)/shard_map/ppermute | solution.py:376
  80.8 4.8 %collective-permute-done.17.rest_11_ = bf16[4,512,256]{2,1,0:T(8,128)(2,1)S(1)} collective-permute-done((bf16[4,512,256]{2,1,0:T(8,128)(2,1)S(1)}, bf16[4,512,256]{2,1,0:T(8,128)(2,1)S(1)}, u32[]{:S(2)}, u32[]{:S(2)}) %collective-permute-start.17) | collective-permute-done | bytes 1048608 | tf_op jit(solution)/shard_map/ppermute | solution.py:33
  85.6 0.7 collective-permute-start.23
  86.3 3.1 %collective-permute-start.24 = (bf16[4,512,256]{2,1,0:T(8,128)(2,1)S(1)}, bf16[4,512,256]{2,1,0:T(8,128)(2,1)S(1)}, u32[]{:S(2)}, u32[]{:S(2)}) collective-permute-start(bf16[4,512,256]{2,1,0:T(8,128)(2,1)S(1)} %pad_maximum_fusion.rest_6_), channel_id=1, source_target_pairs={{0,96},{32,0},{64,32},{96,64},{1,97},{33,1},{65,33},{97,65},{2,98}... | collective-permute-start | bytes 3145736 | tf_op jit(solution)/shard_map/ppermute | solution.py:33
  89.4 1.1 collective-permute-start.25
  90.5 2.1 %collective-permute-start.26 = (bf16[4,512,256]{2,1,0:T(8,128)(2,1)S(1)}, bf16[4,512,256]{2,1,0:T(8,128)(2,1)S(1)}, u32[]{:S(2)}, u32[]{:S(2)}) collective-permute-start(bf16[4,512,256]{2,1,0:T(8,128)(2,1)S(1)} %pad_maximum_fusion.2.rest_0_), channel_id=1, source_target_pairs={{0,6},{1,7},{2,0},{3,1},{4,2},{5,3},{6,4},{7,5},{8,14},{9,15},{10,... | collective-permute-start | bytes 3145736 | tf_op jit(solution)/shard_map/ppermute | solution.py:37
  92.6 3.2 %collective-permute-start.27 = (bf16[512,512]{1,0:T(8,128)(2,1)S(1)}, bf16[512,512]{1,0:T(8,128)(2,1)S(1)}, u32[]{:S(2)}, u32[]{:S(2)}) collective-permute-start(bf16[512,512]{1,0:T(8,128)(2,1)S(1)} %collective-permute-done.22.own_ref), channel_id=1, source_target_pairs={{0,16},{8,24},{16,0},{24,8},{1,17},{9,25},{17,1},{25,9},{2,18},{10... | collective-permute-start | bytes 1572872 | tf_op jit(solution)/shard_map/ppermute | solution.py:381
  95.8 11.6 %collective-permute-done.27.own_z_ref = bf16[512,512]{1,0:T(8,128)(2,1)S(1)} collective-permute-done((bf16[512,512]{1,0:T(8,128)(2,1)S(1)}, bf16[512,512]{1,0:T(8,128)(2,1)S(1)}, u32[]{:S(2)}, u32[]{:S(2)}) %collective-permute-start.27) | collective-permute-done | bytes 524320 | tf_op jit(solution)/shard_map/ppermute | solution.py:381
  107.4 3.2 %collective-permute-done.23.rest_9_ = bf16[4,512,256]{2,1,0:T(8,128)(2,1)S(1)} collective-permute-done((bf16[4,512,256]{2,1,0:T(8,128)(2,1)S(1)}, bf16[4,512,256]{2,1,0:T(8,128)(2,1)S(1)}, u32[]{:S(2)}, u32[]{:S(2)}) %collective-permute-start.23) | collective-permute-done | bytes 1048608 | tf_op jit(solution)/shard_map/ppermute | solution.py:33
  110.6 3.9 %collective-permute-done.25.rest_3_ = bf16[4,512,256]{2,1,0:T(8,128)(2,1)S(1)} collective-permute-done((bf16[4,512,256]{2,1,0:T(8,128)(2,1)S(1)}, bf16[4,512,256]{2,1,0:T(8,128)(2,1)S(1)}, u32[]{:S(2)}, u32[]{:S(2)}) %collective-permute-start.25) | collective-permute-done | bytes 1048608 | tf_op jit(solution)/shard_map/ppermute | solution.py:37
  114.6 1.0 collective-permute-done.26.rest_4_
  115.7 0.9 collective-permute-start.28
  116.6 0.5 collective-permute-start.29
  117.2 2.7 %collective-permute-start.30 = (bf16[4,512,256]{2,1,0:T(8,128)(2,1)S(1)}, bf16[4,512,256]{2,1,0:T(8,128)(2,1)S(1)}, u32[]{:S(2)}, u32[]{:S(2)}) collective-permute-start(bf16[4,512,256]{2,1,0:T(8,128)(2,1)S(1)} %collective-permute-done.19.rest_5_), channel_id=1, source_target_pairs={{0,6},{1,7},{2,0},{3,1},{4,2},{5,3},{6,4},{7,5},{8,14},{9,15},{10,... | collective-permute-start | bytes 3145736 | tf_op jit(solution)/shard_map/ppermute | solution.py:37
  119.9 3.2 %collective-permute-start.32 = (bf16[4,512,256]{2,1,0:T(8,128)(2,1)S(1)}, bf16[4,512,256]{2,1,0:T(8,128)(2,1)S(1)}, u32[]{:S(2)}, u32[]{:S(2)}) collective-permute-start(bf16[4,512,256]{2,1,0:T(8,128)(2,1)S(1)} %collective-permute-done.17.rest_11_), channel_id=1, source_target_pairs={{0,96},{32,0},{64,32},{96,64},{1,97},{33,1},{65,33},{97,65},{2,98}... | collective-permute-start | bytes 3145736 | tf_op jit(solution)/shard_map/ppermute | solution.py:33
  123.1 1.3 lhs.1.lhs_hbm
  124.4 14.2 %columns.2 = (bf16[256,4096]{1,0:T(8,128)(2,1)}, f32[512,4096]{1,0:T(8,128)}, f32[4,648,512]{2,1,0:T(8,128)S(1)}) custom-call(s32[16]{0:T(128)S(1)} %concatenate.29.info, bf16[640,2048]{1,0:T(8,128)(2,1)S(1)} %lhs.1.lhs_hbm, f32[256,128]{1,0:T(8,128)S(1)} %get-tuple-element.76.corr_ref, bf16[256,128]{1,0:T(8,128)(2,1)S(1)} %get-tuple-element.77.panel_ref, ...), custom_call_target="tpu_custom_call" | custom-call | flops 9395240960 | bytes 28311552 | tf_op jit(solution)/shard_map/columns/pallas_call | solution.py:275
  138.6 4.6 %collective-permute-done.29.rest_0_ = bf16[4,512,256]{2,1,0:T(8,128)(2,1)S(1)} collective-permute-done((bf16[4,512,256]{2,1,0:T(8,128)(2,1)S(1)}, bf16[4,512,256]{2,1,0:T(8,128)(2,1)S(1)}, u32[]{:S(2)}, u32[]{:S(2)}) %collective-permute-start.29) | collective-permute-done | bytes 1048608 | tf_op jit(solution)/shard_map/ppermute | solution.py:37
  143.3 0.5 collective-permute-done.30.rest_1_
  143.7 2.3 %collective-permute-done.31.rest_2_ = bf16[4,512,256]{2,1,0:T(8,128)(2,1)S(1)} collective-permute-done((bf16[4,512,256]{2,1,0:T(8,128)(2,1)S(1)}, bf16[4,512,256]{2,1,0:T(8,128)(2,1)S(1)}, u32[]{:S(2)}, u32[]{:S(2)}) %collective-permute-start.31) | collective-permute-done | bytes 1048608 | tf_op jit(solution)/shard_map/ppermute | solution.py:33
  146.0 9.8 %columns.3 = (bf16[256,4096]{1,0:T(8,128)(2,1)}, f32[512,4096]{1,0:T(8,128)}) custom-call(s32[12]{0:T(128)S(1)} %concatenate.30.info, bf16[640,2048]{1,0:T(8,128)(2,1)S(1)} %lhs.1.lhs_hbm, f32[256,128]{1,0:T(8,128)S(1)} %get-tuple-element.76.corr_ref, ...), custom_call_target="tpu_custom_call", output_to_operand_aliasing={{0}: (10, {}), {1}: (11, {})} | custom-call | flops 6710886400 | bytes 20971520 | tf_op jit(solution)/shard_map/columns/pallas_call | solution.py:275
  (39 shorter events, 0.9 us)
Async XLA Ops:
  0.6 24.0 %copy-start.3 = (bf16[512,512]{1,0:T(8,128)(2,1)S(1)}, bf16[512,512]{1,0:T(8,128)(2,1)}, u32[]{:S(2)}) copy-start(bf16[512,512]{1,0:T(8,128)(2,1)} %param.4) | copy-start | bytes 1572868
  0.6 14.0 %collective-permute-start.3 = (bf16[512,512]{1,0:T(8,128)(2,1)}, bf16[512,512]{1,0:T(8,128)(2,1)S(1)}, u32[]{:S(2)}, u32[]{:S(2)}) collective-permute-start(bf16[512,512]{1,0:T(8,128)(2,1)} %param.4), channel_id=1, source_target_pairs={{0,1},{1,0},{2,3},{3,2},{4,5},{5,4},{6,7},{7,6},{8,9},{9,8},{10,11... | collective-permute-start | bytes 1572872 | tf_op jit(solution)/shard_map/ppermute | solution.py:41
  3.3 6.3 %collective-permute-start = (bf16[512,128]{1,0:T(8,128)(2,1)S(1)}, bf16[512,128]{1,0:T(8,128)(2,1)S(1)}, u32[]{:S(2)}, u32[]{:S(2)}) collective-permute-start(bf16[512,128]{1,0:T(8,128)(2,1)S(1)} %slice_select_fusion), channel_id=1, source_target_pairs={{0,2},{1,3},{2,4},{3,5},{4,6},{5,7},{6,0},{7,1},{8,10},{9,11},{10,... | collective-permute-start | bytes 393224 | tf_op jit(solution)/shard_map/ppermute | solution.py:37
  4.9 6.0 %collective-permute-start.1 = (bf16[512,128]{1,0:T(8,128)(2,1)S(1)}, bf16[512,128]{1,0:T(8,128)(2,1)S(1)}, u32[]{:S(2)}, u32[]{:S(2)}) collective-permute-start(bf16[512,128]{1,0:T(8,128)(2,1)S(1)} %slice_select_fusion), channel_id=1, source_target_pairs={{0,6},{1,7},{2,0},{3,1},{4,2},{5,3},{6,4},{7,5},{8,14},{9,15},{10,... | collective-permute-start | bytes 393224 | tf_op jit(solution)/shard_map/ppermute | solution.py:37
  6.6 7.0 %collective-permute-start.2 = (bf16[512,128]{1,0:T(8,128)(2,1)S(1)}, bf16[512,128]{1,0:T(8,128)(2,1)S(1)}, u32[]{:S(2)}, u32[]{:S(2)}) collective-permute-start(bf16[512,128]{1,0:T(8,128)(2,1)S(1)} %slice_select_fusion), channel_id=1, source_target_pairs={{0,4},{1,5},{2,6},{3,7},{4,0},{5,1},{6,2},{7,3},{8,12},{9,13},{10,... | collective-permute-start | bytes 393224 | tf_op jit(solution)/shard_map/ppermute | solution.py:37
  14.6 6.5 %collective-permute-start.4 = (bf16[512,128]{1,0:T(8,128)(2,1)S(1)}, bf16[512,128]{1,0:T(8,128)(2,1)S(1)}, u32[]{:S(2)}, u32[]{:S(2)}) collective-permute-start(bf16[512,128]{1,0:T(8,128)(2,1)S(1)} %add_add_fusion), channel_id=1, source_target_pairs={{0,32},{32,64},{64,96},{96,0},{1,33},{33,65},{65,97},{97,1},{2,34}... | collective-permute-start | bytes 393224 | tf_op jit(solution)/shard_map/ppermute | solution.py:33
  16.1 6.1 %collective-permute-start.5 = (bf16[512,128]{1,0:T(8,128)(2,1)S(1)}, bf16[512,128]{1,0:T(8,128)(2,1)S(1)}, u32[]{:S(2)}, u32[]{:S(2)}) collective-permute-start(bf16[512,128]{1,0:T(8,128)(2,1)S(1)} %add_add_fusion), channel_id=1, source_target_pairs={{0,96},{32,0},{64,32},{96,64},{1,97},{33,1},{65,33},{97,65},{2,98}... | collective-permute-start | bytes 393224 | tf_op jit(solution)/shard_map/ppermute | solution.py:33
  17.9 6.7 %collective-permute-start.6 = (bf16[512,128]{1,0:T(8,128)(2,1)S(1)}, bf16[512,128]{1,0:T(8,128)(2,1)S(1)}, u32[]{:S(2)}, u32[]{:S(2)}) collective-permute-start(bf16[512,128]{1,0:T(8,128)(2,1)S(1)} %add_add_fusion), channel_id=1, source_target_pairs={{0,64},{32,96},{64,0},{96,32},{1,65},{33,97},{65,1},{97,33},{2,66}... | collective-permute-start | bytes 393224 | tf_op jit(solution)/shard_map/ppermute | solution.py:33
  24.6 6.3 %copy-start = (bf16[256,4096]{1,0:T(8,128)(2,1)S(1)}, bf16[256,4096]{1,0:T(8,128)(2,1)}, u32[]{:S(2)}) copy-start(bf16[256,4096]{1,0:T(8,128)(2,1)} %w_hbm.3) | copy-start | bytes 6291460
  24.8 12.7 %collective-permute-start.10 = (bf16[2,512,256]{2,1,0:T(8,128)(2,1)S(1)}, bf16[2,512,256]{2,1,0:T(8,128)(2,1)S(1)}, u32[]{:S(2)}, u32[]{:S(2)}) collective-permute-start(bf16[2,512,256]{2,1,0:T(8,128)(2,1)S(1)} %pad_maximum_fusion.8), channel_id=1, source_target_pairs={{0,96},{32,0},{64,32},{96,64},{1,97},{33,1},{65,33},{97,65},{2,98}... | collective-permute-start | bytes 1572872 | tf_op jit(solution)/shard_map/ppermute | solution.py:33
  26.7 12.7 %collective-permute-start.9 = (bf16[2,512,256]{2,1,0:T(8,128)(2,1)S(1)}, bf16[2,512,256]{2,1,0:T(8,128)(2,1)S(1)}, u32[]{:S(2)}, u32[]{:S(2)}) collective-permute-start(bf16[2,512,256]{2,1,0:T(8,128)(2,1)S(1)} %pad_maximum_fusion.8), channel_id=1, source_target_pairs={{0,32},{32,64},{64,96},{96,0},{1,33},{33,65},{65,97},{97,1},{2,34}... | collective-permute-start | bytes 1572872 | tf_op jit(solution)/shard_map/ppermute | solution.py:33
  26.9 4.1 %collective-permute-start.11 = (bf16[2048,128]{1,0:T(8,128)(2,1)S(1)}, bf16[2048,128]{1,0:T(8,128)(2,1)S(1)}, u32[]{:S(2)}, u32[]{:S(2)}) collective-permute-start(bf16[2048,128]{1,0:T(8,128)(2,1)S(1)} %pad_maximum_fusion.6), channel_id=1, source_target_pairs={{0,1},{2,3},{4,5},{6,7},{32,33},{34,35},{36,37},{38,39},{64,65},{6... | collective-permute-start | bytes 1572872 | tf_op jit(solution)/shard_map/ppermute | solution.py:358
  27.6 13.4 %collective-permute-start.7 = (bf16[2,512,256]{2,1,0:T(8,128)(2,1)S(1)}, bf16[2,512,256]{2,1,0:T(8,128)(2,1)S(1)}, u32[]{:S(2)}, u32[]{:S(2)}) collective-permute-start(bf16[2,512,256]{2,1,0:T(8,128)(2,1)S(1)} %pad_maximum_fusion.7), channel_id=1, source_target_pairs={{0,2},{1,3},{2,4},{3,5},{4,6},{5,7},{6,0},{7,1},{8,10},{9,11},{10,... | collective-permute-start | bytes 1572872 | tf_op jit(solution)/shard_map/ppermute | solution.py:37
  29.2 11.8 %collective-permute-start.8 = (bf16[2,512,256]{2,1,0:T(8,128)(2,1)S(1)}, bf16[2,512,256]{2,1,0:T(8,128)(2,1)S(1)}, u32[]{:S(2)}, u32[]{:S(2)}) collective-permute-start(bf16[2,512,256]{2,1,0:T(8,128)(2,1)S(1)} %pad_maximum_fusion.7), channel_id=1, source_target_pairs={{0,6},{1,7},{2,0},{3,1},{4,2},{5,3},{6,4},{7,5},{8,14},{9,15},{10,... | collective-permute-start | bytes 1572872 | tf_op jit(solution)/shard_map/ppermute | solution.py:37
  41.0 7.7 %collective-permute-start.20 = (bf16[2304,128]{1,0:T(8,128)(2,1)S(1)}, bf16[2304,128]{1,0:T(8,128)(2,1)S(1)}, u32[]{:S(2)}, u32[]{:S(2)}) collective-permute-start(bf16[2304,128]{1,0:T(8,128)(2,1)S(1)} %pad_maximum_fusion.5), channel_id=1, source_target_pairs={{0,8},{1,9},{2,10},{3,11},{4,12},{5,13},{6,14},{7,15},{32,40},{33,... | collective-permute-start | bytes 1769480 | tf_op jit(solution)/shard_map/ppermute | solution.py:366
  41.8 8.5 %collective-permute-start.14 = (bf16[1,512,256]{2,1,0:T(8,128)(2,1)S(1)}, bf16[1,512,256]{2,1,0:T(8,128)(2,1)S(1)}, u32[]{:S(2)}, u32[]{:S(2)}) collective-permute-start(bf16[1,512,256]{2,1,0:T(8,128)(2,1)S(1)} %slice.43), channel_id=1, source_target_pairs={{0,32},{32,64},{64,96},{96,0},{1,33},{33,65},{65,97},{97,1},{2,34}... | collective-permute-start | bytes 786440 | tf_op jit(solution)/shard_map/ppermute | solution.py:33
  42.1 8.1 %collective-permute-start.15 = (bf16[1,512,256]{2,1,0:T(8,128)(2,1)S(1)}, bf16[1,512,256]{2,1,0:T(8,128)(2,1)S(1)}, u32[]{:S(2)}, u32[]{:S(2)}) collective-permute-start(bf16[1,512,256]{2,1,0:T(8,128)(2,1)S(1)} %slice.44), channel_id=1, source_target_pairs={{0,96},{32,0},{64,32},{96,64},{1,97},{33,1},{65,33},{97,65},{2,98}... | collective-permute-start | bytes 786440 | tf_op jit(solution)/shard_map/ppermute | solution.py:33
  45.2 7.7 %collective-permute-start.12 = (bf16[1,512,256]{2,1,0:T(8,128)(2,1)S(1)}, bf16[1,512,256]{2,1,0:T(8,128)(2,1)S(1)}, u32[]{:S(2)}, u32[]{:S(2)}) collective-permute-start(bf16[1,512,256]{2,1,0:T(8,128)(2,1)S(1)} %slice.41), channel_id=1, source_target_pairs={{0,2},{1,3},{2,4},{3,5},{4,6},{5,7},{6,0},{7,1},{8,10},{9,11},{10,... | collective-permute-start | bytes 786440 | tf_op jit(solution)/shard_map/ppermute | solution.py:37
  46.5 6.4 %collective-permute-start.13 = (bf16[1,512,256]{2,1,0:T(8,128)(2,1)S(1)}, bf16[1,512,256]{2,1,0:T(8,128)(2,1)S(1)}, u32[]{:S(2)}, u32[]{:S(2)}) collective-permute-start(bf16[1,512,256]{2,1,0:T(8,128)(2,1)S(1)} %slice.42), channel_id=1, source_target_pairs={{0,6},{1,7},{2,0},{3,1},{4,2},{5,3},{6,4},{7,5},{8,14},{9,15},{10,... | collective-permute-start | bytes 786440 | tf_op jit(solution)/shard_map/ppermute | solution.py:37
  48.9 14.8 %collective-permute-start.21 = (bf16[2304,128]{1,0:T(8,128)(2,1)S(1)}, bf16[2304,128]{1,0:T(8,128)(2,1)S(1)}, u32[]{:S(2)}, u32[]{:S(2)}) collective-permute-start(bf16[2304,128]{1,0:T(8,128)(2,1)S(1)} %fusion.1), channel_id=1, source_target_pairs={{0,16},{8,24},{1,17},{9,25},{2,18},{10,26},{3,19},{11,27},{4,20},{... | collective-permute-start | bytes 1769480 | tf_op jit(solution)/shard_map/ppermute | solution.py:367
  50.4 15.6 %copy-start.1 = (s32[256,128]{1,0:T(8,128)S(1)}, s32[256,128]{1,0:T(8,128)}, u32[]{:S(2)}) copy-start(s32[256,128]{1,0:T(8,128)} %mask_ref.1) | copy-start | bytes 393220
  50.4 15.6 %copy-start.2 = (s32[128]{0:T(128)S(1)}, s32[128]{0:T(128)}, u32[]{:S(2)}) copy-start(s32[128]{0:T(128)} %param.7) | copy-start | bytes 1540
  53.0 27.7 %collective-permute-start.16 = (bf16[4,512,256]{2,1,0:T(8,128)(2,1)S(1)}, bf16[4,512,256]{2,1,0:T(8,128)(2,1)S(1)}, u32[]{:S(2)}, u32[]{:S(2)}) collective-permute-start(bf16[4,512,256]{2,1,0:T(8,128)(2,1)S(1)} %pad_maximum_fusion.rest_6_), channel_id=1, source_target_pairs={{0,32},{32,64},{64,96},{96,0},{1,33},{33,65},{65,97},{97,1},{2,34}... | collective-permute-start | bytes 3145736 | tf_op jit(solution)/shard_map/ppermute | solution.py:33
  53.1 32.5 %collective-permute-start.17 = (bf16[4,512,256]{2,1,0:T(8,128)(2,1)S(1)}, bf16[4,512,256]{2,1,0:T(8,128)(2,1)S(1)}, u32[]{:S(2)}, u32[]{:S(2)}) collective-permute-start(bf16[4,512,256]{2,1,0:T(8,128)(2,1)S(1)} %pad_maximum_fusion.1.rest_7_), channel_id=1, source_target_pairs={{0,96},{32,0},{64,32},{96,64},{1,97},{33,1},{65,33},{97,65},{2,98}... | collective-permute-start | bytes 3145736 | tf_op jit(solution)/shard_map/ppermute | solution.py:33
  56.4 29.2 %collective-permute-start.18 = (bf16[4,512,256]{2,1,0:T(8,128)(2,1)S(1)}, bf16[4,512,256]{2,1,0:T(8,128)(2,1)S(1)}, u32[]{:S(2)}, u32[]{:S(2)}) collective-permute-start(bf16[4,512,256]{2,1,0:T(8,128)(2,1)S(1)} %pad_maximum_fusion.2.rest_0_), channel_id=1, source_target_pairs={{0,2},{1,3},{2,4},{3,5},{4,6},{5,7},{6,0},{7,1},{8,10},{9,11},{10,... | collective-permute-start | bytes 3145736 | tf_op jit(solution)/shard_map/ppermute | solution.py:37
  57.6 28.0 %collective-permute-start.19 = (bf16[4,512,256]{2,1,0:T(8,128)(2,1)S(1)}, bf16[4,512,256]{2,1,0:T(8,128)(2,1)S(1)}, u32[]{:S(2)}, u32[]{:S(2)}) collective-permute-start(bf16[4,512,256]{2,1,0:T(8,128)(2,1)S(1)} %pad_maximum_fusion.3.rest_1_), channel_id=1, source_target_pairs={{0,6},{1,7},{2,0},{3,1},{4,2},{5,3},{6,4},{7,5},{8,14},{9,15},{10,... | collective-permute-start | bytes 3145736 | tf_op jit(solution)/shard_map/ppermute | solution.py:37
  63.7 17.0 %collective-permute-start.22 = (bf16[512,512]{1,0:T(8,128)(2,1)S(1)}, bf16[512,512]{1,0:T(8,128)(2,1)S(1)}, u32[]{:S(2)}, u32[]{:S(2)}) collective-permute-start(bf16[512,512]{1,0:T(8,128)(2,1)S(1)} %copy-done.3), channel_id=1, source_target_pairs={{0,0},{8,32},{16,64},{24,96},{32,8},{40,40},{48,72},{56,104},{64,1... | collective-permute-start | bytes 1572872 | tf_op jit(solution)/shard_map/ppermute | solution.py:376
  85.6 25.0 %collective-permute-start.23 = (bf16[4,512,256]{2,1,0:T(8,128)(2,1)S(1)}, bf16[4,512,256]{2,1,0:T(8,128)(2,1)S(1)}, u32[]{:S(2)}, u32[]{:S(2)}) collective-permute-start(bf16[4,512,256]{2,1,0:T(8,128)(2,1)S(1)} %pad_maximum_fusion.1.rest_7_), channel_id=1, source_target_pairs={{0,32},{32,64},{64,96},{96,0},{1,33},{33,65},{65,97},{97,1},{2,34}... | collective-permute-start | bytes 3145736 | tf_op jit(solution)/shard_map/ppermute | solution.py:33
  86.3 24.3 %collective-permute-start.24 = (bf16[4,512,256]{2,1,0:T(8,128)(2,1)S(1)}, bf16[4,512,256]{2,1,0:T(8,128)(2,1)S(1)}, u32[]{:S(2)}, u32[]{:S(2)}) collective-permute-start(bf16[4,512,256]{2,1,0:T(8,128)(2,1)S(1)} %pad_maximum_fusion.rest_6_), channel_id=1, source_target_pairs={{0,96},{32,0},{64,32},{96,64},{1,97},{33,1},{65,33},{97,65},{2,98}... | collective-permute-start | bytes 3145736 | tf_op jit(solution)/shard_map/ppermute | solution.py:33
  89.4 25.2 %collective-permute-start.25 = (bf16[4,512,256]{2,1,0:T(8,128)(2,1)S(1)}, bf16[4,512,256]{2,1,0:T(8,128)(2,1)S(1)}, u32[]{:S(2)}, u32[]{:S(2)}) collective-permute-start(bf16[4,512,256]{2,1,0:T(8,128)(2,1)S(1)} %pad_maximum_fusion.3.rest_1_), channel_id=1, source_target_pairs={{0,2},{1,3},{2,4},{3,5},{4,6},{5,7},{6,0},{7,1},{8,10},{9,11},{10,... | collective-permute-start | bytes 3145736 | tf_op jit(solution)/shard_map/ppermute | solution.py:37
  90.5 25.1 %collective-permute-start.26 = (bf16[4,512,256]{2,1,0:T(8,128)(2,1)S(1)}, bf16[4,512,256]{2,1,0:T(8,128)(2,1)S(1)}, u32[]{:S(2)}, u32[]{:S(2)}) collective-permute-start(bf16[4,512,256]{2,1,0:T(8,128)(2,1)S(1)} %pad_maximum_fusion.2.rest_0_), channel_id=1, source_target_pairs={{0,6},{1,7},{2,0},{3,1},{4,2},{5,3},{6,4},{7,5},{8,14},{9,15},{10,... | collective-permute-start | bytes 3145736 | tf_op jit(solution)/shard_map/ppermute | solution.py:37
  92.6 14.8 %collective-permute-start.27 = (bf16[512,512]{1,0:T(8,128)(2,1)S(1)}, bf16[512,512]{1,0:T(8,128)(2,1)S(1)}, u32[]{:S(2)}, u32[]{:S(2)}) collective-permute-start(bf16[512,512]{1,0:T(8,128)(2,1)S(1)} %collective-permute-done.22.own_ref), channel_id=1, source_target_pairs={{0,16},{8,24},{16,0},{24,8},{1,17},{9,25},{17,1},{25,9},{2,18},{10... | collective-permute-start | bytes 1572872 | tf_op jit(solution)/shard_map/ppermute | solution.py:381
  115.7 7.4 %collective-permute-start.28 = (bf16[2,512,512]{2,1,0:T(8,128)(2,1)S(1)}, bf16[2,512,512]{2,1,0:T(8,128)(2,1)S(1)}, u32[]{:S(2)}, u32[]{:S(2)}) collective-permute-start(bf16[2,512,512]{2,1,0:T(8,128)(2,1)S(1)} %pad_maximum_fusion.4), channel_id=1, source_target_pairs={{0,8},{8,0},{16,24},{24,16},{1,9},{9,1},{17,25},{25,17},{2,10},{10... | collective-permute-start | bytes 3145736 | tf_op jit(solution)/shard_map/ppermute | solution.py:386
  116.6 26.6 %collective-permute-start.29 = (bf16[4,512,256]{2,1,0:T(8,128)(2,1)S(1)}, bf16[4,512,256]{2,1,0:T(8,128)(2,1)S(1)}, u32[]{:S(2)}, u32[]{:S(2)}) collective-permute-start(bf16[4,512,256]{2,1,0:T(8,128)(2,1)S(1)} %collective-permute-done.18.rest_2_), channel_id=1, source_target_pairs={{0,2},{1,3},{2,4},{3,5},{4,6},{5,7},{6,0},{7,1},{8,10},{9,11},{10,... | collective-permute-start | bytes 3145736 | tf_op jit(solution)/shard_map/ppermute | solution.py:37
  117.2 26.6 %collective-permute-start.30 = (bf16[4,512,256]{2,1,0:T(8,128)(2,1)S(1)}, bf16[4,512,256]{2,1,0:T(8,128)(2,1)S(1)}, u32[]{:S(2)}, u32[]{:S(2)}) collective-permute-start(bf16[4,512,256]{2,1,0:T(8,128)(2,1)S(1)} %collective-permute-done.19.rest_5_), channel_id=1, source_target_pairs={{0,6},{1,7},{2,0},{3,1},{4,2},{5,3},{6,4},{7,5},{8,14},{9,15},{10,... | collective-permute-start | bytes 3145736 | tf_op jit(solution)/shard_map/ppermute | solution.py:37
  119.9 26.2 %collective-permute-start.31 = (bf16[4,512,256]{2,1,0:T(8,128)(2,1)S(1)}, bf16[4,512,256]{2,1,0:T(8,128)(2,1)S(1)}, u32[]{:S(2)}, u32[]{:S(2)}) collective-permute-start(bf16[4,512,256]{2,1,0:T(8,128)(2,1)S(1)} %collective-permute-done.16.rest_8_), channel_id=1, source_target_pairs={{0,32},{32,64},{64,96},{96,0},{1,33},{33,65},{65,97},{97,1},{2,34}... | collective-permute-start | bytes 3145736 | tf_op jit(solution)/shard_map/ppermute | solution.py:33
  119.9 26.2 %collective-permute-start.32 = (bf16[4,512,256]{2,1,0:T(8,128)(2,1)S(1)}, bf16[4,512,256]{2,1,0:T(8,128)(2,1)S(1)}, u32[]{:S(2)}, u32[]{:S(2)}) collective-permute-start(bf16[4,512,256]{2,1,0:T(8,128)(2,1)S(1)} %collective-permute-done.17.rest_11_), channel_id=1, source_target_pairs={{0,96},{32,0},{64,32},{96,64},{1,97},{33,1},{65,33},{97,65},{2,98}... | collective-permute-start | bytes 3145736 | tf_op jit(solution)/shard_map/ppermute | solution.py:33
